TPU v7x, 256 devices: a whole 4x4x8 slice. The times are simulated.
256 devices in a mesh: grp: 32 (over x, y, core), dom: 8 (over z).
Axes of the slice: x: 4, y: 4, z: 8, core: 2. Of those that a mesh axis runs over, the one named last changes fastest.
Arguments:
- surplus: float32 [512, 1024, 512], P('grp', 'dom'), may hold values from -0.4 to 0.4
- block_ids: int32 [512, 1024], P('grp', 'dom'), may hold values from 0 to 8191, as said below
- coef: int32 [512], P('grp'), may hold values from -4 to 6, as said below
Outputs:
- updated: float32 [512, 1024, 512], P('grp', 'dom')
Inputs may be any that keep to these rules, and one draw needn't show every extreme that they name: `block_ids`: for each grid, the slots in columns d * 128 to (d + 1) * 128 - 1 hold 128 different numbers from d * 1024 to (d + 1) * 1024 - 1. `coef`: each coefficient is one of 1, -4, 6.
All inputs are finite; a program needn't handle non-finite values.
Results may differ from a plain program's by a relative error of at most 0.000071.
Values sent between devices are 32-bit elements; how exact they have to be, the bound alone decides.
No kernel may reach another device: no remote copies, remote signals or barrier semaphores. Data moves between devices by JAX's collectives and lax.ppermute only.
A program may use at most 64 MiB of HBM per device.

v0:
```python
import jax
import jax.numpy as jnp
from jax import lax
from jax.sharding import PartitionSpec as P

NBD = 1024


def cut_along(value, dim, size):
    before, after = (value.shape[:dim], value.shape[dim + 1 :])
    return jnp.moveaxis(value.reshape(*before, size, -1, *after), dim, 0)


def summed_on_arrival(value, axis, dim):
    parts = cut_along(value, dim, lax.axis_size(axis))
    arrived = lax.all_to_all(parts, axis, split_axis=0, concat_axis=0, tiled=True)
    return arrived.sum(axis=0)


def from_everyone(value, axis):
    copies = jnp.broadcast_to(value, (lax.axis_size(axis), *value.shape))
    return lax.all_to_all(copies, axis, split_axis=0, concat_axis=0, tiled=True)


def joined_along(parts, dim):
    shape = list(parts.shape[1:])
    shape[dim] *= parts.shape[0]
    return jnp.moveaxis(parts, 0, dim).reshape(shape)


def collect(value, axis, dim):
    parts = from_everyone(value, axis)
    return joined_along(parts, dim)


def local(surplus, block_ids, coef):
    offset = lax.axis_index("dom") * NBD
    local_ids = block_ids - offset
    columns = lax.broadcasted_iota(jnp.int32, (1, 1, NBD), 2)
    onehot = (local_ids[:, :, None] == columns).astype(jnp.float32)
    scaled = surplus * coef.astype(jnp.float32)[:, None, None]
    partial_sum = jnp.einsum("gkn,gkb->nb", onehot, scaled, precision=lax.Precision.HIGHEST)
    shares = summed_on_arrival(partial_sum, "grp", 0)
    combined = collect(shares, "grp", 0)
    return jnp.einsum("gkn,nb->gkb", onehot, combined, precision=lax.Precision.HIGHEST)


def solution(mesh):
    return jax.shard_map(
        local,
        mesh=mesh,
        in_specs=(P("grp", "dom", None), P("grp", "dom"), P("grp")),
        out_specs=P("grp", "dom", None),
        check_vma=False,
    )
```

profile of v0, /device:TPU:1, one launch (start us, length us, event | category | flops | bytes accessed | tf_op | source)
XLA Modules:
  0.0 94.8 jit_solution(17651580814565918927)
XLA Ops:
  0.0 0.7 convert_element_type.4
  0.7 0.7 broadcast_subtract_fusion
  1.4 16.3 %fusion.1 = f32[1024,512,1]{1,0,2:T(8,128)S(1)} fusion(f32[16,128,512]{2,1,0:T(8,128)} %param.3, s32[16,128]{1,0:T(8,128)S(1)} %broadcast_subtract_fusion, f32[16]{0:T(128)S(1)} %convert_element_type.4), kind=kOutput, calls=%fused_computation.2 | convolution fusion | flops 12888047616 | bytes 6299712 | tf_op jit(solution)/shard_map/gkn,gkb->nb/dot_general | solution.py:42
  17.6 36.5 %all_to_all.10 = f32[32,32,512]{2,1,0:T(8,128)S(1)} all-to-all(f32[32,32,512]{2,1,0:T(8,128)S(1)} %bitcast.8), channel_id=1, replica_groups=mesh['grp'=32,'dom'=8] {'grp'}, dimensions={0} | all-to-all | bytes 4194304 | tf_op jit(solution)/shard_map/all_to_all | solution.py:16
  54.2 0.1 reduce_sum.9
  54.3 0.2 broadcast_in_dim.2
  54.6 31.9 %all_to_all.11 = f32[32,32,512]{2,1,0:T(8,128)S(1)} all-to-all(f32[32,32,512]{2,1,0:T(8,128)S(1)} %broadcast_in_dim.2), channel_id=1, replica_groups=mesh['grp'=32,'dom'=8] {'grp'}, dimensions={0} | all-to-all | bytes 4194304 | tf_op jit(solution)/shard_map/all_to_all | solution.py:22
  86.5 8.3 %fusion = f32[16,128,512]{2,1,0:T(8,128)} fusion(f32[1024,512,1]{1,0,2:T(8,128)S(1)} %bitcast.7, s32[16,128]{1,0:T(8,128)S(1)} %broadcast_subtract_fusion), kind=kOutput, calls=%fused_computation.1 | convolution fusion | flops 12886999040 | bytes 6299648 | tf_op jit(solution)/shard_map/gkn,nb->gkb/dot_general | solution.py:45
where the time goes:
time: 95 us; the launch traced here: 94.8 us
  blocking collectives  68.4 us (72%)
  matrix products  24.6 us (26%)
  other arithmetic  1.5 us (2%)
    all_to_all x1, blocking collectives, summed_on_arrival(): lax.all_to_all(parts, axis, split_axis=0, concat_axis=0, tiled=True)  36.5 us
    all_to_all x1, blocking collectives, from_everyone(): return lax.all_to_all(copies, axis, split_axis=0, concat_axis=0, tiled=True)  31.9 us
    dot_general x1, matrix products, local(): jnp.einsum('gkn,gkb->nb', onehot, scaled, precision=lax.Precision.HIGHEST)  16.3 us
    dot_general x1, matrix products, local(): jnp.einsum('gkn,nb->gkb', onehot, combined, precision=lax.Precision.HIGHEST)  8.34 us

commit v1 on v0

v1 whole, which is shorter than its diff:
```python
import jax
import jax.numpy as jnp
from jax import lax
from jax.experimental import pallas as pl
from jax.experimental.pallas import tpu as pltpu
from jax.sharding import PartitionSpec as P

GRIDS = 16
K = 128
BLK = 512
NBD = 1024
HALF = NBD // 2
ROWS = HALF // 4
CHUNK = 4
VMEM = pltpu.VMEM
VMEM_LIMIT = 48 * 1024 * 1024


def device(x, y, core):
    return (x * 4 + y) * 2 + core


def pairs(partner):
    return [
        (device(x, y, c), device(*partner(x, y, c)))
        for x in range(4)
        for y in range(4)
        for c in range(2)
    ]


def own_line(step):
    return pairs(lambda x, y, c: (x, y ^ step, c) if c else (x ^ step, y, c))


def other_line(step):
    return pairs(lambda x, y, c: (x ^ step, y, c) if c else (x, y ^ step, c))


OTHER_CORE = pairs(lambda x, y, c: (x, y, 1 - c))


def send(value, partner):
    return lax.ppermute(value, "grp", partner)


def split(value):
    high = value.astype(jnp.bfloat16)
    low = (value - high.astype(jnp.float32)).astype(jnp.bfloat16)
    return high, low


def weights(ids_ref, coef_ref, where_ref, half, rows, grids):
    base = where_ref[0] + half * HALF
    line = where_ref[1 + half]
    block = lax.broadcasted_iota(jnp.int32, (ROWS, K), 0)
    columns = []
    for g in grids:
        slot = ids_ref[pl.ds(g, 1), :] - base
        quarters = []
        for k in range(4):
            hit = block == slot - (line ^ k) * ROWS
            quarters.append(jnp.where(hit, coef_ref[g].astype(jnp.float32), 0.0))
        columns.append(jnp.concatenate(quarters, 0).astype(jnp.bfloat16))
    return jnp.concatenate(columns, 1)


def scatter_other(where_ref, coef_ref, ids_ref, surplus_ref, out_ref, high_ref, low_ref, stage, sems):
    copies = []
    for t in range(GRIDS // CHUNK):
        part = pl.ds(t * CHUNK * K, CHUNK * K)
        copy = pltpu.make_async_copy(surplus_ref.at[part, :], stage.at[part, :], sems.at[t])
        copy.start()
        copies.append(copy)
    half = 1 - where_ref[3]
    for t in range(GRIDS // CHUNK):
        part = pl.ds(t * CHUNK * K, CHUNK * K)
        hot = weights(ids_ref, coef_ref, where_ref, half, ROWS, range(t * CHUNK, (t + 1) * CHUNK))
        copies[t].wait()
        high, low = split(stage[part, :])
        high_ref[part, :] = high
        low_ref[part, :] = low
        term = jnp.dot(hot, high, preferred_element_type=jnp.float32) + jnp.dot(
            hot, low, preferred_element_type=jnp.float32
        )
        if t == 0:
            out_ref[...] = term
        else:
            out_ref[...] += term


def scatter_own(where_ref, coef_ref, ids_ref, high_ref, low_ref, out_ref):
    half = where_ref[3]
    for t in range(GRIDS // CHUNK):
        part = pl.ds(t * CHUNK * K, CHUNK * K)
        hot = weights(ids_ref, coef_ref, where_ref, half, ROWS, range(t * CHUNK, (t + 1) * CHUNK))
        term = jnp.dot(hot, high_ref[part, :], preferred_element_type=jnp.float32) + jnp.dot(
            hot, low_ref[part, :], preferred_element_type=jnp.float32
        )
        if t == 0:
            out_ref[...] = term
        else:
            out_ref[...] += term


def gather(where_ref, ids_ref, *refs):
    pieces, (out_ref, high_ref, low_ref, column_ref) = refs[:8], refs[8:]
    step = pl.program_id(0)

    @pl.when(step == 0)
    def _():
        for side in range(2):
            half = where_ref[3] if side == 0 else 1 - where_ref[3]
            line = where_ref[1 + half]
            for k in range(4):
                rows = pl.ds(pl.multiple_of(half * HALF + (line ^ k) * ROWS, ROWS), ROWS)
                high, low = split(pieces[side * 4 + k][...])
                high_ref[rows, :] = high
                low_ref[rows, :] = low
        column_ref[...] = jnp.transpose(jnp.concatenate([ids_ref[...] - where_ref[0]] * 8, 0))

    block = lax.broadcasted_iota(jnp.int32, (K, NBD), 1)
    lane = lax.broadcasted_iota(jnp.int32, (K, K), 1)
    hots = []
    for i in range(CHUNK):
        column = jnp.sum(jnp.where(lane == step * CHUNK + i, column_ref[...], 0), 1, keepdims=True)
        hots.append(jnp.where(block == column, 1.0, 0.0).astype(jnp.bfloat16))
    hot = jnp.concatenate(hots, 0)
    out_ref[...] = jnp.dot(hot, high_ref[...], preferred_element_type=jnp.float32) + jnp.dot(
        hot, low_ref[...], preferred_element_type=jnp.float32
    )


def local(surplus, block_ids, coef):
    index = lax.axis_index("grp")
    core, x, y = index & 1, index >> 3, (index >> 1) & 3
    where = jnp.stack([lax.axis_index("dom") * NBD, x, y, core]).astype(jnp.int32)
    smem = pl.BlockSpec(memory_space=pltpu.SMEM)
    vmem = pl.BlockSpec(memory_space=VMEM)
    params = pltpu.CompilerParams(vmem_limit_bytes=VMEM_LIMIT)
    slots = GRIDS * K
    other, high, low = pl.pallas_call(
        scatter_other,
        out_shape=(
            jax.ShapeDtypeStruct((HALF, BLK), jnp.float32),
            jax.ShapeDtypeStruct((slots, BLK), jnp.bfloat16),
            jax.ShapeDtypeStruct((slots, BLK), jnp.bfloat16),
        ),
        in_specs=[smem, smem, vmem, pl.BlockSpec(memory_space=pl.ANY)],
        out_specs=(vmem, vmem, vmem),
        scratch_shapes=[VMEM((slots, BLK), jnp.float32), pltpu.SemaphoreType.DMA((GRIDS // CHUNK,))],
        compiler_params=params,
    )(where, coef, block_ids, surplus.reshape(slots, BLK))
    arrived = send(other, OTHER_CORE)
    own = pl.pallas_call(
        scatter_own,
        out_shape=jax.ShapeDtypeStruct((HALF, BLK), jnp.float32),
        in_specs=[smem, smem, vmem, vmem, vmem],
        out_specs=vmem,
        compiler_params=params,
        cost_estimate=pl.CostEstimate(flops=4 * HALF * slots * BLK, bytes_accessed=0, transcendentals=0),
    )(where, coef, block_ids, high, low)
    parts = [own[k * ROWS : (k + 1) * ROWS] + arrived[k * ROWS : (k + 1) * ROWS] for k in range(4)]
    order = (2, 1, 3)
    got = [send(parts[k], own_line(k)) for k in order]
    share = parts[0] + got[0] + got[1] + got[2]
    got = [send(share, other_line(k)) for k in order]
    share = share + got[0] + got[1] + got[2]
    line = [share] + [send(share, own_line(k)) for k in (1, 2, 3)]
    across = [send(piece, OTHER_CORE) for piece in line]
    out = pl.pallas_call(
        gather,
        grid=(GRIDS // CHUNK,),
        out_shape=jax.ShapeDtypeStruct((slots, BLK), jnp.float32),
        in_specs=[smem, vmem] + [vmem] * 8,
        out_specs=pl.BlockSpec((CHUNK * K, BLK), lambda t: (t, 0)),
        scratch_shapes=[
            VMEM((NBD, BLK), jnp.bfloat16),
            VMEM((NBD, BLK), jnp.bfloat16),
            VMEM((K, K), jnp.int32),
        ],
        compiler_params=params,
    )(where, block_ids, *line, *across)
    return out.reshape(surplus.shape)


def solution(mesh):
    return jax.shard_map(
        local,
        mesh=mesh,
        in_specs=(P("grp", "dom", None), P("grp", "dom"), P("grp")),
        out_specs=P("grp", "dom", None),
        check_vma=False,
    )
```

time: 95 us -> 56 us (0.59)
  blocking collectives: 68.4 us -> 0 us
  matrix products: 24.6 us -> 0 us
  starting transfers between devices: 0 us -> 20 us
  waiting for transfers between devices: 0 us -> 18.6 us
  Pallas kernels: 0 us -> 15.4 us
  local copies, waits for them, and re-layouts: 0.25 us -> 1.36 us
  other arithmetic: 1.5 us -> 0.43 us
    all_to_all x2 -> x0, blocking collectives: 68.4 us -> none  [the longest x1 36.5 us: summed_on_arrival(): lax.all_to_all(parts, axis, split_axis=0, concat_axis=0, tiled=True)]
    dot_general x2 -> x0, matrix products: 24.6 us -> none  [the longest x1 16.3 us: local(): jnp.einsum('gkn,gkb->nb', onehot, scaled, precision=lax.Precision.HIGHEST)]
    ppermute x0 -> x14, starting transfers between devices: none -> 20 us  [send(): return lax.ppermute(value, 'grp', partner)]
    ppermute x0 -> x14, waiting for transfers between devices: none -> 18.6 us  [send(): return lax.ppermute(value, 'grp', partner)]
    pallas_call x0 -> x3, Pallas kernels: none -> 15.4 us  [the longest x1 7.65 us: local(): pl.pallas_call(gather, grid=(GRIDS // CHUNK,), out_shape=jax.ShapeDtypeSt...]
    unnamed x0 -> x6, local copies, waits for them, and re-layouts: none -> 1.36 us
  transfers between devices with their start and end apart: 0 -> 14, of which waited for: 0 -> 8; matrix products, arithmetic and copies ran while one was open for 0% -> 0% of each run, Pallas kernels for 0% -> 5%
where the time goes in v1:
time: 56 us; the launch traced here: 55.9 us
  starting transfers between devices  20 us (36%)
  waiting for transfers between devices  18.6 us (33%)
  Pallas kernels  15.4 us (28%)
  local copies, waits for them, and re-layouts  1.36 us (2%)
    ppermute x14, starting transfers between devices, send(): return lax.ppermute(value, 'grp', partner)  20 us
    ppermute x14, waiting for transfers between devices, send(): return lax.ppermute(value, 'grp', partner)  18.6 us
    pallas_call x1, Pallas kernels, local(): pl.pallas_call(gather, grid=(GRIDS // CHUNK,), out_shape=jax.ShapeDtypeSt...  7.65 us
    pallas_call x1, Pallas kernels, local(): pl.pallas_call(scatter_other, out_shape=(jax.ShapeDtypeStruct((HALF, BLK)...  4.93 us
    pallas_call x1, Pallas kernels, local(): pl.pallas_call(scatter_own, out_shape=jax.ShapeDtypeStruct((HALF, BLK), j...  2.86 us
    unnamed x6, local copies, waits for them, and re-layouts  1.36 us
  transfers between devices with their start and end apart: 14, of which 8 were waited for; matrix products, arithmetic and copies ran while one was open for 0% of the time, Pallas kernels for 5%

profile of v1, /device:TPU:1, one launch (start us, length us, event | category | flops | bytes accessed | tf_op | source)
XLA Modules:
  0.0 55.9 jit_solution(10462491811193860927)
XLA Ops:
  0.0 0.1 pad_add_fusion.where_ref
  0.1 0.0 copy-start
  0.1 0.7 %copy-done = s32[16,128]{1,0:T(8,128)S(1)} copy-done((s32[16,128]{1,0:T(8,128)S(1)}, s32[16,128]{1,0:T(8,128)}, u32[]{:S(2)}) %copy-start) | copy-done | bytes 8216
  0.8 0.0 copy-start.2
  0.8 0.7 %copy-done.2 = s32[16]{0:T(128)S(1)} copy-done((s32[16]{0:T(128)S(1)}, s32[16]{0:T(128)}, u32[]{:S(2)}) %copy-start.2) | copy-done | bytes 88
  1.4 4.9 %shard_map.37 = (f32[512,512]{1,0:T(8,128)S(1)}, bf16[2048,512]{1,0:T(8,128)(2,1)S(1)}, bf16[2048,512]{1,0:T(8,128)(2,1)S(1)}) custom-call(s32[4]{0:T(128)S(1)} %pad_add_fusion.where_ref, s32[16]{0:T(128)S(1)} %copy-done.2, s32[16,128]{1,0:T(8,128)S(1)} %copy-done, f32[2048,512]{1,0:T(8,128)} %bitcast.6), custom_call_target="tpu_custom_call" | custom-call | tf_op jit(solution)/shard_map/pallas_call | solution.py:142
  6.4 3.3 %collective-permute-start = (f32[512,512]{1,0:T(8,128)S(1)}, f32[512,512]{1,0:T(8,128)S(1)}, u32[]{:S(2)}, u32[]{:S(2)}) collective-permute-start(f32[512,512]{1,0:T(8,128)S(1)} %get-tuple-element.10), channel_id=1, source_target_pairs={{0,8},{8,0},{16,24},{24,16},{32,40},{40,32},{48,56},{56,48},{64,72... | collective-permute-start | bytes 3145736 | tf_op jit(solution)/shard_map/ppermute | solution.py:44
  9.7 2.9 %shard_map.38 = f32[512,512]{1,0:T(8,128)S(1)} custom-call(s32[4]{0:T(128)S(1)} %pad_add_fusion.where_ref, s32[16]{0:T(128)S(1)} %copy-done.2, s32[16,128]{1,0:T(8,128)S(1)} %copy-done, bf16[2048,512]{1,0:T(8,128)(2,1)S(1)} %get-tuple-element.8.high_ref, bf16[2048,512]{1,0:T(8,128)(2,1)S(1)} %get-tuple-element.9.low_ref), custom_call_target="tpu_custom_call" | custom-call | flops 2147483648 | tf_op jit(solution)/shard_map/pallas_call | solution.py:155
  12.6 0.0 copy-start.1
  12.6 0.0 collective-permute-done
  12.6 0.1 slice_add_fusion.2
  12.7 1.3 %collective-permute-start.1 = (f32[128,512]{1,0:T(8,128)S(1)}, f32[128,512]{1,0:T(8,128)S(1)}, u32[]{:S(2)}, u32[]{:S(2)}) collective-permute-start(f32[128,512]{1,0:T(8,128)S(1)} %get-tuple-element.11), channel_id=1, source_target_pairs={{0,128},{8,40},{16,144},{24,56},{32,160},{40,8},{48,176},{56,24},{... | collective-permute-start | bytes 786440 | tf_op jit(solution)/shard_map/ppermute | solution.py:44
  14.0 0.8 %collective-permute-start.3 = (f32[128,512]{1,0:T(8,128)S(1)}, f32[128,512]{1,0:T(8,128)S(1)}, u32[]{:S(2)}, u32[]{:S(2)}) collective-permute-start(f32[128,512]{1,0:T(8,128)S(1)} %get-tuple-element.12), channel_id=1, source_target_pairs={{0,192},{8,56},{16,208},{24,40},{32,224},{40,24},{48,240},{56,8},{... | collective-permute-start | bytes 786440 | tf_op jit(solution)/shard_map/ppermute | solution.py:44
  14.8 0.7 %collective-permute-start.2 = (f32[128,512]{1,0:T(8,128)S(1)}, f32[128,512]{1,0:T(8,128)S(1)}, u32[]{:S(2)}, u32[]{:S(2)}) collective-permute-start(f32[128,512]{1,0:T(8,128)S(1)} %get-tuple-element.13), channel_id=1, source_target_pairs={{0,64},{8,24},{16,80},{24,8},{32,96},{40,56},{48,112},{56,40},{64,... | collective-permute-start | bytes 786440 | tf_op jit(solution)/shard_map/ppermute | solution.py:44
  15.5 4.4 %collective-permute-done.1 = f32[128,512]{1,0:T(8,128)S(1)} collective-permute-done((f32[128,512]{1,0:T(8,128)S(1)}, f32[128,512]{1,0:T(8,128)S(1)}, u32[]{:S(2)}, u32[]{:S(2)}) %collective-permute-start.1) | collective-permute-done | bytes 262176 | tf_op jit(solution)/shard_map/ppermute | solution.py:44
  19.9 2.8 %collective-permute-done.3 = f32[128,512]{1,0:T(8,128)S(1)} collective-permute-done((f32[128,512]{1,0:T(8,128)S(1)}, f32[128,512]{1,0:T(8,128)S(1)}, u32[]{:S(2)}, u32[]{:S(2)}) %collective-permute-start.3) | collective-permute-done | bytes 262176 | tf_op jit(solution)/shard_map/ppermute | solution.py:44
  22.7 0.0 collective-permute-done.2
  22.7 0.1 fusion.2
  22.8 1.2 %collective-permute-start.6 = (f32[128,512]{1,0:T(8,128)S(1)}, f32[128,512]{1,0:T(8,128)S(1)}, u32[]{:S(2)}, u32[]{:S(2)}) collective-permute-start(f32[128,512]{1,0:T(8,128)S(1)} %fusion.2), channel_id=1, source_target_pairs={{0,48},{8,200},{16,32},{24,216},{32,16},{40,232},{48,0},{56,248},{... | collective-permute-start | bytes 786440 | tf_op jit(solution)/shard_map/ppermute | solution.py:44
  24.0 0.0 collective-permute-start.5
  24.0 2.7 %collective-permute-start.4 = (f32[128,512]{1,0:T(8,128)S(1)}, f32[128,512]{1,0:T(8,128)S(1)}, u32[]{:S(2)}, u32[]{:S(2)}) collective-permute-start(f32[128,512]{1,0:T(8,128)S(1)} %fusion.2), channel_id=1, source_target_pairs={{0,32},{8,136},{16,48},{24,152},{32,0},{40,168},{48,16},{56,184},{... | collective-permute-start | bytes 786440 | tf_op jit(solution)/shard_map/ppermute | solution.py:44
  26.7 2.9 %collective-permute-done.6 = f32[128,512]{1,0:T(8,128)S(1)} collective-permute-done((f32[128,512]{1,0:T(8,128)S(1)}, f32[128,512]{1,0:T(8,128)S(1)}, u32[]{:S(2)}, u32[]{:S(2)}) %collective-permute-start.6) | collective-permute-done | bytes 262176 | tf_op jit(solution)/shard_map/ppermute | solution.py:44
  29.6 0.0 collective-permute-done.5
  29.6 4.0 %collective-permute-done.4 = f32[128,512]{1,0:T(8,128)S(1)} collective-permute-done((f32[128,512]{1,0:T(8,128)S(1)}, f32[128,512]{1,0:T(8,128)S(1)}, u32[]{:S(2)}, u32[]{:S(2)}) %collective-permute-start.4) | collective-permute-done | bytes 262176 | tf_op jit(solution)/shard_map/ppermute | solution.py:44
  33.6 0.1 add_add_fusion.refs_0_
  33.7 1.1 %collective-permute-start.9 = (f32[128,512]{1,0:T(8,128)S(1)}, f32[128,512]{1,0:T(8,128)S(1)}, u32[]{:S(2)}, u32[]{:S(2)}) collective-permute-start(f32[128,512]{1,0:T(8,128)S(1)} %add_add_fusion.refs_0_), channel_id=1, source_target_pairs={{0,192},{8,56},{16,208},{24,40},{32,224},{40,24},{48,240},{56,8},{... | collective-permute-start | bytes 786440 | tf_op jit(solution)/shard_map/ppermute | solution.py:44
  34.8 0.2 collective-permute-start.8
  35.0 2.1 %collective-permute-start.7 = (f32[128,512]{1,0:T(8,128)S(1)}, f32[128,512]{1,0:T(8,128)S(1)}, u32[]{:S(2)}, u32[]{:S(2)}) collective-permute-start(f32[128,512]{1,0:T(8,128)S(1)} %add_add_fusion.refs_0_), channel_id=1, source_target_pairs={{0,64},{8,24},{16,80},{24,8},{32,96},{40,56},{48,112},{56,40},{64,... | collective-permute-start | bytes 786440 | tf_op jit(solution)/shard_map/ppermute | solution.py:44
  37.0 2.8 %collective-permute-start.10 = (f32[128,512]{1,0:T(8,128)S(1)}, f32[128,512]{1,0:T(8,128)S(1)}, u32[]{:S(2)}, u32[]{:S(2)}) collective-permute-start(f32[128,512]{1,0:T(8,128)S(1)} %add_add_fusion.refs_0_), channel_id=1, source_target_pairs={{0,8},{8,0},{16,24},{24,16},{32,40},{40,32},{48,56},{56,48},{64,72... | collective-permute-start | bytes 786440 | tf_op jit(solution)/shard_map/ppermute | solution.py:44
  39.9 3.4 %collective-permute-done.9.refs_3_ = f32[128,512]{1,0:T(8,128)S(1)} collective-permute-done((f32[128,512]{1,0:T(8,128)S(1)}, f32[128,512]{1,0:T(8,128)S(1)}, u32[]{:S(2)}, u32[]{:S(2)}) %collective-permute-start.9) | collective-permute-done | bytes 262176 | tf_op jit(solution)/shard_map/ppermute | solution.py:44
  43.3 2.9 %collective-permute-start.13 = (f32[128,512]{1,0:T(8,128)S(1)}, f32[128,512]{1,0:T(8,128)S(1)}, u32[]{:S(2)}, u32[]{:S(2)}) collective-permute-start(f32[128,512]{1,0:T(8,128)S(1)} %collective-permute-done.9.refs_3_), channel_id=1, source_target_pairs={{0,8},{8,0},{16,24},{24,16},{32,40},{40,32},{48,56},{56,48},{64,72... | collective-permute-start | bytes 786440 | tf_op jit(solution)/shard_map/ppermute | solution.py:44
  46.2 0.0 collective-permute-done.8.refs_2_
  46.2 0.0 collective-permute-start.12
  46.2 0.0 collective-permute-done.7.refs_1_
  46.2 0.9 %collective-permute-start.11 = (f32[128,512]{1,0:T(8,128)S(1)}, f32[128,512]{1,0:T(8,128)S(1)}, u32[]{:S(2)}, u32[]{:S(2)}) collective-permute-start(f32[128,512]{1,0:T(8,128)S(1)} %collective-permute-done.7.refs_1_), channel_id=1, source_target_pairs={{0,8},{8,0},{16,24},{24,16},{32,40},{40,32},{48,56},{56,48},{64,72... | collective-permute-start | bytes 786440 | tf_op jit(solution)/shard_map/ppermute | solution.py:44
  47.1 0.0 collective-permute-done.10.refs_4_
  47.1 0.3 collective-permute-done.13.refs_7_
  47.3 0.4 collective-permute-done.12.refs_6_
  47.7 0.5 collective-permute-done.11.refs_5_
  48.2 0.0 copy-done.1
  48.2 7.7 %shard_map.39 = f32[2048,512]{1,0:T(8,128)} custom-call(s32[4]{0:T(128)S(1)} %pad_add_fusion.where_ref, s32[16,128]{1,0:T(8,128)S(1)} %copy-done.1, f32[128,512]{1,0:T(8,128)S(1)} %add_add_fusion.refs_0_, f32[128,512]{1,0:T(8,128)S(1)} %collective-permute-done.7.refs_1_, f32[128,512]{1,0:T(8,128)S(1)} %collective-permute-done.8.refs_2_, ...), custom_call_target="tpu_custom_call" | custom-call | tf_op jit(solution)/shard_map/pallas_call | solution.py:171
Async XLA Ops:
  0.1 0.7 %copy-start = (s32[16,128]{1,0:T(8,128)S(1)}, s32[16,128]{1,0:T(8,128)}, u32[]{:S(2)}) copy-start(s32[16,128]{1,0:T(8,128)} %ids_ref.5) | copy-start | bytes 24580
  0.8 0.7 %copy-start.2 = (s32[16]{0:T(128)S(1)}, s32[16]{0:T(128)}, u32[]{:S(2)}) copy-start(s32[16]{0:T(128)} %coef_ref.3) | copy-start | bytes 196
  6.4 6.2 %collective-permute-start = (f32[512,512]{1,0:T(8,128)S(1)}, f32[512,512]{1,0:T(8,128)S(1)}, u32[]{:S(2)}, u32[]{:S(2)}) collective-permute-start(f32[512,512]{1,0:T(8,128)S(1)} %get-tuple-element.10), channel_id=1, source_target_pairs={{0,8},{8,0},{16,24},{24,16},{32,40},{40,32},{48,56},{56,48},{64,72... | collective-permute-start | bytes 3145736 | tf_op jit(solution)/shard_map/ppermute | solution.py:44
  12.6 35.7 %copy-start.1 = (s32[16,128]{1,0:T(8,128)S(1)}, s32[16,128]{1,0:T(8,128)}, u32[]{:S(2)}) copy-start(s32[16,128]{1,0:T(8,128)} %ids_ref.5) | copy-start | bytes 24580
  12.7 7.2 %collective-permute-start.1 = (f32[128,512]{1,0:T(8,128)S(1)}, f32[128,512]{1,0:T(8,128)S(1)}, u32[]{:S(2)}, u32[]{:S(2)}) collective-permute-start(f32[128,512]{1,0:T(8,128)S(1)} %get-tuple-element.11), channel_id=1, source_target_pairs={{0,128},{8,40},{16,144},{24,56},{32,160},{40,8},{48,176},{56,24},{... | collective-permute-start | bytes 786440 | tf_op jit(solution)/shard_map/ppermute | solution.py:44
  14.0 8.7 %collective-permute-start.3 = (f32[128,512]{1,0:T(8,128)S(1)}, f32[128,512]{1,0:T(8,128)S(1)}, u32[]{:S(2)}, u32[]{:S(2)}) collective-permute-start(f32[128,512]{1,0:T(8,128)S(1)} %get-tuple-element.12), channel_id=1, source_target_pairs={{0,192},{8,56},{16,208},{24,40},{32,224},{40,24},{48,240},{56,8},{... | collective-permute-start | bytes 786440 | tf_op jit(solution)/shard_map/ppermute | solution.py:44
  14.8 7.9 %collective-permute-start.2 = (f32[128,512]{1,0:T(8,128)S(1)}, f32[128,512]{1,0:T(8,128)S(1)}, u32[]{:S(2)}, u32[]{:S(2)}) collective-permute-start(f32[128,512]{1,0:T(8,128)S(1)} %get-tuple-element.13), channel_id=1, source_target_pairs={{0,64},{8,24},{16,80},{24,8},{32,96},{40,56},{48,112},{56,40},{64,... | collective-permute-start | bytes 786440 | tf_op jit(solution)/shard_map/ppermute | solution.py:44
  22.8 6.8 %collective-permute-start.6 = (f32[128,512]{1,0:T(8,128)S(1)}, f32[128,512]{1,0:T(8,128)S(1)}, u32[]{:S(2)}, u32[]{:S(2)}) collective-permute-start(f32[128,512]{1,0:T(8,128)S(1)} %fusion.2), channel_id=1, source_target_pairs={{0,48},{8,200},{16,32},{24,216},{32,16},{40,232},{48,0},{56,248},{... | collective-permute-start | bytes 786440 | tf_op jit(solution)/shard_map/ppermute | solution.py:44
  24.0 5.6 %collective-permute-start.5 = (f32[128,512]{1,0:T(8,128)S(1)}, f32[128,512]{1,0:T(8,128)S(1)}, u32[]{:S(2)}, u32[]{:S(2)}) collective-permute-start(f32[128,512]{1,0:T(8,128)S(1)} %fusion.2), channel_id=1, source_target_pairs={{0,16},{8,72},{16,0},{24,88},{32,48},{40,104},{48,32},{56,120},{64... | collective-permute-start | bytes 786440 | tf_op jit(solution)/shard_map/ppermute | solution.py:44
  24.0 9.6 %collective-permute-start.4 = (f32[128,512]{1,0:T(8,128)S(1)}, f32[128,512]{1,0:T(8,128)S(1)}, u32[]{:S(2)}, u32[]{:S(2)}) collective-permute-start(f32[128,512]{1,0:T(8,128)S(1)} %fusion.2), channel_id=1, source_target_pairs={{0,32},{8,136},{16,48},{24,152},{32,0},{40,168},{48,16},{56,184},{... | collective-permute-start | bytes 786440 | tf_op jit(solution)/shard_map/ppermute | solution.py:44
  33.7 9.6 %collective-permute-start.9 = (f32[128,512]{1,0:T(8,128)S(1)}, f32[128,512]{1,0:T(8,128)S(1)}, u32[]{:S(2)}, u32[]{:S(2)}) collective-permute-start(f32[128,512]{1,0:T(8,128)S(1)} %add_add_fusion.refs_0_), channel_id=1, source_target_pairs={{0,192},{8,56},{16,208},{24,40},{32,224},{40,24},{48,240},{56,8},{... | collective-permute-start | bytes 786440 | tf_op jit(solution)/shard_map/ppermute | solution.py:44
  34.8 11.4 %collective-permute-start.8 = (f32[128,512]{1,0:T(8,128)S(1)}, f32[128,512]{1,0:T(8,128)S(1)}, u32[]{:S(2)}, u32[]{:S(2)}) collective-permute-start(f32[128,512]{1,0:T(8,128)S(1)} %add_add_fusion.refs_0_), channel_id=1, source_target_pairs={{0,128},{8,40},{16,144},{24,56},{32,160},{40,8},{48,176},{56,24},{... | collective-permute-start | bytes 786440 | tf_op jit(solution)/shard_map/ppermute | solution.py:44
  35.0 11.2 %collective-permute-start.7 = (f32[128,512]{1,0:T(8,128)S(1)}, f32[128,512]{1,0:T(8,128)S(1)}, u32[]{:S(2)}, u32[]{:S(2)}) collective-permute-start(f32[128,512]{1,0:T(8,128)S(1)} %add_add_fusion.refs_0_), channel_id=1, source_target_pairs={{0,64},{8,24},{16,80},{24,8},{32,96},{40,56},{48,112},{56,40},{64,... | collective-permute-start | bytes 786440 | tf_op jit(solution)/shard_map/ppermute | solution.py:44
  37.0 10.1 %collective-permute-start.10 = (f32[128,512]{1,0:T(8,128)S(1)}, f32[128,512]{1,0:T(8,128)S(1)}, u32[]{:S(2)}, u32[]{:S(2)}) collective-permute-start(f32[128,512]{1,0:T(8,128)S(1)} %add_add_fusion.refs_0_), channel_id=1, source_target_pairs={{0,8},{8,0},{16,24},{24,16},{32,40},{40,32},{48,56},{56,48},{64,72... | collective-permute-start | bytes 786440 | tf_op jit(solution)/shard_map/ppermute | solution.py:44
  43.3 4.0 %collective-permute-start.13 = (f32[128,512]{1,0:T(8,128)S(1)}, f32[128,512]{1,0:T(8,128)S(1)}, u32[]{:S(2)}, u32[]{:S(2)}) collective-permute-start(f32[128,512]{1,0:T(8,128)S(1)} %collective-permute-done.9.refs_3_), channel_id=1, source_target_pairs={{0,8},{8,0},{16,24},{24,16},{32,40},{40,32},{48,56},{56,48},{64,72... | collective-permute-start | bytes 786440 | tf_op jit(solution)/shard_map/ppermute | solution.py:44
  46.2 1.5 %collective-permute-start.12 = (f32[128,512]{1,0:T(8,128)S(1)}, f32[128,512]{1,0:T(8,128)S(1)}, u32[]{:S(2)}, u32[]{:S(2)}) collective-permute-start(f32[128,512]{1,0:T(8,128)S(1)} %collective-permute-done.8.refs_2_), channel_id=1, source_target_pairs={{0,8},{8,0},{16,24},{24,16},{32,40},{40,32},{48,56},{56,48},{64,72... | collective-permute-start | bytes 786440 | tf_op jit(solution)/shard_map/ppermute | solution.py:44
  46.2 2.1 %collective-permute-start.11 = (f32[128,512]{1,0:T(8,128)S(1)}, f32[128,512]{1,0:T(8,128)S(1)}, u32[]{:S(2)}, u32[]{:S(2)}) collective-permute-start(f32[128,512]{1,0:T(8,128)S(1)} %collective-permute-done.7.refs_1_), channel_id=1, source_target_pairs={{0,8},{8,0},{16,24},{24,16},{32,40},{40,32},{48,56},{56,48},{64,72... | collective-permute-start | bytes 786440 | tf_op jit(solution)/shard_map/ppermute | solution.py:44

commit v2 on v0

v2 whole, which is shorter than its diff:
```python
import jax
import jax.numpy as jnp
from jax import lax
from jax.experimental import pallas as pl
from jax.experimental.pallas import tpu as pltpu
from jax.sharding import PartitionSpec as P

GRIDS = 16
K = 128
BLK = 512
NBD = 1024
LANES = 128
SUB = BLK // LANES
GRID_ROWS = K * SUB
HALF = NBD // 2 * SUB
PIECE = HALF // 4
BATCH = 16
PAD = 64
VMEM = pltpu.VMEM
VMEM_LIMIT = 48 * 1024 * 1024


def device(x, y, core):
    return (x * 4 + y) * 2 + core


def pairs(partner):
    return [
        (device(x, y, c), device(*partner(x, y, c)))
        for x in range(4)
        for y in range(4)
        for c in range(2)
    ]


def own_line(step):
    return pairs(lambda x, y, c: (x, y ^ step, c) if c else (x ^ step, y, c))


def other_line(step):
    return pairs(lambda x, y, c: (x ^ step, y, c) if c else (x, y ^ step, c))


OTHER_CORE = pairs(lambda x, y, c: (x, y, 1 - c))


def send(value, partner):
    return lax.ppermute(value, "grp", partner)


def to_tiles(value):
    g, slots, _ = value.shape
    return value.reshape(g, slots // 8, 8, SUB, LANES).transpose(0, 1, 3, 2, 4).reshape(-1, LANES)


def from_tiles(rows, shape):
    g, slots, blk = shape
    return rows.reshape(g, slots // 8, SUB, 8, LANES).transpose(0, 1, 3, 2, 4).reshape(shape)


def slot_rows(start, slot):
    return pl.ds(start + (slot // 8) * 8 * SUB + slot % 8, SUB, stride=8)


def block_rows(row):
    return pl.ds(pl.multiple_of(row, SUB), SUB)


def piece_rows(where_ref, half, k):
    line = where_ref[1 + half]
    return pl.ds(pl.multiple_of(half * HALF + (line ^ k) * PIECE, PIECE), PIECE)


def scatter(where_ref, coef_hbm, ids_hbm, surplus_hbm, *refs):
    pieces, (table, stage, ids, coef, sems, small_sems) = refs[:8], refs[8:]

    def load(g):
        part = pl.ds(pl.multiple_of(g * GRID_ROWS, GRID_ROWS), GRID_ROWS)
        return pltpu.make_async_copy(surplus_hbm.at[part, :], stage.at[part, :], sems.at[g])

    ids_copy = pltpu.make_async_copy(ids_hbm, ids, small_sems.at[0])
    coef_copy = pltpu.make_async_copy(coef_hbm, coef, small_sems.at[1])
    ids_copy.start()
    coef_copy.start()
    for g in range(GRIDS):
        load(g).start()
    table[...] = jnp.zeros_like(table)
    base = where_ref[0]
    ids_copy.wait()
    coef_copy.wait()

    def add_grid(g, carry):
        load(g).wait()
        factor = coef[g].astype(jnp.float32)
        start = pl.multiple_of(g * GRID_ROWS, GRID_ROWS)
        for first in range(0, K, BATCH):
            slots = range(first, first + BATCH)
            rows = [block_rows((ids[g, j] - base) * SUB) for j in slots]
            sums = [table[r, :] + stage[slot_rows(start, j), :] * factor for r, j in zip(rows, slots)]
            for r, total in zip(rows, sums):
                table[r, :] = total
        return carry

    lax.fori_loop(0, GRIDS, add_grid, 0)
    core = where_ref[3]
    for k in range(4):
        pieces[k][...] = table[piece_rows(where_ref, 1 - core, k), :]
        pieces[4 + k][...] = table[piece_rows(where_ref, core, k), :]


def gather(where_ref, rows_vmem, *refs):
    pieces, (out_hbm, table, stage, rows_ref, sems, rows_sem) = refs[:8], refs[8:]
    rows_copy = pltpu.make_async_copy(rows_vmem, rows_ref, rows_sem)
    rows_copy.start()
    core = where_ref[3]
    for k in range(4):
        table[piece_rows(where_ref, core, k), :] = pieces[k][...]
        table[piece_rows(where_ref, 1 - core, k), :] = pieces[4 + k][...]
    rows_copy.wait()

    def store(g):
        part = pl.ds(pl.multiple_of(g * GRID_ROWS, GRID_ROWS), GRID_ROWS)
        return pltpu.make_async_copy(stage.at[part, :], out_hbm.at[part, :], sems.at[g])

    def copy_grid(g, carry):
        start = pl.multiple_of(g * GRID_ROWS, GRID_ROWS)
        for first in range(0, K, BATCH):
            slots = range(first, first + BATCH)
            values = [table[block_rows(rows_ref[g, j]), :] for j in slots]
            for j, value in zip(slots, values):
                stage[slot_rows(start, j), :] = value
        store(g).start()
        return carry

    lax.fori_loop(0, GRIDS, copy_grid, 0)
    for g in range(GRIDS):
        store(g).wait()


def local(surplus, block_ids, coef):
    index = lax.axis_index("grp")
    base = lax.axis_index("dom") * NBD
    where = jnp.stack([base, index >> 3, (index >> 1) & 3, index & 1]).astype(jnp.int32)
    smem = pl.BlockSpec(memory_space=pltpu.SMEM)
    vmem = pl.BlockSpec(memory_space=VMEM)
    hbm = pl.BlockSpec(memory_space=pltpu.HBM)
    params = pltpu.CompilerParams(vmem_limit_bytes=VMEM_LIMIT)
    piece = jax.ShapeDtypeStruct((PIECE, LANES), jnp.float32)
    table = VMEM((NBD * SUB + PAD, LANES), jnp.float32)
    stage = VMEM((GRIDS * GRID_ROWS + PAD, LANES), jnp.float32)
    parts = pl.pallas_call(
        scatter,
        out_shape=(piece,) * 8,
        in_specs=[smem, hbm, hbm, hbm],
        out_specs=(vmem,) * 8,
        scratch_shapes=[
            table,
            stage,
            pltpu.SMEM((GRIDS, K), jnp.int32),
            pltpu.SMEM((GRIDS,), jnp.int32),
            pltpu.SemaphoreType.DMA((GRIDS,)),
            pltpu.SemaphoreType.DMA((2,)),
        ],
        compiler_params=params,
    )(where, *(pltpu.with_memory_space_constraint(v, pltpu.HBM) for v in (coef, block_ids, to_tiles(surplus))))
    parts = [own + send(other, OTHER_CORE) for other, own in zip(parts[:4], parts[4:])]
    got = [send(parts[k], own_line(k)) for k in (2, 1, 3)]
    share = parts[0] + got[0] + got[1] + got[2]
    got = [send(share, other_line(k)) for k in (3, 1, 2)]
    share = share + got[0] + got[1] + got[2]
    got = {k: send(share, own_line(k)) for k in (3, 1, 2)}
    line = [share, got[1], got[2], got[3]]
    across = [send(part, OTHER_CORE) for part in line]
    rows = (block_ids - base) * SUB
    out = pl.pallas_call(
        gather,
        out_shape=jax.ShapeDtypeStruct((GRIDS * GRID_ROWS, LANES), jnp.float32),
        in_specs=[smem, vmem] + [vmem] * 8,
        out_specs=hbm,
        scratch_shapes=[
            table,
            stage,
            pltpu.SMEM((GRIDS, K), jnp.int32),
            pltpu.SemaphoreType.DMA((GRIDS,)),
            pltpu.SemaphoreType.DMA,
        ],
        compiler_params=params,
    )(where, rows, *line, *across)
    return from_tiles(out, surplus.shape)


def solution(mesh):
    return jax.shard_map(
        local,
        mesh=mesh,
        in_specs=(P("grp", "dom", None), P("grp", "dom"), P("grp")),
        out_specs=P("grp", "dom", None),
        check_vma=False,
    )
```

time: 95 us -> 48.5 us (0.51)
  blocking collectives: 68.4 us -> 0 us
  matrix products: 24.6 us -> 0 us
  starting transfers between devices: 0 us -> 20.9 us
  waiting for transfers between devices: 0 us -> 18 us
  Pallas kernels: 0 us -> 9.2 us
  other arithmetic: 1.5 us -> 0.28 us
    all_to_all x2 -> x0, blocking collectives: 68.4 us -> none  [the longest x1 36.5 us: summed_on_arrival(): lax.all_to_all(parts, axis, split_axis=0, concat_axis=0, tiled=True)]
    dot_general x2 -> x0, matrix products: 24.6 us -> none  [the longest x1 16.3 us: local(): jnp.einsum('gkn,gkb->nb', onehot, scaled, precision=lax.Precision.HIGHEST)]
    ppermute x0 -> x17, starting transfers between devices: none -> 20.9 us  [send(): return lax.ppermute(value, 'grp', partner)]
    ppermute x0 -> x17, waiting for transfers between devices: none -> 18 us  [send(): return lax.ppermute(value, 'grp', partner)]
    pallas_call x0 -> x2, Pallas kernels: none -> 9.2 us  [the longest x1 5.12 us: local(): pl.pallas_call(scatter, out_shape=(piece,) * 8, in_specs=[smem, hbm, hbm,...]
  transfers between devices with their start and end apart: 0 -> 17, of which waited for: 0 -> 11; matrix products, arithmetic and copies ran while one was open for 0% -> 0% of each run, Pallas kernels for 0% -> 0%
where the time goes in v2:
time: 48.5 us; the launch traced here: 48.4 us
  starting transfers between devices  20.9 us (43%)
  waiting for transfers between devices  18 us (37%)
  Pallas kernels  9.2 us (19%)
    ppermute x17, starting transfers between devices, send(): return lax.ppermute(value, 'grp', partner)  20.9 us
    ppermute x17, waiting for transfers between devices, send(): return lax.ppermute(value, 'grp', partner)  18 us
    pallas_call x1, Pallas kernels, local(): pl.pallas_call(scatter, out_shape=(piece,) * 8, in_specs=[smem, hbm, hbm,...  5.12 us
    pallas_call x1, Pallas kernels, local(): pl.pallas_call(gather, out_shape=jax.ShapeDtypeStruct((GRIDS * GRID_ROWS,...  4.08 us
  transfers between devices with their start and end apart: 17, of which 11 were waited for; matrix products, arithmetic and copies ran while one was open for 0% of the time, Pallas kernels for 0%

profile of v2, /device:TPU:1, one launch (start us, length us, event | category | flops | bytes accessed | tf_op | source)
XLA Modules:
  0.0 48.4 jit_solution(4689334687517489912)
XLA Ops:
  0.0 0.1 pad_add_fusion.where_ref
  0.1 0.0 copy-start
  0.1 5.1 %shard_map.37 = (f32[512,128]{1,0:T(8,128)S(1)}, f32[512,128]{1,0:T(8,128)S(1)}, f32[512,128]{1,0:T(8,128)S(1)}, f32[512,128]{1,0:T(8,128)S(1)}, f32[512,128]{1,...) custom-call(s32[4]{0:T(128)S(1)} %pad_add_fusion.where_ref, s32[16]{0:T(128)} %coef_hbm.1, ...), custom_call_target="tpu_custom_call" | custom-call | tf_op jit(solution)/shard_map/pallas_call | solution.py:151
  5.2 3.3 %collective-permute-start.1 = (f32[512,128]{1,0:T(8,128)S(1)}, f32[512,128]{1,0:T(8,128)S(1)}, u32[]{:S(2)}, u32[]{:S(2)}) collective-permute-start(f32[512,128]{1,0:T(8,128)S(1)} %get-tuple-element.16), channel_id=1, source_target_pairs={{0,8},{8,0},{16,24},{24,16},{32,40},{40,32},{48,56},{56,48},{64,72... | collective-permute-start | bytes 786440 | tf_op jit(solution)/shard_map/ppermute | solution.py:48
  8.5 0.1 collective-permute-start.3
  8.6 0.4 collective-permute-start.5
  9.0 0.1 collective-permute-start
  9.1 0.6 %collective-permute-done.1 = f32[512,128]{1,0:T(8,128)S(1)} collective-permute-done((f32[512,128]{1,0:T(8,128)S(1)}, f32[512,128]{1,0:T(8,128)S(1)}, u32[]{:S(2)}, u32[]{:S(2)}) %collective-permute-start.1) | collective-permute-done | bytes 262176 | tf_op jit(solution)/shard_map/ppermute | solution.py:48
  9.7 1.3 %collective-permute-start.2 = (f32[512,128]{1,0:T(8,128)S(1)}, f32[512,128]{1,0:T(8,128)S(1)}, u32[]{:S(2)}, u32[]{:S(2)}) collective-permute-start(f32[512,128]{1,0:T(8,128)S(1)} %add.31), channel_id=1, source_target_pairs={{0,128},{8,40},{16,144},{24,56},{32,160},{40,8},{48,176},{56,24},{... | collective-permute-start | bytes 786440 | tf_op jit(solution)/shard_map/ppermute | solution.py:48
  11.0 0.0 collective-permute-done.3
  11.0 0.5 %collective-permute-start.4 = (f32[512,128]{1,0:T(8,128)S(1)}, f32[512,128]{1,0:T(8,128)S(1)}, u32[]{:S(2)}, u32[]{:S(2)}) collective-permute-start(f32[512,128]{1,0:T(8,128)S(1)} %add.33), channel_id=1, source_target_pairs={{0,64},{8,24},{16,80},{24,8},{32,96},{40,56},{48,112},{56,40},{64,... | collective-permute-start | bytes 786440 | tf_op jit(solution)/shard_map/ppermute | solution.py:48
  11.5 0.0 collective-permute-done.5
  11.5 1.8 %collective-permute-start.6 = (f32[512,128]{1,0:T(8,128)S(1)}, f32[512,128]{1,0:T(8,128)S(1)}, u32[]{:S(2)}, u32[]{:S(2)}) collective-permute-start(f32[512,128]{1,0:T(8,128)S(1)} %add.35), channel_id=1, source_target_pairs={{0,192},{8,56},{16,208},{24,40},{32,224},{40,24},{48,240},{56,8},{... | collective-permute-start | bytes 786440 | tf_op jit(solution)/shard_map/ppermute | solution.py:48
  13.3 0.0 collective-permute-done
  13.3 3.5 %collective-permute-done.2 = f32[512,128]{1,0:T(8,128)S(1)} collective-permute-done((f32[512,128]{1,0:T(8,128)S(1)}, f32[512,128]{1,0:T(8,128)S(1)}, u32[]{:S(2)}, u32[]{:S(2)}) %collective-permute-start.2) | collective-permute-done | bytes 262176 | tf_op jit(solution)/shard_map/ppermute | solution.py:48
  16.8 1.4 %collective-permute-done.4 = f32[512,128]{1,0:T(8,128)S(1)} collective-permute-done((f32[512,128]{1,0:T(8,128)S(1)}, f32[512,128]{1,0:T(8,128)S(1)}, u32[]{:S(2)}, u32[]{:S(2)}) %collective-permute-start.4) | collective-permute-done | bytes 262176 | tf_op jit(solution)/shard_map/ppermute | solution.py:48
  18.2 1.4 %collective-permute-done.6 = f32[512,128]{1,0:T(8,128)S(1)} collective-permute-done((f32[512,128]{1,0:T(8,128)S(1)}, f32[512,128]{1,0:T(8,128)S(1)}, u32[]{:S(2)}, u32[]{:S(2)}) %collective-permute-start.6) | collective-permute-done | bytes 262176 | tf_op jit(solution)/shard_map/ppermute | solution.py:48
  19.6 0.1 add_add_fusion.1
  19.7 1.5 %collective-permute-start.9 = (f32[512,128]{1,0:T(8,128)S(1)}, f32[512,128]{1,0:T(8,128)S(1)}, u32[]{:S(2)}, u32[]{:S(2)}) collective-permute-start(f32[512,128]{1,0:T(8,128)S(1)} %add_add_fusion.1), channel_id=1, source_target_pairs={{0,32},{8,136},{16,48},{24,152},{32,0},{40,168},{48,16},{56,184},{... | collective-permute-start | bytes 786440 | tf_op jit(solution)/shard_map/ppermute | solution.py:48
  21.2 0.4 collective-permute-start.8
  21.6 1.5 %collective-permute-start.7 = (f32[512,128]{1,0:T(8,128)S(1)}, f32[512,128]{1,0:T(8,128)S(1)}, u32[]{:S(2)}, u32[]{:S(2)}) collective-permute-start(f32[512,128]{1,0:T(8,128)S(1)} %add_add_fusion.1), channel_id=1, source_target_pairs={{0,48},{8,200},{16,32},{24,216},{32,16},{40,232},{48,0},{56,248},{... | collective-permute-start | bytes 786440 | tf_op jit(solution)/shard_map/ppermute | solution.py:48
  23.0 3.8 %collective-permute-done.9 = f32[512,128]{1,0:T(8,128)S(1)} collective-permute-done((f32[512,128]{1,0:T(8,128)S(1)}, f32[512,128]{1,0:T(8,128)S(1)}, u32[]{:S(2)}, u32[]{:S(2)}) %collective-permute-start.9) | collective-permute-done | bytes 262176 | tf_op jit(solution)/shard_map/ppermute | solution.py:48
  26.8 1.6 %collective-permute-done.8 = f32[512,128]{1,0:T(8,128)S(1)} collective-permute-done((f32[512,128]{1,0:T(8,128)S(1)}, f32[512,128]{1,0:T(8,128)S(1)}, u32[]{:S(2)}, u32[]{:S(2)}) %collective-permute-start.8) | collective-permute-done | bytes 262176 | tf_op jit(solution)/shard_map/ppermute | solution.py:48
  28.4 1.2 %collective-permute-done.7 = f32[512,128]{1,0:T(8,128)S(1)} collective-permute-done((f32[512,128]{1,0:T(8,128)S(1)}, f32[512,128]{1,0:T(8,128)S(1)}, u32[]{:S(2)}, u32[]{:S(2)}) %collective-permute-start.7) | collective-permute-done | bytes 262176 | tf_op jit(solution)/shard_map/ppermute | solution.py:48
  29.7 1.2 %collective-permute-start.12 = (f32[512,128]{1,0:T(8,128)S(1)}, f32[512,128]{1,0:T(8,128)S(1)}, u32[]{:S(2)}, u32[]{:S(2)}) collective-permute-start(f32[512,128]{1,0:T(8,128)S(1)} %add_add_fusion.refs_0_), channel_id=1, source_target_pairs={{0,192},{8,56},{16,208},{24,40},{32,224},{40,24},{48,240},{56,8},{... | collective-permute-start | bytes 786440 | tf_op jit(solution)/shard_map/ppermute | solution.py:48
  30.9 0.5 %collective-permute-start.11 = (f32[512,128]{1,0:T(8,128)S(1)}, f32[512,128]{1,0:T(8,128)S(1)}, u32[]{:S(2)}, u32[]{:S(2)}) collective-permute-start(f32[512,128]{1,0:T(8,128)S(1)} %add_add_fusion.refs_0_), channel_id=1, source_target_pairs={{0,128},{8,40},{16,144},{24,56},{32,160},{40,8},{48,176},{56,24},{... | collective-permute-start | bytes 786440 | tf_op jit(solution)/shard_map/ppermute | solution.py:48
  31.4 1.6 %collective-permute-start.10 = (f32[512,128]{1,0:T(8,128)S(1)}, f32[512,128]{1,0:T(8,128)S(1)}, u32[]{:S(2)}, u32[]{:S(2)}) collective-permute-start(f32[512,128]{1,0:T(8,128)S(1)} %add_add_fusion.refs_0_), channel_id=1, source_target_pairs={{0,64},{8,24},{16,80},{24,8},{32,96},{40,56},{48,112},{56,40},{64,... | collective-permute-start | bytes 786440 | tf_op jit(solution)/shard_map/ppermute | solution.py:48
  33.0 2.9 %collective-permute-start.13 = (f32[512,128]{1,0:T(8,128)S(1)}, f32[512,128]{1,0:T(8,128)S(1)}, u32[]{:S(2)}, u32[]{:S(2)}) collective-permute-start(f32[512,128]{1,0:T(8,128)S(1)} %add_add_fusion.refs_0_), channel_id=1, source_target_pairs={{0,8},{8,0},{16,24},{24,16},{32,40},{40,32},{48,56},{56,48},{64,72... | collective-permute-start | bytes 786440 | tf_op jit(solution)/shard_map/ppermute | solution.py:48
  35.9 3.4 %collective-permute-done.12.refs_3_ = f32[512,128]{1,0:T(8,128)S(1)} collective-permute-done((f32[512,128]{1,0:T(8,128)S(1)}, f32[512,128]{1,0:T(8,128)S(1)}, u32[]{:S(2)}, u32[]{:S(2)}) %collective-permute-start.12) | collective-permute-done | bytes 262176 | tf_op jit(solution)/shard_map/ppermute | solution.py:48
  39.3 2.9 %collective-permute-start.16 = (f32[512,128]{1,0:T(8,128)S(1)}, f32[512,128]{1,0:T(8,128)S(1)}, u32[]{:S(2)}, u32[]{:S(2)}) collective-permute-start(f32[512,128]{1,0:T(8,128)S(1)} %collective-permute-done.12.refs_3_), channel_id=1, source_target_pairs={{0,8},{8,0},{16,24},{24,16},{32,40},{40,32},{48,56},{56,48},{64,72... | collective-permute-start | bytes 786440 | tf_op jit(solution)/shard_map/ppermute | solution.py:48
  42.2 0.0 collective-permute-done.11.refs_2_
  42.2 0.0 collective-permute-start.15
  42.2 0.0 collective-permute-done.10.refs_1_
  42.3 0.9 %collective-permute-start.14 = (f32[512,128]{1,0:T(8,128)S(1)}, f32[512,128]{1,0:T(8,128)S(1)}, u32[]{:S(2)}, u32[]{:S(2)}) collective-permute-start(f32[512,128]{1,0:T(8,128)S(1)} %collective-permute-done.10.refs_1_), channel_id=1, source_target_pairs={{0,8},{8,0},{16,24},{24,16},{32,40},{40,32},{48,56},{56,48},{64,72... | collective-permute-start | bytes 786440 | tf_op jit(solution)/shard_map/ppermute | solution.py:48
  43.1 0.0 copy-done
  43.1 0.0 collective-permute-done.13.refs_4_
  43.2 0.2 collective-permute-done.16.refs_7_
  43.4 0.4 collective-permute-done.15.refs_6_
  43.8 0.5 %collective-permute-done.14.refs_5_ = f32[512,128]{1,0:T(8,128)S(1)} collective-permute-done((f32[512,128]{1,0:T(8,128)S(1)}, f32[512,128]{1,0:T(8,128)S(1)}, u32[]{:S(2)}, u32[]{:S(2)}) %collective-permute-start.14) | collective-permute-done | bytes 262176 | tf_op jit(solution)/shard_map/ppermute | solution.py:48
  44.3 4.1 %shard_map.38 = f32[8192,128]{1,0:T(8,128)} custom-call(s32[4]{0:T(128)S(1)} %pad_add_fusion.where_ref, s32[16,128]{1,0:T(8,128)S(1)} %subtract_multiply_fusion.rows_vmem, f32[512,128]{1,0:T(8,128)S(1)} %add_add_fusion.refs_0_, f32[512,128]{1,0:T(8,128)S(1)} %collective-permute-done.10.refs_1_, f32[512,128]{1,0:T(8,128)S(1)} %collective-permute-done.11.refs_2_, ...), custom_call_target="tpu_custom_call" | custom-call | tf_op jit(solution)/shard_map/pallas_call | solution.py:175
  (5 shorter events, 0.1 us)
Async XLA Ops:
  0.1 43.1 %copy-start = (s32[16,128]{1,0:T(8,128)S(1)}, s32[16,128]{1,0:T(8,128)}, u32[]{:S(2)}) copy-start(s32[16,128]{1,0:T(8,128)} %ids_hbm.1) | copy-start | bytes 24580
  5.2 4.5 %collective-permute-start.1 = (f32[512,128]{1,0:T(8,128)S(1)}, f32[512,128]{1,0:T(8,128)S(1)}, u32[]{:S(2)}, u32[]{:S(2)}) collective-permute-start(f32[512,128]{1,0:T(8,128)S(1)} %get-tuple-element.16), channel_id=1, source_target_pairs={{0,8},{8,0},{16,24},{24,16},{32,40},{40,32},{48,56},{56,48},{64,72... | collective-permute-start | bytes 786440 | tf_op jit(solution)/shard_map/ppermute | solution.py:48
  8.5 2.5 %collective-permute-start.3 = (f32[512,128]{1,0:T(8,128)S(1)}, f32[512,128]{1,0:T(8,128)S(1)}, u32[]{:S(2)}, u32[]{:S(2)}) collective-permute-start(f32[512,128]{1,0:T(8,128)S(1)} %get-tuple-element.18), channel_id=1, source_target_pairs={{0,8},{8,0},{16,24},{24,16},{32,40},{40,32},{48,56},{56,48},{64,72... | collective-permute-start | bytes 786440 | tf_op jit(solution)/shard_map/ppermute | solution.py:48
  8.6 2.9 %collective-permute-start.5 = (f32[512,128]{1,0:T(8,128)S(1)}, f32[512,128]{1,0:T(8,128)S(1)}, u32[]{:S(2)}, u32[]{:S(2)}) collective-permute-start(f32[512,128]{1,0:T(8,128)S(1)} %get-tuple-element.20), channel_id=1, source_target_pairs={{0,8},{8,0},{16,24},{24,16},{32,40},{40,32},{48,56},{56,48},{64,72... | collective-permute-start | bytes 786440 | tf_op jit(solution)/shard_map/ppermute | solution.py:48
  9.0 4.3 %collective-permute-start = (f32[512,128]{1,0:T(8,128)S(1)}, f32[512,128]{1,0:T(8,128)S(1)}, u32[]{:S(2)}, u32[]{:S(2)}) collective-permute-start(f32[512,128]{1,0:T(8,128)S(1)} %get-tuple-element.14), channel_id=1, source_target_pairs={{0,8},{8,0},{16,24},{24,16},{32,40},{40,32},{48,56},{56,48},{64,72... | collective-permute-start | bytes 786440 | tf_op jit(solution)/shard_map/ppermute | solution.py:48
  9.7 7.1 %collective-permute-start.2 = (f32[512,128]{1,0:T(8,128)S(1)}, f32[512,128]{1,0:T(8,128)S(1)}, u32[]{:S(2)}, u32[]{:S(2)}) collective-permute-start(f32[512,128]{1,0:T(8,128)S(1)} %add.31), channel_id=1, source_target_pairs={{0,128},{8,40},{16,144},{24,56},{32,160},{40,8},{48,176},{56,24},{... | collective-permute-start | bytes 786440 | tf_op jit(solution)/shard_map/ppermute | solution.py:48
  11.0 7.2 %collective-permute-start.4 = (f32[512,128]{1,0:T(8,128)S(1)}, f32[512,128]{1,0:T(8,128)S(1)}, u32[]{:S(2)}, u32[]{:S(2)}) collective-permute-start(f32[512,128]{1,0:T(8,128)S(1)} %add.33), channel_id=1, source_target_pairs={{0,64},{8,24},{16,80},{24,8},{32,96},{40,56},{48,112},{56,40},{64,... | collective-permute-start | bytes 786440 | tf_op jit(solution)/shard_map/ppermute | solution.py:48
  11.5 8.1 %collective-permute-start.6 = (f32[512,128]{1,0:T(8,128)S(1)}, f32[512,128]{1,0:T(8,128)S(1)}, u32[]{:S(2)}, u32[]{:S(2)}) collective-permute-start(f32[512,128]{1,0:T(8,128)S(1)} %add.35), channel_id=1, source_target_pairs={{0,192},{8,56},{16,208},{24,40},{32,224},{40,24},{48,240},{56,8},{... | collective-permute-start | bytes 786440 | tf_op jit(solution)/shard_map/ppermute | solution.py:48
  19.7 7.1 %collective-permute-start.9 = (f32[512,128]{1,0:T(8,128)S(1)}, f32[512,128]{1,0:T(8,128)S(1)}, u32[]{:S(2)}, u32[]{:S(2)}) collective-permute-start(f32[512,128]{1,0:T(8,128)S(1)} %add_add_fusion.1), channel_id=1, source_target_pairs={{0,32},{8,136},{16,48},{24,152},{32,0},{40,168},{48,16},{56,184},{... | collective-permute-start | bytes 786440 | tf_op jit(solution)/shard_map/ppermute | solution.py:48
  21.2 7.2 %collective-permute-start.8 = (f32[512,128]{1,0:T(8,128)S(1)}, f32[512,128]{1,0:T(8,128)S(1)}, u32[]{:S(2)}, u32[]{:S(2)}) collective-permute-start(f32[512,128]{1,0:T(8,128)S(1)} %add_add_fusion.1), channel_id=1, source_target_pairs={{0,16},{8,72},{16,0},{24,88},{32,48},{40,104},{48,32},{56,120},{64... | collective-permute-start | bytes 786440 | tf_op jit(solution)/shard_map/ppermute | solution.py:48
  21.6 8.1 %collective-permute-start.7 = (f32[512,128]{1,0:T(8,128)S(1)}, f32[512,128]{1,0:T(8,128)S(1)}, u32[]{:S(2)}, u32[]{:S(2)}) collective-permute-start(f32[512,128]{1,0:T(8,128)S(1)} %add_add_fusion.1), channel_id=1, source_target_pairs={{0,48},{8,200},{16,32},{24,216},{32,16},{40,232},{48,0},{56,248},{... | collective-permute-start | bytes 786440 | tf_op jit(solution)/shard_map/ppermute | solution.py:48
  29.7 9.6 %collective-permute-start.12 = (f32[512,128]{1,0:T(8,128)S(1)}, f32[512,128]{1,0:T(8,128)S(1)}, u32[]{:S(2)}, u32[]{:S(2)}) collective-permute-start(f32[512,128]{1,0:T(8,128)S(1)} %add_add_fusion.refs_0_), channel_id=1, source_target_pairs={{0,192},{8,56},{16,208},{24,40},{32,224},{40,24},{48,240},{56,8},{... | collective-permute-start | bytes 786440 | tf_op jit(solution)/shard_map/ppermute | solution.py:48
  30.9 11.3 %collective-permute-start.11 = (f32[512,128]{1,0:T(8,128)S(1)}, f32[512,128]{1,0:T(8,128)S(1)}, u32[]{:S(2)}, u32[]{:S(2)}) collective-permute-start(f32[512,128]{1,0:T(8,128)S(1)} %add_add_fusion.refs_0_), channel_id=1, source_target_pairs={{0,128},{8,40},{16,144},{24,56},{32,160},{40,8},{48,176},{56,24},{... | collective-permute-start | bytes 786440 | tf_op jit(solution)/shard_map/ppermute | solution.py:48
  31.4 10.8 %collective-permute-start.10 = (f32[512,128]{1,0:T(8,128)S(1)}, f32[512,128]{1,0:T(8,128)S(1)}, u32[]{:S(2)}, u32[]{:S(2)}) collective-permute-start(f32[512,128]{1,0:T(8,128)S(1)} %add_add_fusion.refs_0_), channel_id=1, source_target_pairs={{0,64},{8,24},{16,80},{24,8},{32,96},{40,56},{48,112},{56,40},{64,... | collective-permute-start | bytes 786440 | tf_op jit(solution)/shard_map/ppermute | solution.py:48
  33.0 10.1 %collective-permute-start.13 = (f32[512,128]{1,0:T(8,128)S(1)}, f32[512,128]{1,0:T(8,128)S(1)}, u32[]{:S(2)}, u32[]{:S(2)}) collective-permute-start(f32[512,128]{1,0:T(8,128)S(1)} %add_add_fusion.refs_0_), channel_id=1, source_target_pairs={{0,8},{8,0},{16,24},{24,16},{32,40},{40,32},{48,56},{56,48},{64,72... | collective-permute-start | bytes 786440 | tf_op jit(solution)/shard_map/ppermute | solution.py:48
  39.3 4.1 %collective-permute-start.16 = (f32[512,128]{1,0:T(8,128)S(1)}, f32[512,128]{1,0:T(8,128)S(1)}, u32[]{:S(2)}, u32[]{:S(2)}) collective-permute-start(f32[512,128]{1,0:T(8,128)S(1)} %collective-permute-done.12.refs_3_), channel_id=1, source_target_pairs={{0,8},{8,0},{16,24},{24,16},{32,40},{40,32},{48,56},{56,48},{64,72... | collective-permute-start | bytes 786440 | tf_op jit(solution)/shard_map/ppermute | solution.py:48
  42.2 1.5 %collective-permute-start.15 = (f32[512,128]{1,0:T(8,128)S(1)}, f32[512,128]{1,0:T(8,128)S(1)}, u32[]{:S(2)}, u32[]{:S(2)}) collective-permute-start(f32[512,128]{1,0:T(8,128)S(1)} %collective-permute-done.11.refs_2_), channel_id=1, source_target_pairs={{0,8},{8,0},{16,24},{24,16},{32,40},{40,32},{48,56},{56,48},{64,72... | collective-permute-start | bytes 786440 | tf_op jit(solution)/shard_map/ppermute | solution.py:48
  42.3 2.1 %collective-permute-start.14 = (f32[512,128]{1,0:T(8,128)S(1)}, f32[512,128]{1,0:T(8,128)S(1)}, u32[]{:S(2)}, u32[]{:S(2)}) collective-permute-start(f32[512,128]{1,0:T(8,128)S(1)} %collective-permute-done.10.refs_1_), channel_id=1, source_target_pairs={{0,8},{8,0},{16,24},{24,16},{32,40},{40,32},{48,56},{56,48},{64,72... | collective-permute-start | bytes 786440 | tf_op jit(solution)/shard_map/ppermute | solution.py:48

commit v3 on v2

--- a/solution.py
+++ b/solution.py
@@ -33,14 +33,18 @@
     ]
 
 
-def own_line(step):
-    return pairs(lambda x, y, c: (x, y ^ step, c) if c else (x ^ step, y, c))
-
-
-def other_line(step):
-    return pairs(lambda x, y, c: (x ^ step, y, c) if c else (x, y ^ step, c))
-
-
+def far(line):
+    if line == "x":
+        return pairs(lambda x, y, c: (x ^ (3 - c), y, c))
+    return pairs(lambda x, y, c: (x, y ^ (3 - c), c))
+
+
+def along_y(step):
+    return pairs(lambda x, y, c: (x, y ^ step, c))
+
+
+NEAR_X = pairs(lambda x, y, c: (x ^ 1, y, c))
+FAR_X = far("x")
 OTHER_CORE = pairs(lambda x, y, c: (x, y, 1 - c))
 
 
@@ -66,9 +70,13 @@
     return pl.ds(pl.multiple_of(row, SUB), SUB)
 
 
-def piece_rows(where_ref, half, k):
-    line = where_ref[1 + half]
-    return pl.ds(pl.multiple_of(half * HALF + (line ^ k) * PIECE, PIECE), PIECE)
+def piece_rows(where_ref):
+    x, core = where_ref[1], where_ref[2]
+    rows = []
+    for c in (core, 1 - core):
+        for half, step in ((1 - c, 3 - c), (c, 3 - c), (c, 1), (c, 0)):
+            rows.append(pl.ds(pl.multiple_of(half * HALF + (x ^ step) * PIECE, PIECE), PIECE))
+    return rows
 
 
 def scatter(where_ref, coef_hbm, ids_hbm, surplus_hbm, *refs):
@@ -102,20 +110,16 @@
         return carry
 
     lax.fori_loop(0, GRIDS, add_grid, 0)
-    core = where_ref[3]
-    for k in range(4):
-        pieces[k][...] = table[piece_rows(where_ref, 1 - core, k), :]
-        pieces[4 + k][...] = table[piece_rows(where_ref, core, k), :]
+    for piece, rows in zip(pieces, piece_rows(where_ref)):
+        piece[...] = table[rows, :]
 
 
 def gather(where_ref, rows_vmem, *refs):
     pieces, (out_hbm, table, stage, rows_ref, sems, rows_sem) = refs[:8], refs[8:]
     rows_copy = pltpu.make_async_copy(rows_vmem, rows_ref, rows_sem)
     rows_copy.start()
-    core = where_ref[3]
-    for k in range(4):
-        table[piece_rows(where_ref, core, k), :] = pieces[k][...]
-        table[piece_rows(where_ref, 1 - core, k), :] = pieces[4 + k][...]
+    for piece, rows in zip(pieces, piece_rows(where_ref)):
+        table[rows, :] = piece[...]
     rows_copy.wait()
 
     def store(g):
@@ -140,7 +144,7 @@
 def local(surplus, block_ids, coef):
     index = lax.axis_index("grp")
     base = lax.axis_index("dom") * NBD
-    where = jnp.stack([base, index >> 3, (index >> 1) & 3, index & 1]).astype(jnp.int32)
+    where = jnp.stack([base, index >> 3, index & 1]).astype(jnp.int32)
     smem = pl.BlockSpec(memory_space=pltpu.SMEM)
     vmem = pl.BlockSpec(memory_space=VMEM)
     hbm = pl.BlockSpec(memory_space=pltpu.HBM)
@@ -163,14 +167,19 @@
         ],
         compiler_params=params,
     )(where, *(pltpu.with_memory_space_constraint(v, pltpu.HBM) for v in (coef, block_ids, to_tiles(surplus))))
-    parts = [own + send(other, OTHER_CORE) for other, own in zip(parts[:4], parts[4:])]
-    got = [send(parts[k], own_line(k)) for k in (2, 1, 3)]
-    share = parts[0] + got[0] + got[1] + got[2]
-    got = [send(share, other_line(k)) for k in (3, 1, 2)]
-    share = share + got[0] + got[1] + got[2]
-    got = {k: send(share, own_line(k)) for k in (3, 1, 2)}
-    line = [share, got[1], got[2], got[3]]
-    across = [send(part, OTHER_CORE) for part in line]
+    swap = lambda value: send(value, OTHER_CORE)
+    crossing, straight, near, own = [mine + swap(theirs) for mine, theirs in zip(parts[:4], parts[4:])]
+    crossing = send(crossing, FAR_X)
+    straight = send(straight, FAR_X)
+    near = send(near, NEAR_X)
+    share = own + straight + swap(crossing) + near
+    got = [send(share, along_y(k)) for k in (3, 1, 2)]
+    own = share + got[0] + got[1] + got[2]
+    straight = send(own, FAR_X)
+    other = swap(own)
+    crossing = send(other, FAR_X)
+    near = send(own, NEAR_X)
+    mine = [swap(crossing), swap(straight), swap(near), other]
     rows = (block_ids - base) * SUB
     out = pl.pallas_call(
         gather,
@@ -185,7 +194,7 @@
             pltpu.SemaphoreType.DMA,
         ],
         compiler_params=params,
-    )(where, rows, *line, *across)
+    )(where, rows, crossing, straight, near, own, *mine)
     return from_tiles(out, surplus.shape)
 
 

time: 48.5 us -> 62.7 us (1.29)
  waiting for transfers between devices: 18 us -> 27.4 us
  starting transfers between devices: 20.9 us -> 25.8 us
    ppermute x17 -> x18, waiting for transfers between devices: 18 us -> 27.4 us  [send(): return lax.ppermute(value, 'grp', partner)]
    ppermute x17 -> x18, starting transfers between devices: 20.9 us -> 25.8 us  [send(): return lax.ppermute(value, 'grp', partner)]
  transfers between devices with their start and end apart: 17 -> 18, of which waited for: 11 -> 11; matrix products, arithmetic and copies ran while one was open for 0% -> 0% of each run, Pallas kernels for 0% -> 0%
where the time goes in v3:
time: 62.7 us
  waiting for transfers between devices  27.4 us (44%)
  starting transfers between devices  25.8 us (41%)
  Pallas kernels  9.17 us (15%)
    ppermute x18, waiting for transfers between devices, send(): return lax.ppermute(value, 'grp', partner)  27.4 us
    ppermute x18, starting transfers between devices, send(): return lax.ppermute(value, 'grp', partner)  25.8 us
    pallas_call x1, Pallas kernels, local(): pl.pallas_call(scatter, out_shape=(piece,) * 8, in_specs=[smem, hbm, hbm,...  5.11 us
    pallas_call x1, Pallas kernels, local(): pl.pallas_call(gather, out_shape=jax.ShapeDtypeStruct((GRIDS * GRID_ROWS,...  4.06 us
  transfers between devices with their start and end apart: 18, of which 11 were waited for; matrix products, arithmetic and copies ran while one was open for 0% of the time, Pallas kernels for 0%

profile of v3, /device:TPU:1, one launch (start us, length us, event | category | flops | bytes accessed | tf_op | source)
XLA Modules:
  0.0 62.7 jit_solution(9343799676524105817)
XLA Ops:
  0.0 0.1 pad_add_fusion.where_ref
  0.1 0.0 copy-start
  0.1 5.1 %shard_map.37 = (f32[512,128]{1,0:T(8,128)S(1)}, f32[512,128]{1,0:T(8,128)S(1)}, f32[512,128]{1,0:T(8,128)S(1)}, f32[512,128]{1,0:T(8,128)S(1)}, f32[512,128]{1,...) custom-call(s32[3]{0:T(128)S(1)} %pad_add_fusion.where_ref, s32[16]{0:T(128)} %coef_hbm.1, ...), custom_call_target="tpu_custom_call" | custom-call | tf_op jit(solution)/shard_map/pallas_call | solution.py:155
  5.2 3.3 %collective-permute-start.3 = (f32[512,128]{1,0:T(8,128)S(1)}, f32[512,128]{1,0:T(8,128)S(1)}, u32[]{:S(2)}, u32[]{:S(2)}) collective-permute-start(f32[512,128]{1,0:T(8,128)S(1)} %get-tuple-element.18), channel_id=1, source_target_pairs={{0,8},{8,0},{16,24},{24,16},{32,40},{40,32},{48,56},{56,48},{64,72... | collective-permute-start | bytes 786440 | tf_op jit(solution)/shard_map/ppermute | solution.py:52
  8.5 0.1 collective-permute-start.1
  8.6 0.4 collective-permute-start.6
  9.0 0.7 %collective-permute-done.3 = f32[512,128]{1,0:T(8,128)S(1)} collective-permute-done((f32[512,128]{1,0:T(8,128)S(1)}, f32[512,128]{1,0:T(8,128)S(1)}, u32[]{:S(2)}, u32[]{:S(2)}) %collective-permute-start.3) | collective-permute-done | bytes 262176 | tf_op jit(solution)/shard_map/ppermute | solution.py:52
  9.7 1.1 %collective-permute-start.4 = (f32[512,128]{1,0:T(8,128)S(1)}, f32[512,128]{1,0:T(8,128)S(1)}, u32[]{:S(2)}, u32[]{:S(2)}) collective-permute-start(f32[512,128]{1,0:T(8,128)S(1)} %add.33), channel_id=1, source_target_pairs={{0,192},{8,136},{16,208},{24,152},{32,224},{40,168},{48,240},{56,1... | collective-permute-start | bytes 786440 | tf_op jit(solution)/shard_map/ppermute | solution.py:52
  10.8 0.4 collective-permute-start
  11.2 0.0 collective-permute-done.1
  11.2 1.7 %collective-permute-start.2 = (f32[512,128]{1,0:T(8,128)S(1)}, f32[512,128]{1,0:T(8,128)S(1)}, u32[]{:S(2)}, u32[]{:S(2)}) collective-permute-start(f32[512,128]{1,0:T(8,128)S(1)} %add.31), channel_id=1, source_target_pairs={{0,192},{8,136},{16,208},{24,152},{32,224},{40,168},{48,240},{56,1... | collective-permute-start | bytes 786440 | tf_op jit(solution)/shard_map/ppermute | solution.py:52
  12.9 0.0 collective-permute-done.6
  12.9 1.0 %collective-permute-start.7 = (f32[512,128]{1,0:T(8,128)S(1)}, f32[512,128]{1,0:T(8,128)S(1)}, u32[]{:S(2)}, u32[]{:S(2)}) collective-permute-start(f32[512,128]{1,0:T(8,128)S(1)} %add.35), channel_id=1, source_target_pairs={{0,64},{8,72},{16,80},{24,88},{32,96},{40,104},{48,112},{56,120},{... | collective-permute-start | bytes 786440 | tf_op jit(solution)/shard_map/ppermute | solution.py:52
  14.0 2.7 %collective-permute-done.4 = f32[512,128]{1,0:T(8,128)S(1)} collective-permute-done((f32[512,128]{1,0:T(8,128)S(1)}, f32[512,128]{1,0:T(8,128)S(1)}, u32[]{:S(2)}, u32[]{:S(2)}) %collective-permute-start.4) | collective-permute-done | bytes 262176 | tf_op jit(solution)/shard_map/ppermute | solution.py:52
  16.6 6.2 %collective-permute-start.5 = (f32[512,128]{1,0:T(8,128)S(1)}, f32[512,128]{1,0:T(8,128)S(1)}, u32[]{:S(2)}, u32[]{:S(2)}) collective-permute-start(f32[512,128]{1,0:T(8,128)S(1)} %collective-permute-done.4), channel_id=1, source_target_pairs={{0,8},{8,0},{16,24},{24,16},{32,40},{40,32},{48,56},{56,48},{64,72... | collective-permute-start | bytes 786440 | tf_op jit(solution)/shard_map/ppermute | solution.py:52
  22.8 0.0 collective-permute-done
  22.8 0.0 collective-permute-done.2
  22.9 0.8 %collective-permute-done.7 = f32[512,128]{1,0:T(8,128)S(1)} collective-permute-done((f32[512,128]{1,0:T(8,128)S(1)}, f32[512,128]{1,0:T(8,128)S(1)}, u32[]{:S(2)}, u32[]{:S(2)}) %collective-permute-start.7) | collective-permute-done | bytes 262176 | tf_op jit(solution)/shard_map/ppermute | solution.py:52
  23.7 0.4 collective-permute-done.5
  24.0 0.1 add_add_fusion.1
  24.1 2.5 %collective-permute-start.10 = (f32[512,128]{1,0:T(8,128)S(1)}, f32[512,128]{1,0:T(8,128)S(1)}, u32[]{:S(2)}, u32[]{:S(2)}) collective-permute-start(f32[512,128]{1,0:T(8,128)S(1)} %add_add_fusion.1), channel_id=1, source_target_pairs={{0,32},{8,40},{16,48},{24,56},{32,0},{40,8},{48,16},{56,24},{64,96... | collective-permute-start | bytes 786440 | tf_op jit(solution)/shard_map/ppermute | solution.py:52
  26.6 0.4 collective-permute-start.9
  27.0 0.4 collective-permute-start.8
  27.4 4.5 %collective-permute-done.10 = f32[512,128]{1,0:T(8,128)S(1)} collective-permute-done((f32[512,128]{1,0:T(8,128)S(1)}, f32[512,128]{1,0:T(8,128)S(1)}, u32[]{:S(2)}, u32[]{:S(2)}) %collective-permute-start.10) | collective-permute-done | bytes 262176 | tf_op jit(solution)/shard_map/ppermute | solution.py:52
  31.9 6.7 %collective-permute-done.9 = f32[512,128]{1,0:T(8,128)S(1)} collective-permute-done((f32[512,128]{1,0:T(8,128)S(1)}, f32[512,128]{1,0:T(8,128)S(1)}, u32[]{:S(2)}, u32[]{:S(2)}) %collective-permute-start.9) | collective-permute-done | bytes 262176 | tf_op jit(solution)/shard_map/ppermute | solution.py:52
  38.7 0.7 %collective-permute-done.8 = f32[512,128]{1,0:T(8,128)S(1)} collective-permute-done((f32[512,128]{1,0:T(8,128)S(1)}, f32[512,128]{1,0:T(8,128)S(1)}, u32[]{:S(2)}, u32[]{:S(2)}) %collective-permute-start.8) | collective-permute-done | bytes 262176 | tf_op jit(solution)/shard_map/ppermute | solution.py:52
  39.4 0.7 %collective-permute-start.11 = (f32[512,128]{1,0:T(8,128)S(1)}, f32[512,128]{1,0:T(8,128)S(1)}, u32[]{:S(2)}, u32[]{:S(2)}) collective-permute-start(f32[512,128]{1,0:T(8,128)S(1)} %add_add_fusion.refs_3_), channel_id=1, source_target_pairs={{0,8},{8,0},{16,24},{24,16},{32,40},{40,32},{48,56},{56,48},{64,72... | collective-permute-start | bytes 786440 | tf_op jit(solution)/shard_map/ppermute | solution.py:52
  40.1 0.9 %collective-permute-start.14 = (f32[512,128]{1,0:T(8,128)S(1)}, f32[512,128]{1,0:T(8,128)S(1)}, u32[]{:S(2)}, u32[]{:S(2)}) collective-permute-start(f32[512,128]{1,0:T(8,128)S(1)} %add_add_fusion.refs_3_), channel_id=1, source_target_pairs={{0,64},{8,72},{16,80},{24,88},{32,96},{40,104},{48,112},{56,120},{... | collective-permute-start | bytes 786440 | tf_op jit(solution)/shard_map/ppermute | solution.py:52
  41.1 1.9 %collective-permute-start.13 = (f32[512,128]{1,0:T(8,128)S(1)}, f32[512,128]{1,0:T(8,128)S(1)}, u32[]{:S(2)}, u32[]{:S(2)}) collective-permute-start(f32[512,128]{1,0:T(8,128)S(1)} %add_add_fusion.refs_3_), channel_id=1, source_target_pairs={{0,192},{8,136},{16,208},{24,152},{32,224},{40,168},{48,240},{56,1... | collective-permute-start | bytes 786440 | tf_op jit(solution)/shard_map/ppermute | solution.py:52
  42.9 0.0 collective-permute-done.11.refs_7_
  42.9 1.1 %collective-permute-start.12 = (f32[512,128]{1,0:T(8,128)S(1)}, f32[512,128]{1,0:T(8,128)S(1)}, u32[]{:S(2)}, u32[]{:S(2)}) collective-permute-start(f32[512,128]{1,0:T(8,128)S(1)} %collective-permute-done.11.refs_7_), channel_id=1, source_target_pairs={{0,192},{8,136},{16,208},{24,152},{32,224},{40,168},{48,240},{56,1... | collective-permute-start | bytes 786440 | tf_op jit(solution)/shard_map/ppermute | solution.py:52
  44.0 4.0 %collective-permute-done.14.refs_2_ = f32[512,128]{1,0:T(8,128)S(1)} collective-permute-done((f32[512,128]{1,0:T(8,128)S(1)}, f32[512,128]{1,0:T(8,128)S(1)}, u32[]{:S(2)}, u32[]{:S(2)}) %collective-permute-start.14) | collective-permute-done | bytes 262176 | tf_op jit(solution)/shard_map/ppermute | solution.py:52
  48.0 1.3 %collective-permute-start.17 = (f32[512,128]{1,0:T(8,128)S(1)}, f32[512,128]{1,0:T(8,128)S(1)}, u32[]{:S(2)}, u32[]{:S(2)}) collective-permute-start(f32[512,128]{1,0:T(8,128)S(1)} %collective-permute-done.14.refs_2_), channel_id=1, source_target_pairs={{0,8},{8,0},{16,24},{24,16},{32,40},{40,32},{48,56},{56,48},{64,72... | collective-permute-start | bytes 786440 | tf_op jit(solution)/shard_map/ppermute | solution.py:52
  49.4 3.0 %collective-permute-done.13.refs_1_ = f32[512,128]{1,0:T(8,128)S(1)} collective-permute-done((f32[512,128]{1,0:T(8,128)S(1)}, f32[512,128]{1,0:T(8,128)S(1)}, u32[]{:S(2)}, u32[]{:S(2)}) %collective-permute-start.13) | collective-permute-done | bytes 262176 | tf_op jit(solution)/shard_map/ppermute | solution.py:52
  52.4 0.0 collective-permute-start.16
  52.4 2.8 %collective-permute-done.12.refs_0_ = f32[512,128]{1,0:T(8,128)S(1)} collective-permute-done((f32[512,128]{1,0:T(8,128)S(1)}, f32[512,128]{1,0:T(8,128)S(1)}, u32[]{:S(2)}, u32[]{:S(2)}) %collective-permute-start.12) | collective-permute-done | bytes 262176 | tf_op jit(solution)/shard_map/ppermute | solution.py:52
  55.2 2.2 %collective-permute-start.15 = (f32[512,128]{1,0:T(8,128)S(1)}, f32[512,128]{1,0:T(8,128)S(1)}, u32[]{:S(2)}, u32[]{:S(2)}) collective-permute-start(f32[512,128]{1,0:T(8,128)S(1)} %collective-permute-done.12.refs_0_), channel_id=1, source_target_pairs={{0,8},{8,0},{16,24},{24,16},{32,40},{40,32},{48,56},{56,48},{64,72... | collective-permute-start | bytes 786440 | tf_op jit(solution)/shard_map/ppermute | solution.py:52
  57.4 0.0 copy-done
  57.4 0.0 collective-permute-done.17.refs_6_
  57.4 0.0 collective-permute-done.16.refs_5_
  57.5 1.1 %collective-permute-done.15.refs_4_ = f32[512,128]{1,0:T(8,128)S(1)} collective-permute-done((f32[512,128]{1,0:T(8,128)S(1)}, f32[512,128]{1,0:T(8,128)S(1)}, u32[]{:S(2)}, u32[]{:S(2)}) %collective-permute-start.15) | collective-permute-done | bytes 262176 | tf_op jit(solution)/shard_map/ppermute | solution.py:52
  58.6 4.1 %shard_map.38 = f32[8192,128]{1,0:T(8,128)} custom-call(s32[3]{0:T(128)S(1)} %pad_add_fusion.where_ref, s32[16,128]{1,0:T(8,128)S(1)} %subtract_multiply_fusion.rows_vmem, f32[512,128]{1,0:T(8,128)S(1)} %collective-permute-done.12.refs_0_, f32[512,128]{1,0:T(8,128)S(1)} %collective-permute-done.13.refs_1_, f32[512,128]{1,0:T(8,128)S(1)} %collective-permute-done.14.refs_2_, ...), custom_call_target="tpu_custom_call" | custom-call | tf_op jit(solution)/shard_map/pallas_call | solution.py:184
  (5 shorter events, 0.1 us)
Async XLA Ops:
  0.1 57.4 %copy-start = (s32[16,128]{1,0:T(8,128)S(1)}, s32[16,128]{1,0:T(8,128)}, u32[]{:S(2)}) copy-start(s32[16,128]{1,0:T(8,128)} %ids_hbm.1) | copy-start | bytes 24580
  5.2 4.5 %collective-permute-start.3 = (f32[512,128]{1,0:T(8,128)S(1)}, f32[512,128]{1,0:T(8,128)S(1)}, u32[]{:S(2)}, u32[]{:S(2)}) collective-permute-start(f32[512,128]{1,0:T(8,128)S(1)} %get-tuple-element.18), channel_id=1, source_target_pairs={{0,8},{8,0},{16,24},{24,16},{32,40},{40,32},{48,56},{56,48},{64,72... | collective-permute-start | bytes 786440 | tf_op jit(solution)/shard_map/ppermute | solution.py:52
  8.5 2.7 %collective-permute-start.1 = (f32[512,128]{1,0:T(8,128)S(1)}, f32[512,128]{1,0:T(8,128)S(1)}, u32[]{:S(2)}, u32[]{:S(2)}) collective-permute-start(f32[512,128]{1,0:T(8,128)S(1)} %get-tuple-element.16), channel_id=1, source_target_pairs={{0,8},{8,0},{16,24},{24,16},{32,40},{40,32},{48,56},{56,48},{64,72... | collective-permute-start | bytes 786440 | tf_op jit(solution)/shard_map/ppermute | solution.py:52
  8.6 4.3 %collective-permute-start.6 = (f32[512,128]{1,0:T(8,128)S(1)}, f32[512,128]{1,0:T(8,128)S(1)}, u32[]{:S(2)}, u32[]{:S(2)}) collective-permute-start(f32[512,128]{1,0:T(8,128)S(1)} %get-tuple-element.20), channel_id=1, source_target_pairs={{0,8},{8,0},{16,24},{24,16},{32,40},{40,32},{48,56},{56,48},{64,72... | collective-permute-start | bytes 786440 | tf_op jit(solution)/shard_map/ppermute | solution.py:52
  9.7 6.9 %collective-permute-start.4 = (f32[512,128]{1,0:T(8,128)S(1)}, f32[512,128]{1,0:T(8,128)S(1)}, u32[]{:S(2)}, u32[]{:S(2)}) collective-permute-start(f32[512,128]{1,0:T(8,128)S(1)} %add.33), channel_id=1, source_target_pairs={{0,192},{8,136},{16,208},{24,152},{32,224},{40,168},{48,240},{56,1... | collective-permute-start | bytes 786440 | tf_op jit(solution)/shard_map/ppermute | solution.py:52
  10.8 12.0 %collective-permute-start = (f32[512,128]{1,0:T(8,128)S(1)}, f32[512,128]{1,0:T(8,128)S(1)}, u32[]{:S(2)}, u32[]{:S(2)}) collective-permute-start(f32[512,128]{1,0:T(8,128)S(1)} %get-tuple-element.14), channel_id=1, source_target_pairs={{0,8},{8,0},{16,24},{24,16},{32,40},{40,32},{48,56},{56,48},{64,72... | collective-permute-start | bytes 786440 | tf_op jit(solution)/shard_map/ppermute | solution.py:52
  11.2 11.6 %collective-permute-start.2 = (f32[512,128]{1,0:T(8,128)S(1)}, f32[512,128]{1,0:T(8,128)S(1)}, u32[]{:S(2)}, u32[]{:S(2)}) collective-permute-start(f32[512,128]{1,0:T(8,128)S(1)} %add.31), channel_id=1, source_target_pairs={{0,192},{8,136},{16,208},{24,152},{32,224},{40,168},{48,240},{56,1... | collective-permute-start | bytes 786440 | tf_op jit(solution)/shard_map/ppermute | solution.py:52
  12.9 10.7 %collective-permute-start.7 = (f32[512,128]{1,0:T(8,128)S(1)}, f32[512,128]{1,0:T(8,128)S(1)}, u32[]{:S(2)}, u32[]{:S(2)}) collective-permute-start(f32[512,128]{1,0:T(8,128)S(1)} %add.35), channel_id=1, source_target_pairs={{0,64},{8,72},{16,80},{24,88},{32,96},{40,104},{48,112},{56,120},{... | collective-permute-start | bytes 786440 | tf_op jit(solution)/shard_map/ppermute | solution.py:52
  16.6 7.4 %collective-permute-start.5 = (f32[512,128]{1,0:T(8,128)S(1)}, f32[512,128]{1,0:T(8,128)S(1)}, u32[]{:S(2)}, u32[]{:S(2)}) collective-permute-start(f32[512,128]{1,0:T(8,128)S(1)} %collective-permute-done.4), channel_id=1, source_target_pairs={{0,8},{8,0},{16,24},{24,16},{32,40},{40,32},{48,56},{56,48},{64,72... | collective-permute-start | bytes 786440 | tf_op jit(solution)/shard_map/ppermute | solution.py:52
  24.1 7.8 %collective-permute-start.10 = (f32[512,128]{1,0:T(8,128)S(1)}, f32[512,128]{1,0:T(8,128)S(1)}, u32[]{:S(2)}, u32[]{:S(2)}) collective-permute-start(f32[512,128]{1,0:T(8,128)S(1)} %add_add_fusion.1), channel_id=1, source_target_pairs={{0,32},{8,40},{16,48},{24,56},{32,0},{40,8},{48,16},{56,24},{64,96... | collective-permute-start | bytes 786440 | tf_op jit(solution)/shard_map/ppermute | solution.py:52
  26.6 12.1 %collective-permute-start.9 = (f32[512,128]{1,0:T(8,128)S(1)}, f32[512,128]{1,0:T(8,128)S(1)}, u32[]{:S(2)}, u32[]{:S(2)}) collective-permute-start(f32[512,128]{1,0:T(8,128)S(1)} %add_add_fusion.1), channel_id=1, source_target_pairs={{0,16},{8,24},{16,0},{24,8},{32,48},{40,56},{48,32},{56,40},{64,80... | collective-permute-start | bytes 786440 | tf_op jit(solution)/shard_map/ppermute | solution.py:52
  27.0 12.4 %collective-permute-start.8 = (f32[512,128]{1,0:T(8,128)S(1)}, f32[512,128]{1,0:T(8,128)S(1)}, u32[]{:S(2)}, u32[]{:S(2)}) collective-permute-start(f32[512,128]{1,0:T(8,128)S(1)} %add_add_fusion.1), channel_id=1, source_target_pairs={{0,48},{8,56},{16,32},{24,40},{32,16},{40,24},{48,0},{56,8},{64,11... | collective-permute-start | bytes 786440 | tf_op jit(solution)/shard_map/ppermute | solution.py:52
  39.4 3.5 %collective-permute-start.11 = (f32[512,128]{1,0:T(8,128)S(1)}, f32[512,128]{1,0:T(8,128)S(1)}, u32[]{:S(2)}, u32[]{:S(2)}) collective-permute-start(f32[512,128]{1,0:T(8,128)S(1)} %add_add_fusion.refs_3_), channel_id=1, source_target_pairs={{0,8},{8,0},{16,24},{24,16},{32,40},{40,32},{48,56},{56,48},{64,72... | collective-permute-start | bytes 786440 | tf_op jit(solution)/shard_map/ppermute | solution.py:52
  40.1 7.9 %collective-permute-start.14 = (f32[512,128]{1,0:T(8,128)S(1)}, f32[512,128]{1,0:T(8,128)S(1)}, u32[]{:S(2)}, u32[]{:S(2)}) collective-permute-start(f32[512,128]{1,0:T(8,128)S(1)} %add_add_fusion.refs_3_), channel_id=1, source_target_pairs={{0,64},{8,72},{16,80},{24,88},{32,96},{40,104},{48,112},{56,120},{... | collective-permute-start | bytes 786440 | tf_op jit(solution)/shard_map/ppermute | solution.py:52
  41.1 11.3 %collective-permute-start.13 = (f32[512,128]{1,0:T(8,128)S(1)}, f32[512,128]{1,0:T(8,128)S(1)}, u32[]{:S(2)}, u32[]{:S(2)}) collective-permute-start(f32[512,128]{1,0:T(8,128)S(1)} %add_add_fusion.refs_3_), channel_id=1, source_target_pairs={{0,192},{8,136},{16,208},{24,152},{32,224},{40,168},{48,240},{56,1... | collective-permute-start | bytes 786440 | tf_op jit(solution)/shard_map/ppermute | solution.py:52
  42.9 12.3 %collective-permute-start.12 = (f32[512,128]{1,0:T(8,128)S(1)}, f32[512,128]{1,0:T(8,128)S(1)}, u32[]{:S(2)}, u32[]{:S(2)}) collective-permute-start(f32[512,128]{1,0:T(8,128)S(1)} %collective-permute-done.11.refs_7_), channel_id=1, source_target_pairs={{0,192},{8,136},{16,208},{24,152},{32,224},{40,168},{48,240},{56,1... | collective-permute-start | bytes 786440 | tf_op jit(solution)/shard_map/ppermute | solution.py:52
  48.0 9.4 %collective-permute-start.17 = (f32[512,128]{1,0:T(8,128)S(1)}, f32[512,128]{1,0:T(8,128)S(1)}, u32[]{:S(2)}, u32[]{:S(2)}) collective-permute-start(f32[512,128]{1,0:T(8,128)S(1)} %collective-permute-done.14.refs_2_), channel_id=1, source_target_pairs={{0,8},{8,0},{16,24},{24,16},{32,40},{40,32},{48,56},{56,48},{64,72... | collective-permute-start | bytes 786440 | tf_op jit(solution)/shard_map/ppermute | solution.py:52
  52.4 5.0 %collective-permute-start.16 = (f32[512,128]{1,0:T(8,128)S(1)}, f32[512,128]{1,0:T(8,128)S(1)}, u32[]{:S(2)}, u32[]{:S(2)}) collective-permute-start(f32[512,128]{1,0:T(8,128)S(1)} %collective-permute-done.13.refs_1_), channel_id=1, source_target_pairs={{0,8},{8,0},{16,24},{24,16},{32,40},{40,32},{48,56},{56,48},{64,72... | collective-permute-start | bytes 786440 | tf_op jit(solution)/shard_map/ppermute | solution.py:52
  55.2 3.4 %collective-permute-start.15 = (f32[512,128]{1,0:T(8,128)S(1)}, f32[512,128]{1,0:T(8,128)S(1)}, u32[]{:S(2)}, u32[]{:S(2)}) collective-permute-start(f32[512,128]{1,0:T(8,128)S(1)} %collective-permute-done.12.refs_0_), channel_id=1, source_target_pairs={{0,8},{8,0},{16,24},{24,16},{32,40},{40,32},{48,56},{56,48},{64,72... | collective-permute-start | bytes 786440 | tf_op jit(solution)/shard_map/ppermute | solution.py:52

commit v4 on v3

--- a/solution.py
+++ b/solution.py
@@ -33,18 +33,16 @@
     ]
 
 
-def far(line):
-    if line == "x":
-        return pairs(lambda x, y, c: (x ^ (3 - c), y, c))
-    return pairs(lambda x, y, c: (x, y ^ (3 - c), c))
-
-
-def along_y(step):
-    return pairs(lambda x, y, c: (x, y ^ step, c))
-
-
-NEAR_X = pairs(lambda x, y, c: (x ^ 1, y, c))
-FAR_X = far("x")
+def along(axis_of, step_of):
+    return pairs(
+        lambda x, y, c: (x, y ^ step_of(c), c) if axis_of(c) else (x ^ step_of(c), y, c)
+    )
+
+
+CROSSING = along(lambda c: 1 - c, lambda c: 3 - c)
+STRAIGHT = along(lambda c: c, lambda c: 3 - c)
+NEAR = along(lambda c: c, lambda c: 1)
+ACROSS = [along(lambda c: 1 - c, lambda c, step=step: step) for step in (3, 1, 2)]
 OTHER_CORE = pairs(lambda x, y, c: (x, y, 1 - c))
 
 
@@ -71,11 +69,12 @@
 
 
 def piece_rows(where_ref):
-    x, core = where_ref[1], where_ref[2]
+    core = where_ref[3]
     rows = []
     for c in (core, 1 - core):
         for half, step in ((1 - c, 3 - c), (c, 3 - c), (c, 1), (c, 0)):
-            rows.append(pl.ds(pl.multiple_of(half * HALF + (x ^ step) * PIECE, PIECE), PIECE))
+            place = half * HALF + (where_ref[1 + half] ^ step) * PIECE
+            rows.append(pl.ds(pl.multiple_of(place, PIECE), PIECE))
     return rows
 
 
@@ -144,7 +143,7 @@
 def local(surplus, block_ids, coef):
     index = lax.axis_index("grp")
     base = lax.axis_index("dom") * NBD
-    where = jnp.stack([base, index >> 3, index & 1]).astype(jnp.int32)
+    where = jnp.stack([base, index >> 3, (index >> 1) & 3, index & 1]).astype(jnp.int32)
     smem = pl.BlockSpec(memory_space=pltpu.SMEM)
     vmem = pl.BlockSpec(memory_space=VMEM)
     hbm = pl.BlockSpec(memory_space=pltpu.HBM)
@@ -169,16 +168,16 @@
     )(where, *(pltpu.with_memory_space_constraint(v, pltpu.HBM) for v in (coef, block_ids, to_tiles(surplus))))
     swap = lambda value: send(value, OTHER_CORE)
     crossing, straight, near, own = [mine + swap(theirs) for mine, theirs in zip(parts[:4], parts[4:])]
-    crossing = send(crossing, FAR_X)
-    straight = send(straight, FAR_X)
-    near = send(near, NEAR_X)
+    crossing = send(crossing, CROSSING)
+    straight = send(straight, STRAIGHT)
+    near = send(near, NEAR)
     share = own + straight + swap(crossing) + near
-    got = [send(share, along_y(k)) for k in (3, 1, 2)]
+    got = [send(share, partner) for partner in ACROSS]
     own = share + got[0] + got[1] + got[2]
-    straight = send(own, FAR_X)
+    straight = send(own, STRAIGHT)
     other = swap(own)
-    crossing = send(other, FAR_X)
-    near = send(own, NEAR_X)
+    crossing = send(other, CROSSING)
+    near = send(own, NEAR)
     mine = [swap(crossing), swap(straight), swap(near), other]
     rows = (block_ids - base) * SUB
     out = pl.pallas_call(

time: 62.7 us -> 50.7 us (0.81)
  waiting for transfers between devices: 27.4 us -> 14.8 us
    ppermute x18, waiting for transfers between devices: 27.4 us -> 14.8 us  [send(): return lax.ppermute(value, 'grp', partner)]
  transfers between devices with their start and end apart: 18 -> 18, of which waited for: 11 -> 10; matrix products, arithmetic and copies ran while one was open for 0% -> 0% of each run, Pallas kernels for 0% -> 0%
where the time goes in v4:
time: 50.7 us; the launch traced here: 50.6 us
  starting transfers between devices  26.3 us (52%)
  waiting for transfers between devices  14.8 us (29%)
  Pallas kernels  9.21 us (18%)
    ppermute x18, starting transfers between devices, send(): return lax.ppermute(value, 'grp', partner)  26.3 us
    ppermute x18, waiting for transfers between devices, send(): return lax.ppermute(value, 'grp', partner)  14.8 us
    pallas_call x1, Pallas kernels, local(): pl.pallas_call(scatter, out_shape=(piece,) * 8, in_specs=[smem, hbm, hbm,...  5.12 us
    pallas_call x1, Pallas kernels, local(): pl.pallas_call(gather, out_shape=jax.ShapeDtypeStruct((GRIDS * GRID_ROWS,...  4.09 us
  transfers between devices with their start and end apart: 18, of which 10 were waited for; matrix products, arithmetic and copies ran while one was open for 0% of the time, Pallas kernels for 0%

profile of v4, /device:TPU:1, one launch (start us, length us, event | category | flops | bytes accessed | tf_op | source)
XLA Modules:
  0.0 50.6 jit_solution(12611038153422839053)
XLA Ops:
  0.0 0.1 pad_add_fusion.where_ref
  0.1 0.0 copy-start
  0.1 5.1 %shard_map.37 = (f32[512,128]{1,0:T(8,128)S(1)}, f32[512,128]{1,0:T(8,128)S(1)}, f32[512,128]{1,0:T(8,128)S(1)}, f32[512,128]{1,0:T(8,128)S(1)}, f32[512,128]{1,...) custom-call(s32[4]{0:T(128)S(1)} %pad_add_fusion.where_ref, s32[16]{0:T(128)} %coef_hbm.1, ...), custom_call_target="tpu_custom_call" | custom-call | tf_op jit(solution)/shard_map/pallas_call | solution.py:154
  5.2 3.3 %collective-permute-start.3 = (f32[512,128]{1,0:T(8,128)S(1)}, f32[512,128]{1,0:T(8,128)S(1)}, u32[]{:S(2)}, u32[]{:S(2)}) collective-permute-start(f32[512,128]{1,0:T(8,128)S(1)} %get-tuple-element.18), channel_id=1, source_target_pairs={{0,8},{8,0},{16,24},{24,16},{32,40},{40,32},{48,56},{56,48},{64,72... | collective-permute-start | bytes 786440 | tf_op jit(solution)/shard_map/ppermute | solution.py:50
  8.5 0.1 collective-permute-start.1
  8.6 0.4 collective-permute-start.6
  9.0 0.7 %collective-permute-done.3 = f32[512,128]{1,0:T(8,128)S(1)} collective-permute-done((f32[512,128]{1,0:T(8,128)S(1)}, f32[512,128]{1,0:T(8,128)S(1)}, u32[]{:S(2)}, u32[]{:S(2)}) %collective-permute-start.3) | collective-permute-done | bytes 262176 | tf_op jit(solution)/shard_map/ppermute | solution.py:50
  9.7 1.1 %collective-permute-start.4 = (f32[512,128]{1,0:T(8,128)S(1)}, f32[512,128]{1,0:T(8,128)S(1)}, u32[]{:S(2)}, u32[]{:S(2)}) collective-permute-start(f32[512,128]{1,0:T(8,128)S(1)} %add.33), channel_id=1, source_target_pairs={{0,48},{8,136},{16,32},{24,152},{32,16},{40,168},{48,0},{56,184},{... | collective-permute-start | bytes 786440 | tf_op jit(solution)/shard_map/ppermute | solution.py:50
  10.8 0.6 %collective-permute-start = (f32[512,128]{1,0:T(8,128)S(1)}, f32[512,128]{1,0:T(8,128)S(1)}, u32[]{:S(2)}, u32[]{:S(2)}) collective-permute-start(f32[512,128]{1,0:T(8,128)S(1)} %get-tuple-element.14), channel_id=1, source_target_pairs={{0,8},{8,0},{16,24},{24,16},{32,40},{40,32},{48,56},{56,48},{64,72... | collective-permute-start | bytes 786440 | tf_op jit(solution)/shard_map/ppermute | solution.py:50
  11.5 0.0 collective-permute-done.1
  11.5 2.4 %collective-permute-start.2 = (f32[512,128]{1,0:T(8,128)S(1)}, f32[512,128]{1,0:T(8,128)S(1)}, u32[]{:S(2)}, u32[]{:S(2)}) collective-permute-start(f32[512,128]{1,0:T(8,128)S(1)} %add.31), channel_id=1, source_target_pairs={{0,192},{8,40},{16,208},{24,56},{32,224},{40,8},{48,240},{56,24},{... | collective-permute-start | bytes 786440 | tf_op jit(solution)/shard_map/ppermute | solution.py:50
  13.9 0.0 collective-permute-done.6
  13.9 0.5 collective-permute-start.7
  14.4 2.3 %collective-permute-done.4 = f32[512,128]{1,0:T(8,128)S(1)} collective-permute-done((f32[512,128]{1,0:T(8,128)S(1)}, f32[512,128]{1,0:T(8,128)S(1)}, u32[]{:S(2)}, u32[]{:S(2)}) %collective-permute-start.4) | collective-permute-done | bytes 262176 | tf_op jit(solution)/shard_map/ppermute | solution.py:50
  16.6 3.9 %collective-permute-start.5 = (f32[512,128]{1,0:T(8,128)S(1)}, f32[512,128]{1,0:T(8,128)S(1)}, u32[]{:S(2)}, u32[]{:S(2)}) collective-permute-start(f32[512,128]{1,0:T(8,128)S(1)} %collective-permute-done.4), channel_id=1, source_target_pairs={{0,8},{8,0},{16,24},{24,16},{32,40},{40,32},{48,56},{56,48},{64,72... | collective-permute-start | bytes 786440 | tf_op jit(solution)/shard_map/ppermute | solution.py:50
  20.6 0.0 collective-permute-done
  20.6 0.0 collective-permute-done.2
  20.6 0.3 collective-permute-done.7
  20.9 0.9 %collective-permute-done.5 = f32[512,128]{1,0:T(8,128)S(1)} collective-permute-done((f32[512,128]{1,0:T(8,128)S(1)}, f32[512,128]{1,0:T(8,128)S(1)}, u32[]{:S(2)}, u32[]{:S(2)}) %collective-permute-start.5) | collective-permute-done | bytes 262176 | tf_op jit(solution)/shard_map/ppermute | solution.py:50
  21.7 0.1 add_add_fusion.1
  21.8 0.4 collective-permute-start.10
  22.2 0.3 collective-permute-start.9
  22.5 2.6 %collective-permute-start.8 = (f32[512,128]{1,0:T(8,128)S(1)}, f32[512,128]{1,0:T(8,128)S(1)}, u32[]{:S(2)}, u32[]{:S(2)}) collective-permute-start(f32[512,128]{1,0:T(8,128)S(1)} %add_add_fusion.1), channel_id=1, source_target_pairs={{0,48},{8,200},{16,32},{24,216},{32,16},{40,232},{48,0},{56,248},{... | collective-permute-start | bytes 786440 | tf_op jit(solution)/shard_map/ppermute | solution.py:50
  25.1 3.8 %collective-permute-done.10 = f32[512,128]{1,0:T(8,128)S(1)} collective-permute-done((f32[512,128]{1,0:T(8,128)S(1)}, f32[512,128]{1,0:T(8,128)S(1)}, u32[]{:S(2)}, u32[]{:S(2)}) %collective-permute-start.10) | collective-permute-done | bytes 262176 | tf_op jit(solution)/shard_map/ppermute | solution.py:50
  29.0 0.4 collective-permute-done.9
  29.4 2.3 %collective-permute-done.8 = f32[512,128]{1,0:T(8,128)S(1)} collective-permute-done((f32[512,128]{1,0:T(8,128)S(1)}, f32[512,128]{1,0:T(8,128)S(1)}, u32[]{:S(2)}, u32[]{:S(2)}) %collective-permute-start.8) | collective-permute-done | bytes 262176 | tf_op jit(solution)/shard_map/ppermute | solution.py:50
  31.8 1.3 %collective-permute-start.11 = (f32[512,128]{1,0:T(8,128)S(1)}, f32[512,128]{1,0:T(8,128)S(1)}, u32[]{:S(2)}, u32[]{:S(2)}) collective-permute-start(f32[512,128]{1,0:T(8,128)S(1)} %add_add_fusion.refs_3_), channel_id=1, source_target_pairs={{0,8},{8,0},{16,24},{24,16},{32,40},{40,32},{48,56},{56,48},{64,72... | collective-permute-start | bytes 786440 | tf_op jit(solution)/shard_map/ppermute | solution.py:50
  33.1 0.0 collective-permute-start.14
  33.1 2.2 %collective-permute-start.13 = (f32[512,128]{1,0:T(8,128)S(1)}, f32[512,128]{1,0:T(8,128)S(1)}, u32[]{:S(2)}, u32[]{:S(2)}) collective-permute-start(f32[512,128]{1,0:T(8,128)S(1)} %add_add_fusion.refs_3_), channel_id=1, source_target_pairs={{0,192},{8,40},{16,208},{24,56},{32,224},{40,8},{48,240},{56,24},{... | collective-permute-start | bytes 786440 | tf_op jit(solution)/shard_map/ppermute | solution.py:50
  35.3 0.0 collective-permute-done.11.refs_7_
  35.3 2.7 %collective-permute-start.12 = (f32[512,128]{1,0:T(8,128)S(1)}, f32[512,128]{1,0:T(8,128)S(1)}, u32[]{:S(2)}, u32[]{:S(2)}) collective-permute-start(f32[512,128]{1,0:T(8,128)S(1)} %collective-permute-done.11.refs_7_), channel_id=1, source_target_pairs={{0,48},{8,136},{16,32},{24,152},{32,16},{40,168},{48,0},{56,184},{... | collective-permute-start | bytes 786440 | tf_op jit(solution)/shard_map/ppermute | solution.py:50
  38.0 0.6 %collective-permute-done.14.refs_2_ = f32[512,128]{1,0:T(8,128)S(1)} collective-permute-done((f32[512,128]{1,0:T(8,128)S(1)}, f32[512,128]{1,0:T(8,128)S(1)}, u32[]{:S(2)}, u32[]{:S(2)}) %collective-permute-start.14) | collective-permute-done | bytes 262176 | tf_op jit(solution)/shard_map/ppermute | solution.py:50
  38.6 1.0 %collective-permute-start.17 = (f32[512,128]{1,0:T(8,128)S(1)}, f32[512,128]{1,0:T(8,128)S(1)}, u32[]{:S(2)}, u32[]{:S(2)}) collective-permute-start(f32[512,128]{1,0:T(8,128)S(1)} %collective-permute-done.14.refs_2_), channel_id=1, source_target_pairs={{0,8},{8,0},{16,24},{24,16},{32,40},{40,32},{48,56},{56,48},{64,72... | collective-permute-start | bytes 786440 | tf_op jit(solution)/shard_map/ppermute | solution.py:50
  39.6 2.4 %collective-permute-done.13.refs_1_ = f32[512,128]{1,0:T(8,128)S(1)} collective-permute-done((f32[512,128]{1,0:T(8,128)S(1)}, f32[512,128]{1,0:T(8,128)S(1)}, u32[]{:S(2)}, u32[]{:S(2)}) %collective-permute-start.13) | collective-permute-done | bytes 262176 | tf_op jit(solution)/shard_map/ppermute | solution.py:50
  41.9 2.2 %collective-permute-start.16 = (f32[512,128]{1,0:T(8,128)S(1)}, f32[512,128]{1,0:T(8,128)S(1)}, u32[]{:S(2)}, u32[]{:S(2)}) collective-permute-start(f32[512,128]{1,0:T(8,128)S(1)} %collective-permute-done.13.refs_1_), channel_id=1, source_target_pairs={{0,8},{8,0},{16,24},{24,16},{32,40},{40,32},{48,56},{56,48},{64,72... | collective-permute-start | bytes 786440 | tf_op jit(solution)/shard_map/ppermute | solution.py:50
  44.1 0.0 collective-permute-done.12.refs_0_
  44.1 1.2 %collective-permute-start.15 = (f32[512,128]{1,0:T(8,128)S(1)}, f32[512,128]{1,0:T(8,128)S(1)}, u32[]{:S(2)}, u32[]{:S(2)}) collective-permute-start(f32[512,128]{1,0:T(8,128)S(1)} %collective-permute-done.12.refs_0_), channel_id=1, source_target_pairs={{0,8},{8,0},{16,24},{24,16},{32,40},{40,32},{48,56},{56,48},{64,72... | collective-permute-start | bytes 786440 | tf_op jit(solution)/shard_map/ppermute | solution.py:50
  45.3 0.0 copy-done
  45.3 0.0 collective-permute-done.17.refs_6_
  45.3 0.0 collective-permute-done.16.refs_5_
  45.4 1.1 %collective-permute-done.15.refs_4_ = f32[512,128]{1,0:T(8,128)S(1)} collective-permute-done((f32[512,128]{1,0:T(8,128)S(1)}, f32[512,128]{1,0:T(8,128)S(1)}, u32[]{:S(2)}, u32[]{:S(2)}) %collective-permute-start.15) | collective-permute-done | bytes 262176 | tf_op jit(solution)/shard_map/ppermute | solution.py:50
  46.5 4.1 %shard_map.38 = f32[8192,128]{1,0:T(8,128)} custom-call(s32[4]{0:T(128)S(1)} %pad_add_fusion.where_ref, s32[16,128]{1,0:T(8,128)S(1)} %subtract_multiply_fusion.rows_vmem, f32[512,128]{1,0:T(8,128)S(1)} %collective-permute-done.12.refs_0_, f32[512,128]{1,0:T(8,128)S(1)} %collective-permute-done.13.refs_1_, f32[512,128]{1,0:T(8,128)S(1)} %collective-permute-done.14.refs_2_, ...), custom_call_target="tpu_custom_call" | custom-call | tf_op jit(solution)/shard_map/pallas_call | solution.py:183
  (5 shorter events, 0.1 us)
Async XLA Ops:
  0.1 45.3 %copy-start = (s32[16,128]{1,0:T(8,128)S(1)}, s32[16,128]{1,0:T(8,128)}, u32[]{:S(2)}) copy-start(s32[16,128]{1,0:T(8,128)} %ids_hbm.1) | copy-start | bytes 24580
  5.2 4.5 %collective-permute-start.3 = (f32[512,128]{1,0:T(8,128)S(1)}, f32[512,128]{1,0:T(8,128)S(1)}, u32[]{:S(2)}, u32[]{:S(2)}) collective-permute-start(f32[512,128]{1,0:T(8,128)S(1)} %get-tuple-element.18), channel_id=1, source_target_pairs={{0,8},{8,0},{16,24},{24,16},{32,40},{40,32},{48,56},{56,48},{64,72... | collective-permute-start | bytes 786440 | tf_op jit(solution)/shard_map/ppermute | solution.py:50
  8.5 2.9 %collective-permute-start.1 = (f32[512,128]{1,0:T(8,128)S(1)}, f32[512,128]{1,0:T(8,128)S(1)}, u32[]{:S(2)}, u32[]{:S(2)}) collective-permute-start(f32[512,128]{1,0:T(8,128)S(1)} %get-tuple-element.16), channel_id=1, source_target_pairs={{0,8},{8,0},{16,24},{24,16},{32,40},{40,32},{48,56},{56,48},{64,72... | collective-permute-start | bytes 786440 | tf_op jit(solution)/shard_map/ppermute | solution.py:50
  8.6 5.2 %collective-permute-start.6 = (f32[512,128]{1,0:T(8,128)S(1)}, f32[512,128]{1,0:T(8,128)S(1)}, u32[]{:S(2)}, u32[]{:S(2)}) collective-permute-start(f32[512,128]{1,0:T(8,128)S(1)} %get-tuple-element.20), channel_id=1, source_target_pairs={{0,8},{8,0},{16,24},{24,16},{32,40},{40,32},{48,56},{56,48},{64,72... | collective-permute-start | bytes 786440 | tf_op jit(solution)/shard_map/ppermute | solution.py:50
  9.7 6.9 %collective-permute-start.4 = (f32[512,128]{1,0:T(8,128)S(1)}, f32[512,128]{1,0:T(8,128)S(1)}, u32[]{:S(2)}, u32[]{:S(2)}) collective-permute-start(f32[512,128]{1,0:T(8,128)S(1)} %add.33), channel_id=1, source_target_pairs={{0,48},{8,136},{16,32},{24,152},{32,16},{40,168},{48,0},{56,184},{... | collective-permute-start | bytes 786440 | tf_op jit(solution)/shard_map/ppermute | solution.py:50
  10.8 9.8 %collective-permute-start = (f32[512,128]{1,0:T(8,128)S(1)}, f32[512,128]{1,0:T(8,128)S(1)}, u32[]{:S(2)}, u32[]{:S(2)}) collective-permute-start(f32[512,128]{1,0:T(8,128)S(1)} %get-tuple-element.14), channel_id=1, source_target_pairs={{0,8},{8,0},{16,24},{24,16},{32,40},{40,32},{48,56},{56,48},{64,72... | collective-permute-start | bytes 786440 | tf_op jit(solution)/shard_map/ppermute | solution.py:50
  11.5 9.1 %collective-permute-start.2 = (f32[512,128]{1,0:T(8,128)S(1)}, f32[512,128]{1,0:T(8,128)S(1)}, u32[]{:S(2)}, u32[]{:S(2)}) collective-permute-start(f32[512,128]{1,0:T(8,128)S(1)} %add.31), channel_id=1, source_target_pairs={{0,192},{8,40},{16,208},{24,56},{32,224},{40,8},{48,240},{56,24},{... | collective-permute-start | bytes 786440 | tf_op jit(solution)/shard_map/ppermute | solution.py:50
  13.9 7.0 %collective-permute-start.7 = (f32[512,128]{1,0:T(8,128)S(1)}, f32[512,128]{1,0:T(8,128)S(1)}, u32[]{:S(2)}, u32[]{:S(2)}) collective-permute-start(f32[512,128]{1,0:T(8,128)S(1)} %add.35), channel_id=1, source_target_pairs={{0,64},{8,24},{16,80},{24,8},{32,96},{40,56},{48,112},{56,40},{64,... | collective-permute-start | bytes 786440 | tf_op jit(solution)/shard_map/ppermute | solution.py:50
  16.6 5.1 %collective-permute-start.5 = (f32[512,128]{1,0:T(8,128)S(1)}, f32[512,128]{1,0:T(8,128)S(1)}, u32[]{:S(2)}, u32[]{:S(2)}) collective-permute-start(f32[512,128]{1,0:T(8,128)S(1)} %collective-permute-done.4), channel_id=1, source_target_pairs={{0,8},{8,0},{16,24},{24,16},{32,40},{40,32},{48,56},{56,48},{64,72... | collective-permute-start | bytes 786440 | tf_op jit(solution)/shard_map/ppermute | solution.py:50
  21.8 7.2 %collective-permute-start.10 = (f32[512,128]{1,0:T(8,128)S(1)}, f32[512,128]{1,0:T(8,128)S(1)}, u32[]{:S(2)}, u32[]{:S(2)}) collective-permute-start(f32[512,128]{1,0:T(8,128)S(1)} %add_add_fusion.1), channel_id=1, source_target_pairs={{0,32},{8,136},{16,48},{24,152},{32,0},{40,168},{48,16},{56,184},{... | collective-permute-start | bytes 786440 | tf_op jit(solution)/shard_map/ppermute | solution.py:50
  22.2 7.2 %collective-permute-start.9 = (f32[512,128]{1,0:T(8,128)S(1)}, f32[512,128]{1,0:T(8,128)S(1)}, u32[]{:S(2)}, u32[]{:S(2)}) collective-permute-start(f32[512,128]{1,0:T(8,128)S(1)} %add_add_fusion.1), channel_id=1, source_target_pairs={{0,16},{8,72},{16,0},{24,88},{32,48},{40,104},{48,32},{56,120},{64... | collective-permute-start | bytes 786440 | tf_op jit(solution)/shard_map/ppermute | solution.py:50
  22.5 9.2 %collective-permute-start.8 = (f32[512,128]{1,0:T(8,128)S(1)}, f32[512,128]{1,0:T(8,128)S(1)}, u32[]{:S(2)}, u32[]{:S(2)}) collective-permute-start(f32[512,128]{1,0:T(8,128)S(1)} %add_add_fusion.1), channel_id=1, source_target_pairs={{0,48},{8,200},{16,32},{24,216},{32,16},{40,232},{48,0},{56,248},{... | collective-permute-start | bytes 786440 | tf_op jit(solution)/shard_map/ppermute | solution.py:50
  31.8 3.5 %collective-permute-start.11 = (f32[512,128]{1,0:T(8,128)S(1)}, f32[512,128]{1,0:T(8,128)S(1)}, u32[]{:S(2)}, u32[]{:S(2)}) collective-permute-start(f32[512,128]{1,0:T(8,128)S(1)} %add_add_fusion.refs_3_), channel_id=1, source_target_pairs={{0,8},{8,0},{16,24},{24,16},{32,40},{40,32},{48,56},{56,48},{64,72... | collective-permute-start | bytes 786440 | tf_op jit(solution)/shard_map/ppermute | solution.py:50
  33.1 5.5 %collective-permute-start.14 = (f32[512,128]{1,0:T(8,128)S(1)}, f32[512,128]{1,0:T(8,128)S(1)}, u32[]{:S(2)}, u32[]{:S(2)}) collective-permute-start(f32[512,128]{1,0:T(8,128)S(1)} %add_add_fusion.refs_3_), channel_id=1, source_target_pairs={{0,64},{8,24},{16,80},{24,8},{32,96},{40,56},{48,112},{56,40},{64,... | collective-permute-start | bytes 786440 | tf_op jit(solution)/shard_map/ppermute | solution.py:50
  33.1 8.8 %collective-permute-start.13 = (f32[512,128]{1,0:T(8,128)S(1)}, f32[512,128]{1,0:T(8,128)S(1)}, u32[]{:S(2)}, u32[]{:S(2)}) collective-permute-start(f32[512,128]{1,0:T(8,128)S(1)} %add_add_fusion.refs_3_), channel_id=1, source_target_pairs={{0,192},{8,40},{16,208},{24,56},{32,224},{40,8},{48,240},{56,24},{... | collective-permute-start | bytes 786440 | tf_op jit(solution)/shard_map/ppermute | solution.py:50
  35.3 8.8 %collective-permute-start.12 = (f32[512,128]{1,0:T(8,128)S(1)}, f32[512,128]{1,0:T(8,128)S(1)}, u32[]{:S(2)}, u32[]{:S(2)}) collective-permute-start(f32[512,128]{1,0:T(8,128)S(1)} %collective-permute-done.11.refs_7_), channel_id=1, source_target_pairs={{0,48},{8,136},{16,32},{24,152},{32,16},{40,168},{48,0},{56,184},{... | collective-permute-start | bytes 786440 | tf_op jit(solution)/shard_map/ppermute | solution.py:50
  38.6 6.7 %collective-permute-start.17 = (f32[512,128]{1,0:T(8,128)S(1)}, f32[512,128]{1,0:T(8,128)S(1)}, u32[]{:S(2)}, u32[]{:S(2)}) collective-permute-start(f32[512,128]{1,0:T(8,128)S(1)} %collective-permute-done.14.refs_2_), channel_id=1, source_target_pairs={{0,8},{8,0},{16,24},{24,16},{32,40},{40,32},{48,56},{56,48},{64,72... | collective-permute-start | bytes 786440 | tf_op jit(solution)/shard_map/ppermute | solution.py:50
  41.9 3.4 %collective-permute-start.16 = (f32[512,128]{1,0:T(8,128)S(1)}, f32[512,128]{1,0:T(8,128)S(1)}, u32[]{:S(2)}, u32[]{:S(2)}) collective-permute-start(f32[512,128]{1,0:T(8,128)S(1)} %collective-permute-done.13.refs_1_), channel_id=1, source_target_pairs={{0,8},{8,0},{16,24},{24,16},{32,40},{40,32},{48,56},{56,48},{64,72... | collective-permute-start | bytes 786440 | tf_op jit(solution)/shard_map/ppermute | solution.py:50
  44.1 2.4 %collective-permute-start.15 = (f32[512,128]{1,0:T(8,128)S(1)}, f32[512,128]{1,0:T(8,128)S(1)}, u32[]{:S(2)}, u32[]{:S(2)}) collective-permute-start(f32[512,128]{1,0:T(8,128)S(1)} %collective-permute-done.12.refs_0_), channel_id=1, source_target_pairs={{0,8},{8,0},{16,24},{24,16},{32,40},{40,32},{48,56},{56,48},{64,72... | collective-permute-start | bytes 786440 | tf_op jit(solution)/shard_map/ppermute | solution.py:50

commit v5 on v2

--- a/solution.py
+++ b/solution.py
@@ -14,8 +14,10 @@
 GRID_ROWS = K * SUB
 HALF = NBD // 2 * SUB
 PIECE = HALF // 4
+ALL_BLOCKS = 8 * NBD
 BATCH = 16
 PAD = 64
+ORDER = (0, 3, 1, 2)
 VMEM = pltpu.VMEM
 VMEM_LIMIT = 48 * 1024 * 1024
 
@@ -66,9 +68,9 @@
     return pl.ds(pl.multiple_of(row, SUB), SUB)
 
 
-def piece_rows(where_ref, half, k):
+def piece_rows(where_ref, half, k, base=0):
     line = where_ref[1 + half]
-    return pl.ds(pl.multiple_of(half * HALF + (line ^ k) * PIECE, PIECE), PIECE)
+    return pl.ds(pl.multiple_of(base + half * HALF + (line ^ k) * PIECE, PIECE), PIECE)
 
 
 def scatter(where_ref, coef_hbm, ids_hbm, surplus_hbm, *refs):
@@ -84,8 +86,9 @@
     coef_copy.start()
     for g in range(GRIDS):
         load(g).start()
-    table[...] = jnp.zeros_like(table)
-    base = where_ref[0]
+    base = where_ref[0] * SUB
+    own_rows = pl.ds(pl.multiple_of(base, NBD * SUB), NBD * SUB)
+    table[own_rows, :] = jnp.zeros((NBD * SUB, LANES), jnp.float32)
     ids_copy.wait()
     coef_copy.wait()
 
@@ -95,7 +98,7 @@
         start = pl.multiple_of(g * GRID_ROWS, GRID_ROWS)
         for first in range(0, K, BATCH):
             slots = range(first, first + BATCH)
-            rows = [block_rows((ids[g, j] - base) * SUB) for j in slots]
+            rows = [block_rows(ids[g, j] * SUB) for j in slots]
             sums = [table[r, :] + stage[slot_rows(start, j), :] * factor for r, j in zip(rows, slots)]
             for r, total in zip(rows, sums):
                 table[r, :] = total
@@ -104,8 +107,8 @@
     lax.fori_loop(0, GRIDS, add_grid, 0)
     core = where_ref[3]
     for k in range(4):
-        pieces[k][...] = table[piece_rows(where_ref, 1 - core, k), :]
-        pieces[4 + k][...] = table[piece_rows(where_ref, core, k), :]
+        pieces[k][...] = table[piece_rows(where_ref, 1 - core, k, base), :]
+        pieces[4 + k][...] = table[piece_rows(where_ref, core, k, base), :]
 
 
 def gather(where_ref, rows_vmem, *refs):
@@ -113,9 +116,9 @@
     rows_copy = pltpu.make_async_copy(rows_vmem, rows_ref, rows_sem)
     rows_copy.start()
     core = where_ref[3]
-    for k in range(4):
-        table[piece_rows(where_ref, core, k), :] = pieces[k][...]
-        table[piece_rows(where_ref, 1 - core, k), :] = pieces[4 + k][...]
+    for i, k in enumerate(ORDER):
+        table[piece_rows(where_ref, core, k), :] = pieces[i][...]
+        table[piece_rows(where_ref, 1 - core, k), :] = pieces[4 + i][...]
     rows_copy.wait()
 
     def store(g):
@@ -154,7 +157,7 @@
         in_specs=[smem, hbm, hbm, hbm],
         out_specs=(vmem,) * 8,
         scratch_shapes=[
-            table,
+            VMEM((ALL_BLOCKS * SUB + PAD, LANES), jnp.float32),
             stage,
             pltpu.SMEM((GRIDS, K), jnp.int32),
             pltpu.SMEM((GRIDS,), jnp.int32),
@@ -168,8 +171,7 @@
     share = parts[0] + got[0] + got[1] + got[2]
     got = [send(share, other_line(k)) for k in (3, 1, 2)]
     share = share + got[0] + got[1] + got[2]
-    got = {k: send(share, own_line(k)) for k in (3, 1, 2)}
-    line = [share, got[1], got[2], got[3]]
+    line = [send(share, own_line(k)) if k else share for k in ORDER]
     across = [send(part, OTHER_CORE) for part in line]
     rows = (block_ids - base) * SUB
     out = pl.pallas_call(

time: 48.5 us -> 47.3 us (0.975)
  waiting for transfers between devices: 18 us -> 15.5 us
  starting transfers between devices: 20.9 us -> 22.8 us
  Pallas kernels: 9.2 us -> 8.61 us
    ppermute x17, waiting for transfers between devices: 18 us -> 15.5 us  [send(): return lax.ppermute(value, 'grp', partner)]
    ppermute x17, starting transfers between devices: 20.9 us -> 22.8 us  [send(): return lax.ppermute(value, 'grp', partner)]
    pallas_call x1, Pallas kernels: 5.12 us -> 4.53 us  [local(): pl.pallas_call(scatter, out_shape=(piece,) * 8, in_specs=[smem, hbm, hbm,...]
  transfers between devices with their start and end apart: 17 -> 17, of which waited for: 11 -> 10; matrix products, arithmetic and copies ran while one was open for 0% -> 0% of each run, Pallas kernels for 0% -> 0%
where the time goes in v5:
time: 47.3 us; the launch traced here: 47.2 us
  starting transfers between devices  22.8 us (48%)
  waiting for transfers between devices  15.5 us (33%)
  Pallas kernels  8.61 us (18%)
    ppermute x17, starting transfers between devices, send(): return lax.ppermute(value, 'grp', partner)  22.8 us
    ppermute x17, waiting for transfers between devices, send(): return lax.ppermute(value, 'grp', partner)  15.5 us
    pallas_call x1, Pallas kernels, local(): pl.pallas_call(scatter, out_shape=(piece,) * 8, in_specs=[smem, hbm, hbm,...  4.53 us
    pallas_call x1, Pallas kernels, local(): pl.pallas_call(gather, out_shape=jax.ShapeDtypeStruct((GRIDS * GRID_ROWS,...  4.08 us
  transfers between devices with their start and end apart: 17, of which 10 were waited for; matrix products, arithmetic and copies ran while one was open for 0% of the time, Pallas kernels for 0%

profile of v5, /device:TPU:1, one launch (start us, length us, event | category | flops | bytes accessed | tf_op | source)
XLA Modules:
  0.0 47.2 jit_solution(4216848511574127204)
XLA Ops:
  0.0 0.1 pad_add_fusion.where_ref
  0.1 0.0 copy-start
  0.1 4.5 %shard_map.37 = (f32[512,128]{1,0:T(8,128)S(1)}, f32[512,128]{1,0:T(8,128)S(1)}, f32[512,128]{1,0:T(8,128)S(1)}, f32[512,128]{1,0:T(8,128)S(1)}, f32[512,128]{1,...) custom-call(s32[4]{0:T(128)S(1)} %pad_add_fusion.where_ref, s32[16]{0:T(128)} %coef_hbm.1, ...), custom_call_target="tpu_custom_call" | custom-call | tf_op jit(solution)/shard_map/pallas_call | solution.py:154
  4.6 3.3 %collective-permute-start.1 = (f32[512,128]{1,0:T(8,128)S(1)}, f32[512,128]{1,0:T(8,128)S(1)}, u32[]{:S(2)}, u32[]{:S(2)}) collective-permute-start(f32[512,128]{1,0:T(8,128)S(1)} %get-tuple-element.16), channel_id=1, source_target_pairs={{0,8},{8,0},{16,24},{24,16},{32,40},{40,32},{48,56},{56,48},{64,72... | collective-permute-start | bytes 786440 | tf_op jit(solution)/shard_map/ppermute | solution.py:50
  7.9 0.1 collective-permute-start.3
  8.0 0.4 collective-permute-start.5
  8.5 0.1 collective-permute-start
  8.6 0.6 %collective-permute-done.1 = f32[512,128]{1,0:T(8,128)S(1)} collective-permute-done((f32[512,128]{1,0:T(8,128)S(1)}, f32[512,128]{1,0:T(8,128)S(1)}, u32[]{:S(2)}, u32[]{:S(2)}) %collective-permute-start.1) | collective-permute-done | bytes 262176 | tf_op jit(solution)/shard_map/ppermute | solution.py:50
  9.1 1.3 %collective-permute-start.2 = (f32[512,128]{1,0:T(8,128)S(1)}, f32[512,128]{1,0:T(8,128)S(1)}, u32[]{:S(2)}, u32[]{:S(2)}) collective-permute-start(f32[512,128]{1,0:T(8,128)S(1)} %add.31), channel_id=1, source_target_pairs={{0,128},{8,40},{16,144},{24,56},{32,160},{40,8},{48,176},{56,24},{... | collective-permute-start | bytes 786440 | tf_op jit(solution)/shard_map/ppermute | solution.py:50
  10.4 0.0 collective-permute-done.3
  10.4 0.5 %collective-permute-start.4 = (f32[512,128]{1,0:T(8,128)S(1)}, f32[512,128]{1,0:T(8,128)S(1)}, u32[]{:S(2)}, u32[]{:S(2)}) collective-permute-start(f32[512,128]{1,0:T(8,128)S(1)} %add.33), channel_id=1, source_target_pairs={{0,64},{8,24},{16,80},{24,8},{32,96},{40,56},{48,112},{56,40},{64,... | collective-permute-start | bytes 786440 | tf_op jit(solution)/shard_map/ppermute | solution.py:50
  10.9 0.0 collective-permute-done.5
  11.0 1.8 %collective-permute-start.6 = (f32[512,128]{1,0:T(8,128)S(1)}, f32[512,128]{1,0:T(8,128)S(1)}, u32[]{:S(2)}, u32[]{:S(2)}) collective-permute-start(f32[512,128]{1,0:T(8,128)S(1)} %add.35), channel_id=1, source_target_pairs={{0,192},{8,56},{16,208},{24,40},{32,224},{40,24},{48,240},{56,8},{... | collective-permute-start | bytes 786440 | tf_op jit(solution)/shard_map/ppermute | solution.py:50
  12.7 0.0 collective-permute-done
  12.7 3.5 %collective-permute-done.2 = f32[512,128]{1,0:T(8,128)S(1)} collective-permute-done((f32[512,128]{1,0:T(8,128)S(1)}, f32[512,128]{1,0:T(8,128)S(1)}, u32[]{:S(2)}, u32[]{:S(2)}) %collective-permute-start.2) | collective-permute-done | bytes 262176 | tf_op jit(solution)/shard_map/ppermute | solution.py:50
  16.2 1.4 %collective-permute-done.4 = f32[512,128]{1,0:T(8,128)S(1)} collective-permute-done((f32[512,128]{1,0:T(8,128)S(1)}, f32[512,128]{1,0:T(8,128)S(1)}, u32[]{:S(2)}, u32[]{:S(2)}) %collective-permute-start.4) | collective-permute-done | bytes 262176 | tf_op jit(solution)/shard_map/ppermute | solution.py:50
  17.7 1.4 %collective-permute-done.6 = f32[512,128]{1,0:T(8,128)S(1)} collective-permute-done((f32[512,128]{1,0:T(8,128)S(1)}, f32[512,128]{1,0:T(8,128)S(1)}, u32[]{:S(2)}, u32[]{:S(2)}) %collective-permute-start.6) | collective-permute-done | bytes 262176 | tf_op jit(solution)/shard_map/ppermute | solution.py:50
  19.1 0.1 add_add_fusion.1
  19.1 1.5 %collective-permute-start.9 = (f32[512,128]{1,0:T(8,128)S(1)}, f32[512,128]{1,0:T(8,128)S(1)}, u32[]{:S(2)}, u32[]{:S(2)}) collective-permute-start(f32[512,128]{1,0:T(8,128)S(1)} %add_add_fusion.1), channel_id=1, source_target_pairs={{0,32},{8,136},{16,48},{24,152},{32,0},{40,168},{48,16},{56,184},{... | collective-permute-start | bytes 786440 | tf_op jit(solution)/shard_map/ppermute | solution.py:50
  20.6 0.4 collective-permute-start.8
  21.0 1.5 %collective-permute-start.7 = (f32[512,128]{1,0:T(8,128)S(1)}, f32[512,128]{1,0:T(8,128)S(1)}, u32[]{:S(2)}, u32[]{:S(2)}) collective-permute-start(f32[512,128]{1,0:T(8,128)S(1)} %add_add_fusion.1), channel_id=1, source_target_pairs={{0,48},{8,200},{16,32},{24,216},{32,16},{40,232},{48,0},{56,248},{... | collective-permute-start | bytes 786440 | tf_op jit(solution)/shard_map/ppermute | solution.py:50
  22.5 3.8 %collective-permute-done.9 = f32[512,128]{1,0:T(8,128)S(1)} collective-permute-done((f32[512,128]{1,0:T(8,128)S(1)}, f32[512,128]{1,0:T(8,128)S(1)}, u32[]{:S(2)}, u32[]{:S(2)}) %collective-permute-start.9) | collective-permute-done | bytes 262176 | tf_op jit(solution)/shard_map/ppermute | solution.py:50
  26.2 1.6 %collective-permute-done.8 = f32[512,128]{1,0:T(8,128)S(1)} collective-permute-done((f32[512,128]{1,0:T(8,128)S(1)}, f32[512,128]{1,0:T(8,128)S(1)}, u32[]{:S(2)}, u32[]{:S(2)}) %collective-permute-start.8) | collective-permute-done | bytes 262176 | tf_op jit(solution)/shard_map/ppermute | solution.py:50
  27.8 1.2 %collective-permute-done.7 = f32[512,128]{1,0:T(8,128)S(1)} collective-permute-done((f32[512,128]{1,0:T(8,128)S(1)}, f32[512,128]{1,0:T(8,128)S(1)}, u32[]{:S(2)}, u32[]{:S(2)}) %collective-permute-start.7) | collective-permute-done | bytes 262176 | tf_op jit(solution)/shard_map/ppermute | solution.py:50
  29.1 1.4 %collective-permute-start.12 = (f32[512,128]{1,0:T(8,128)S(1)}, f32[512,128]{1,0:T(8,128)S(1)}, u32[]{:S(2)}, u32[]{:S(2)}) collective-permute-start(f32[512,128]{1,0:T(8,128)S(1)} %add_add_fusion.refs_0_), channel_id=1, source_target_pairs={{0,128},{8,40},{16,144},{24,56},{32,160},{40,8},{48,176},{56,24},{... | collective-permute-start | bytes 786440 | tf_op jit(solution)/shard_map/ppermute | solution.py:50
  30.5 0.4 collective-permute-start.11
  30.9 1.5 %collective-permute-start.10 = (f32[512,128]{1,0:T(8,128)S(1)}, f32[512,128]{1,0:T(8,128)S(1)}, u32[]{:S(2)}, u32[]{:S(2)}) collective-permute-start(f32[512,128]{1,0:T(8,128)S(1)} %add_add_fusion.refs_0_), channel_id=1, source_target_pairs={{0,192},{8,56},{16,208},{24,40},{32,224},{40,24},{48,240},{56,8},{... | collective-permute-start | bytes 786440 | tf_op jit(solution)/shard_map/ppermute | solution.py:50
  32.4 2.9 %collective-permute-start.13 = (f32[512,128]{1,0:T(8,128)S(1)}, f32[512,128]{1,0:T(8,128)S(1)}, u32[]{:S(2)}, u32[]{:S(2)}) collective-permute-start(f32[512,128]{1,0:T(8,128)S(1)} %add_add_fusion.refs_0_), channel_id=1, source_target_pairs={{0,8},{8,0},{16,24},{24,16},{32,40},{40,32},{48,56},{56,48},{64,72... | collective-permute-start | bytes 786440 | tf_op jit(solution)/shard_map/ppermute | solution.py:50
  35.4 0.8 %collective-permute-done.12.refs_3_ = f32[512,128]{1,0:T(8,128)S(1)} collective-permute-done((f32[512,128]{1,0:T(8,128)S(1)}, f32[512,128]{1,0:T(8,128)S(1)}, u32[]{:S(2)}, u32[]{:S(2)}) %collective-permute-start.12) | collective-permute-done | bytes 262176 | tf_op jit(solution)/shard_map/ppermute | solution.py:50
  36.2 3.0 %collective-permute-start.16 = (f32[512,128]{1,0:T(8,128)S(1)}, f32[512,128]{1,0:T(8,128)S(1)}, u32[]{:S(2)}, u32[]{:S(2)}) collective-permute-start(f32[512,128]{1,0:T(8,128)S(1)} %collective-permute-done.12.refs_3_), channel_id=1, source_target_pairs={{0,8},{8,0},{16,24},{24,16},{32,40},{40,32},{48,56},{56,48},{64,72... | collective-permute-start | bytes 786440 | tf_op jit(solution)/shard_map/ppermute | solution.py:50
  39.2 0.0 collective-permute-done.11.refs_2_
  39.2 1.9 %collective-permute-start.15 = (f32[512,128]{1,0:T(8,128)S(1)}, f32[512,128]{1,0:T(8,128)S(1)}, u32[]{:S(2)}, u32[]{:S(2)}) collective-permute-start(f32[512,128]{1,0:T(8,128)S(1)} %collective-permute-done.11.refs_2_), channel_id=1, source_target_pairs={{0,8},{8,0},{16,24},{24,16},{32,40},{40,32},{48,56},{56,48},{64,72... | collective-permute-start | bytes 786440 | tf_op jit(solution)/shard_map/ppermute | solution.py:50
  41.1 0.0 collective-permute-done.10.refs_1_
  41.1 0.9 %collective-permute-start.14 = (f32[512,128]{1,0:T(8,128)S(1)}, f32[512,128]{1,0:T(8,128)S(1)}, u32[]{:S(2)}, u32[]{:S(2)}) collective-permute-start(f32[512,128]{1,0:T(8,128)S(1)} %collective-permute-done.10.refs_1_), channel_id=1, source_target_pairs={{0,8},{8,0},{16,24},{24,16},{32,40},{40,32},{48,56},{56,48},{64,72... | collective-permute-start | bytes 786440 | tf_op jit(solution)/shard_map/ppermute | solution.py:50
  41.9 0.0 copy-done
  42.0 0.0 collective-permute-done.13.refs_4_
  42.0 0.0 collective-permute-done.16.refs_7_
  42.0 0.3 collective-permute-done.15.refs_6_
  42.2 0.9 %collective-permute-done.14.refs_5_ = f32[512,128]{1,0:T(8,128)S(1)} collective-permute-done((f32[512,128]{1,0:T(8,128)S(1)}, f32[512,128]{1,0:T(8,128)S(1)}, u32[]{:S(2)}, u32[]{:S(2)}) %collective-permute-start.14) | collective-permute-done | bytes 262176 | tf_op jit(solution)/shard_map/ppermute | solution.py:50
  43.1 4.1 %shard_map.38 = f32[8192,128]{1,0:T(8,128)} custom-call(s32[4]{0:T(128)S(1)} %pad_add_fusion.where_ref, s32[16,128]{1,0:T(8,128)S(1)} %subtract_multiply_fusion.rows_vmem, f32[512,128]{1,0:T(8,128)S(1)} %add_add_fusion.refs_0_, f32[512,128]{1,0:T(8,128)S(1)} %collective-permute-done.10.refs_1_, f32[512,128]{1,0:T(8,128)S(1)} %collective-permute-done.11.refs_2_, ...), custom_call_target="tpu_custom_call" | custom-call | tf_op jit(solution)/shard_map/pallas_call | solution.py:177
  (5 shorter events, 0.1 us)
Async XLA Ops:
  0.1 41.9 %copy-start = (s32[16,128]{1,0:T(8,128)S(1)}, s32[16,128]{1,0:T(8,128)}, u32[]{:S(2)}) copy-start(s32[16,128]{1,0:T(8,128)} %ids_hbm.1) | copy-start | bytes 24580
  4.6 4.5 %collective-permute-start.1 = (f32[512,128]{1,0:T(8,128)S(1)}, f32[512,128]{1,0:T(8,128)S(1)}, u32[]{:S(2)}, u32[]{:S(2)}) collective-permute-start(f32[512,128]{1,0:T(8,128)S(1)} %get-tuple-element.16), channel_id=1, source_target_pairs={{0,8},{8,0},{16,24},{24,16},{32,40},{40,32},{48,56},{56,48},{64,72... | collective-permute-start | bytes 786440 | tf_op jit(solution)/shard_map/ppermute | solution.py:50
  7.9 2.5 %collective-permute-start.3 = (f32[512,128]{1,0:T(8,128)S(1)}, f32[512,128]{1,0:T(8,128)S(1)}, u32[]{:S(2)}, u32[]{:S(2)}) collective-permute-start(f32[512,128]{1,0:T(8,128)S(1)} %get-tuple-element.18), channel_id=1, source_target_pairs={{0,8},{8,0},{16,24},{24,16},{32,40},{40,32},{48,56},{56,48},{64,72... | collective-permute-start | bytes 786440 | tf_op jit(solution)/shard_map/ppermute | solution.py:50
  8.0 2.9 %collective-permute-start.5 = (f32[512,128]{1,0:T(8,128)S(1)}, f32[512,128]{1,0:T(8,128)S(1)}, u32[]{:S(2)}, u32[]{:S(2)}) collective-permute-start(f32[512,128]{1,0:T(8,128)S(1)} %get-tuple-element.20), channel_id=1, source_target_pairs={{0,8},{8,0},{16,24},{24,16},{32,40},{40,32},{48,56},{56,48},{64,72... | collective-permute-start | bytes 786440 | tf_op jit(solution)/shard_map/ppermute | solution.py:50
  8.5 4.3 %collective-permute-start = (f32[512,128]{1,0:T(8,128)S(1)}, f32[512,128]{1,0:T(8,128)S(1)}, u32[]{:S(2)}, u32[]{:S(2)}) collective-permute-start(f32[512,128]{1,0:T(8,128)S(1)} %get-tuple-element.14), channel_id=1, source_target_pairs={{0,8},{8,0},{16,24},{24,16},{32,40},{40,32},{48,56},{56,48},{64,72... | collective-permute-start | bytes 786440 | tf_op jit(solution)/shard_map/ppermute | solution.py:50
  9.1 7.1 %collective-permute-start.2 = (f32[512,128]{1,0:T(8,128)S(1)}, f32[512,128]{1,0:T(8,128)S(1)}, u32[]{:S(2)}, u32[]{:S(2)}) collective-permute-start(f32[512,128]{1,0:T(8,128)S(1)} %add.31), channel_id=1, source_target_pairs={{0,128},{8,40},{16,144},{24,56},{32,160},{40,8},{48,176},{56,24},{... | collective-permute-start | bytes 786440 | tf_op jit(solution)/shard_map/ppermute | solution.py:50
  10.4 7.2 %collective-permute-start.4 = (f32[512,128]{1,0:T(8,128)S(1)}, f32[512,128]{1,0:T(8,128)S(1)}, u32[]{:S(2)}, u32[]{:S(2)}) collective-permute-start(f32[512,128]{1,0:T(8,128)S(1)} %add.33), channel_id=1, source_target_pairs={{0,64},{8,24},{16,80},{24,8},{32,96},{40,56},{48,112},{56,40},{64,... | collective-permute-start | bytes 786440 | tf_op jit(solution)/shard_map/ppermute | solution.py:50
  11.0 8.1 %collective-permute-start.6 = (f32[512,128]{1,0:T(8,128)S(1)}, f32[512,128]{1,0:T(8,128)S(1)}, u32[]{:S(2)}, u32[]{:S(2)}) collective-permute-start(f32[512,128]{1,0:T(8,128)S(1)} %add.35), channel_id=1, source_target_pairs={{0,192},{8,56},{16,208},{24,40},{32,224},{40,24},{48,240},{56,8},{... | collective-permute-start | bytes 786440 | tf_op jit(solution)/shard_map/ppermute | solution.py:50
  19.1 7.1 %collective-permute-start.9 = (f32[512,128]{1,0:T(8,128)S(1)}, f32[512,128]{1,0:T(8,128)S(1)}, u32[]{:S(2)}, u32[]{:S(2)}) collective-permute-start(f32[512,128]{1,0:T(8,128)S(1)} %add_add_fusion.1), channel_id=1, source_target_pairs={{0,32},{8,136},{16,48},{24,152},{32,0},{40,168},{48,16},{56,184},{... | collective-permute-start | bytes 786440 | tf_op jit(solution)/shard_map/ppermute | solution.py:50
  20.6 7.2 %collective-permute-start.8 = (f32[512,128]{1,0:T(8,128)S(1)}, f32[512,128]{1,0:T(8,128)S(1)}, u32[]{:S(2)}, u32[]{:S(2)}) collective-permute-start(f32[512,128]{1,0:T(8,128)S(1)} %add_add_fusion.1), channel_id=1, source_target_pairs={{0,16},{8,72},{16,0},{24,88},{32,48},{40,104},{48,32},{56,120},{64... | collective-permute-start | bytes 786440 | tf_op jit(solution)/shard_map/ppermute | solution.py:50
  21.0 8.1 %collective-permute-start.7 = (f32[512,128]{1,0:T(8,128)S(1)}, f32[512,128]{1,0:T(8,128)S(1)}, u32[]{:S(2)}, u32[]{:S(2)}) collective-permute-start(f32[512,128]{1,0:T(8,128)S(1)} %add_add_fusion.1), channel_id=1, source_target_pairs={{0,48},{8,200},{16,32},{24,216},{32,16},{40,232},{48,0},{56,248},{... | collective-permute-start | bytes 786440 | tf_op jit(solution)/shard_map/ppermute | solution.py:50
  29.1 7.1 %collective-permute-start.12 = (f32[512,128]{1,0:T(8,128)S(1)}, f32[512,128]{1,0:T(8,128)S(1)}, u32[]{:S(2)}, u32[]{:S(2)}) collective-permute-start(f32[512,128]{1,0:T(8,128)S(1)} %add_add_fusion.refs_0_), channel_id=1, source_target_pairs={{0,128},{8,40},{16,144},{24,56},{32,160},{40,8},{48,176},{56,24},{... | collective-permute-start | bytes 786440 | tf_op jit(solution)/shard_map/ppermute | solution.py:50
  30.5 8.7 %collective-permute-start.11 = (f32[512,128]{1,0:T(8,128)S(1)}, f32[512,128]{1,0:T(8,128)S(1)}, u32[]{:S(2)}, u32[]{:S(2)}) collective-permute-start(f32[512,128]{1,0:T(8,128)S(1)} %add_add_fusion.refs_0_), channel_id=1, source_target_pairs={{0,64},{8,24},{16,80},{24,8},{32,96},{40,56},{48,112},{56,40},{64,... | collective-permute-start | bytes 786440 | tf_op jit(solution)/shard_map/ppermute | solution.py:50
  30.9 10.2 %collective-permute-start.10 = (f32[512,128]{1,0:T(8,128)S(1)}, f32[512,128]{1,0:T(8,128)S(1)}, u32[]{:S(2)}, u32[]{:S(2)}) collective-permute-start(f32[512,128]{1,0:T(8,128)S(1)} %add_add_fusion.refs_0_), channel_id=1, source_target_pairs={{0,192},{8,56},{16,208},{24,40},{32,224},{40,24},{48,240},{56,8},{... | collective-permute-start | bytes 786440 | tf_op jit(solution)/shard_map/ppermute | solution.py:50
  32.4 9.5 %collective-permute-start.13 = (f32[512,128]{1,0:T(8,128)S(1)}, f32[512,128]{1,0:T(8,128)S(1)}, u32[]{:S(2)}, u32[]{:S(2)}) collective-permute-start(f32[512,128]{1,0:T(8,128)S(1)} %add_add_fusion.refs_0_), channel_id=1, source_target_pairs={{0,8},{8,0},{16,24},{24,16},{32,40},{40,32},{48,56},{56,48},{64,72... | collective-permute-start | bytes 786440 | tf_op jit(solution)/shard_map/ppermute | solution.py:50
  36.2 5.8 %collective-permute-start.16 = (f32[512,128]{1,0:T(8,128)S(1)}, f32[512,128]{1,0:T(8,128)S(1)}, u32[]{:S(2)}, u32[]{:S(2)}) collective-permute-start(f32[512,128]{1,0:T(8,128)S(1)} %collective-permute-done.12.refs_3_), channel_id=1, source_target_pairs={{0,8},{8,0},{16,24},{24,16},{32,40},{40,32},{48,56},{56,48},{64,72... | collective-permute-start | bytes 786440 | tf_op jit(solution)/shard_map/ppermute | solution.py:50
  39.2 3.0 %collective-permute-start.15 = (f32[512,128]{1,0:T(8,128)S(1)}, f32[512,128]{1,0:T(8,128)S(1)}, u32[]{:S(2)}, u32[]{:S(2)}) collective-permute-start(f32[512,128]{1,0:T(8,128)S(1)} %collective-permute-done.11.refs_2_), channel_id=1, source_target_pairs={{0,8},{8,0},{16,24},{24,16},{32,40},{40,32},{48,56},{56,48},{64,72... | collective-permute-start | bytes 786440 | tf_op jit(solution)/shard_map/ppermute | solution.py:50
  41.1 2.0 %collective-permute-start.14 = (f32[512,128]{1,0:T(8,128)S(1)}, f32[512,128]{1,0:T(8,128)S(1)}, u32[]{:S(2)}, u32[]{:S(2)}) collective-permute-start(f32[512,128]{1,0:T(8,128)S(1)} %collective-permute-done.10.refs_1_), channel_id=1, source_target_pairs={{0,8},{8,0},{16,24},{24,16},{32,40},{40,32},{48,56},{56,48},{64,72... | collective-permute-start | bytes 786440 | tf_op jit(solution)/shard_map/ppermute | solution.py:50

commit v6 on v5

--- a/solution.py
+++ b/solution.py
@@ -74,7 +74,7 @@
 
 
 def scatter(where_ref, coef_hbm, ids_hbm, surplus_hbm, *refs):
-    pieces, (table, stage, ids, coef, sems, small_sems) = refs[:8], refs[8:]
+    pieces, (even, odd, stage, ids, coef, sems, small_sems) = refs[:8], refs[8:]
 
     def load(g):
         part = pl.ds(pl.multiple_of(g * GRID_ROWS, GRID_ROWS), GRID_ROWS)
@@ -88,7 +88,8 @@
         load(g).start()
     base = where_ref[0] * SUB
     own_rows = pl.ds(pl.multiple_of(base, NBD * SUB), NBD * SUB)
-    table[own_rows, :] = jnp.zeros((NBD * SUB, LANES), jnp.float32)
+    for table in (even, odd):
+        table[own_rows, :] = jnp.zeros((NBD * SUB, LANES), jnp.float32)
     ids_copy.wait()
     coef_copy.wait()
 
@@ -98,6 +99,7 @@
         start = pl.multiple_of(g * GRID_ROWS, GRID_ROWS)
         for first in range(0, K, BATCH):
             slots = range(first, first + BATCH)
+            table = odd if first // BATCH % 2 else even
             rows = [block_rows(ids[g, j] * SUB) for j in slots]
             sums = [table[r, :] + stage[slot_rows(start, j), :] * factor for r, j in zip(rows, slots)]
             for r, total in zip(rows, sums):
@@ -107,8 +109,9 @@
     lax.fori_loop(0, GRIDS, add_grid, 0)
     core = where_ref[3]
     for k in range(4):
-        pieces[k][...] = table[piece_rows(where_ref, 1 - core, k, base), :]
-        pieces[4 + k][...] = table[piece_rows(where_ref, core, k, base), :]
+        for piece, half in ((pieces[k], 1 - core), (pieces[4 + k], core)):
+            rows = piece_rows(where_ref, half, k, base)
+            piece[...] = even[rows, :] + odd[rows, :]
 
 
 def gather(where_ref, rows_vmem, *refs):
@@ -157,6 +160,7 @@
         in_specs=[smem, hbm, hbm, hbm],
         out_specs=(vmem,) * 8,
         scratch_shapes=[
+            VMEM((ALL_BLOCKS * SUB + PAD, LANES), jnp.float32),
             VMEM((ALL_BLOCKS * SUB + PAD, LANES), jnp.float32),
             stage,
             pltpu.SMEM((GRIDS, K), jnp.int32),

time: 47.3 us -> 47 us (level)
  no operation moved by 1% of the time
where the time goes in v6:
time: 47 us; the launch traced here: 46.9 us
  starting transfers between devices  22.8 us (49%)
  waiting for transfers between devices  15.5 us (33%)
  Pallas kernels  8.33 us (18%)
    ppermute x17, starting transfers between devices, send(): return lax.ppermute(value, 'grp', partner)  22.8 us
    ppermute x17, waiting for transfers between devices, send(): return lax.ppermute(value, 'grp', partner)  15.5 us
    pallas_call x1, Pallas kernels, local(): pl.pallas_call(scatter, out_shape=(piece,) * 8, in_specs=[smem, hbm, hbm,...  4.25 us
    pallas_call x1, Pallas kernels, local(): pl.pallas_call(gather, out_shape=jax.ShapeDtypeStruct((GRIDS * GRID_ROWS,...  4.08 us
  transfers between devices with their start and end apart: 17, of which 10 were waited for; matrix products, arithmetic and copies ran while one was open for 0% of the time, Pallas kernels for 0%

profile of v6, /device:TPU:1, one launch (start us, length us, event | category | flops | bytes accessed | tf_op | source)
XLA Modules:
  0.0 46.9 jit_solution(14508498157254263401)
XLA Ops:
  0.0 0.1 pad_add_fusion.where_ref
  0.1 0.0 copy-start
  0.1 4.3 %shard_map.37 = (f32[512,128]{1,0:T(8,128)S(1)}, f32[512,128]{1,0:T(8,128)S(1)}, f32[512,128]{1,0:T(8,128)S(1)}, f32[512,128]{1,0:T(8,128)S(1)}, f32[512,128]{1,...) custom-call(s32[4]{0:T(128)S(1)} %pad_add_fusion.where_ref, s32[16]{0:T(128)} %coef_hbm.1, ...), custom_call_target="tpu_custom_call" | custom-call | tf_op jit(solution)/shard_map/pallas_call | solution.py:157
  4.3 3.3 %collective-permute-start.1 = (f32[512,128]{1,0:T(8,128)S(1)}, f32[512,128]{1,0:T(8,128)S(1)}, u32[]{:S(2)}, u32[]{:S(2)}) collective-permute-start(f32[512,128]{1,0:T(8,128)S(1)} %get-tuple-element.16), channel_id=1, source_target_pairs={{0,8},{8,0},{16,24},{24,16},{32,40},{40,32},{48,56},{56,48},{64,72... | collective-permute-start | bytes 786440 | tf_op jit(solution)/shard_map/ppermute | solution.py:50
  7.7 0.1 collective-permute-start.3
  7.8 0.4 collective-permute-start.5
  8.2 0.1 collective-permute-start
  8.3 0.6 %collective-permute-done.1 = f32[512,128]{1,0:T(8,128)S(1)} collective-permute-done((f32[512,128]{1,0:T(8,128)S(1)}, f32[512,128]{1,0:T(8,128)S(1)}, u32[]{:S(2)}, u32[]{:S(2)}) %collective-permute-start.1) | collective-permute-done | bytes 262176 | tf_op jit(solution)/shard_map/ppermute | solution.py:50
  8.9 1.3 %collective-permute-start.2 = (f32[512,128]{1,0:T(8,128)S(1)}, f32[512,128]{1,0:T(8,128)S(1)}, u32[]{:S(2)}, u32[]{:S(2)}) collective-permute-start(f32[512,128]{1,0:T(8,128)S(1)} %add.31), channel_id=1, source_target_pairs={{0,128},{8,40},{16,144},{24,56},{32,160},{40,8},{48,176},{56,24},{... | collective-permute-start | bytes 786440 | tf_op jit(solution)/shard_map/ppermute | solution.py:50
  10.1 0.0 collective-permute-done.3
  10.2 0.5 %collective-permute-start.4 = (f32[512,128]{1,0:T(8,128)S(1)}, f32[512,128]{1,0:T(8,128)S(1)}, u32[]{:S(2)}, u32[]{:S(2)}) collective-permute-start(f32[512,128]{1,0:T(8,128)S(1)} %add.33), channel_id=1, source_target_pairs={{0,64},{8,24},{16,80},{24,8},{32,96},{40,56},{48,112},{56,40},{64,... | collective-permute-start | bytes 786440 | tf_op jit(solution)/shard_map/ppermute | solution.py:50
  10.6 0.0 collective-permute-done.5
  10.7 1.8 %collective-permute-start.6 = (f32[512,128]{1,0:T(8,128)S(1)}, f32[512,128]{1,0:T(8,128)S(1)}, u32[]{:S(2)}, u32[]{:S(2)}) collective-permute-start(f32[512,128]{1,0:T(8,128)S(1)} %add.35), channel_id=1, source_target_pairs={{0,192},{8,56},{16,208},{24,40},{32,224},{40,24},{48,240},{56,8},{... | collective-permute-start | bytes 786440 | tf_op jit(solution)/shard_map/ppermute | solution.py:50
  12.4 0.0 collective-permute-done
  12.5 3.5 %collective-permute-done.2 = f32[512,128]{1,0:T(8,128)S(1)} collective-permute-done((f32[512,128]{1,0:T(8,128)S(1)}, f32[512,128]{1,0:T(8,128)S(1)}, u32[]{:S(2)}, u32[]{:S(2)}) %collective-permute-start.2) | collective-permute-done | bytes 262176 | tf_op jit(solution)/shard_map/ppermute | solution.py:50
  16.0 1.4 %collective-permute-done.4 = f32[512,128]{1,0:T(8,128)S(1)} collective-permute-done((f32[512,128]{1,0:T(8,128)S(1)}, f32[512,128]{1,0:T(8,128)S(1)}, u32[]{:S(2)}, u32[]{:S(2)}) %collective-permute-start.4) | collective-permute-done | bytes 262176 | tf_op jit(solution)/shard_map/ppermute | solution.py:50
  17.4 1.4 %collective-permute-done.6 = f32[512,128]{1,0:T(8,128)S(1)} collective-permute-done((f32[512,128]{1,0:T(8,128)S(1)}, f32[512,128]{1,0:T(8,128)S(1)}, u32[]{:S(2)}, u32[]{:S(2)}) %collective-permute-start.6) | collective-permute-done | bytes 262176 | tf_op jit(solution)/shard_map/ppermute | solution.py:50
  18.8 0.1 add_add_fusion.1
  18.8 1.5 %collective-permute-start.9 = (f32[512,128]{1,0:T(8,128)S(1)}, f32[512,128]{1,0:T(8,128)S(1)}, u32[]{:S(2)}, u32[]{:S(2)}) collective-permute-start(f32[512,128]{1,0:T(8,128)S(1)} %add_add_fusion.1), channel_id=1, source_target_pairs={{0,32},{8,136},{16,48},{24,152},{32,0},{40,168},{48,16},{56,184},{... | collective-permute-start | bytes 786440 | tf_op jit(solution)/shard_map/ppermute | solution.py:50
  20.3 0.4 collective-permute-start.8
  20.7 1.5 %collective-permute-start.7 = (f32[512,128]{1,0:T(8,128)S(1)}, f32[512,128]{1,0:T(8,128)S(1)}, u32[]{:S(2)}, u32[]{:S(2)}) collective-permute-start(f32[512,128]{1,0:T(8,128)S(1)} %add_add_fusion.1), channel_id=1, source_target_pairs={{0,48},{8,200},{16,32},{24,216},{32,16},{40,232},{48,0},{56,248},{... | collective-permute-start | bytes 786440 | tf_op jit(solution)/shard_map/ppermute | solution.py:50
  22.2 3.8 %collective-permute-done.9 = f32[512,128]{1,0:T(8,128)S(1)} collective-permute-done((f32[512,128]{1,0:T(8,128)S(1)}, f32[512,128]{1,0:T(8,128)S(1)}, u32[]{:S(2)}, u32[]{:S(2)}) %collective-permute-start.9) | collective-permute-done | bytes 262176 | tf_op jit(solution)/shard_map/ppermute | solution.py:50
  26.0 1.6 %collective-permute-done.8 = f32[512,128]{1,0:T(8,128)S(1)} collective-permute-done((f32[512,128]{1,0:T(8,128)S(1)}, f32[512,128]{1,0:T(8,128)S(1)}, u32[]{:S(2)}, u32[]{:S(2)}) %collective-permute-start.8) | collective-permute-done | bytes 262176 | tf_op jit(solution)/shard_map/ppermute | solution.py:50
  27.6 1.2 %collective-permute-done.7 = f32[512,128]{1,0:T(8,128)S(1)} collective-permute-done((f32[512,128]{1,0:T(8,128)S(1)}, f32[512,128]{1,0:T(8,128)S(1)}, u32[]{:S(2)}, u32[]{:S(2)}) %collective-permute-start.7) | collective-permute-done | bytes 262176 | tf_op jit(solution)/shard_map/ppermute | solution.py:50
  28.8 1.4 %collective-permute-start.12 = (f32[512,128]{1,0:T(8,128)S(1)}, f32[512,128]{1,0:T(8,128)S(1)}, u32[]{:S(2)}, u32[]{:S(2)}) collective-permute-start(f32[512,128]{1,0:T(8,128)S(1)} %add_add_fusion.refs_0_), channel_id=1, source_target_pairs={{0,128},{8,40},{16,144},{24,56},{32,160},{40,8},{48,176},{56,24},{... | collective-permute-start | bytes 786440 | tf_op jit(solution)/shard_map/ppermute | solution.py:50
  30.2 0.4 collective-permute-start.11
  30.6 1.5 %collective-permute-start.10 = (f32[512,128]{1,0:T(8,128)S(1)}, f32[512,128]{1,0:T(8,128)S(1)}, u32[]{:S(2)}, u32[]{:S(2)}) collective-permute-start(f32[512,128]{1,0:T(8,128)S(1)} %add_add_fusion.refs_0_), channel_id=1, source_target_pairs={{0,192},{8,56},{16,208},{24,40},{32,224},{40,24},{48,240},{56,8},{... | collective-permute-start | bytes 786440 | tf_op jit(solution)/shard_map/ppermute | solution.py:50
  32.2 2.9 %collective-permute-start.13 = (f32[512,128]{1,0:T(8,128)S(1)}, f32[512,128]{1,0:T(8,128)S(1)}, u32[]{:S(2)}, u32[]{:S(2)}) collective-permute-start(f32[512,128]{1,0:T(8,128)S(1)} %add_add_fusion.refs_0_), channel_id=1, source_target_pairs={{0,8},{8,0},{16,24},{24,16},{32,40},{40,32},{48,56},{56,48},{64,72... | collective-permute-start | bytes 786440 | tf_op jit(solution)/shard_map/ppermute | solution.py:50
  35.1 0.8 %collective-permute-done.12.refs_3_ = f32[512,128]{1,0:T(8,128)S(1)} collective-permute-done((f32[512,128]{1,0:T(8,128)S(1)}, f32[512,128]{1,0:T(8,128)S(1)}, u32[]{:S(2)}, u32[]{:S(2)}) %collective-permute-start.12) | collective-permute-done | bytes 262176 | tf_op jit(solution)/shard_map/ppermute | solution.py:50
  35.9 3.0 %collective-permute-start.16 = (f32[512,128]{1,0:T(8,128)S(1)}, f32[512,128]{1,0:T(8,128)S(1)}, u32[]{:S(2)}, u32[]{:S(2)}) collective-permute-start(f32[512,128]{1,0:T(8,128)S(1)} %collective-permute-done.12.refs_3_), channel_id=1, source_target_pairs={{0,8},{8,0},{16,24},{24,16},{32,40},{40,32},{48,56},{56,48},{64,72... | collective-permute-start | bytes 786440 | tf_op jit(solution)/shard_map/ppermute | solution.py:50
  38.9 0.0 collective-permute-done.11.refs_2_
  38.9 1.9 %collective-permute-start.15 = (f32[512,128]{1,0:T(8,128)S(1)}, f32[512,128]{1,0:T(8,128)S(1)}, u32[]{:S(2)}, u32[]{:S(2)}) collective-permute-start(f32[512,128]{1,0:T(8,128)S(1)} %collective-permute-done.11.refs_2_), channel_id=1, source_target_pairs={{0,8},{8,0},{16,24},{24,16},{32,40},{40,32},{48,56},{56,48},{64,72... | collective-permute-start | bytes 786440 | tf_op jit(solution)/shard_map/ppermute | solution.py:50
  40.8 0.0 collective-permute-done.10.refs_1_
  40.8 0.9 %collective-permute-start.14 = (f32[512,128]{1,0:T(8,128)S(1)}, f32[512,128]{1,0:T(8,128)S(1)}, u32[]{:S(2)}, u32[]{:S(2)}) collective-permute-start(f32[512,128]{1,0:T(8,128)S(1)} %collective-permute-done.10.refs_1_), channel_id=1, source_target_pairs={{0,8},{8,0},{16,24},{24,16},{32,40},{40,32},{48,56},{56,48},{64,72... | collective-permute-start | bytes 786440 | tf_op jit(solution)/shard_map/ppermute | solution.py:50
  41.7 0.0 copy-done
  41.7 0.0 collective-permute-done.13.refs_4_
  41.7 0.0 collective-permute-done.16.refs_7_
  41.7 0.3 collective-permute-done.15.refs_6_
  42.0 0.9 %collective-permute-done.14.refs_5_ = f32[512,128]{1,0:T(8,128)S(1)} collective-permute-done((f32[512,128]{1,0:T(8,128)S(1)}, f32[512,128]{1,0:T(8,128)S(1)}, u32[]{:S(2)}, u32[]{:S(2)}) %collective-permute-start.14) | collective-permute-done | bytes 262176 | tf_op jit(solution)/shard_map/ppermute | solution.py:50
  42.8 4.1 %shard_map.38 = f32[8192,128]{1,0:T(8,128)} custom-call(s32[4]{0:T(128)S(1)} %pad_add_fusion.where_ref, s32[16,128]{1,0:T(8,128)S(1)} %subtract_multiply_fusion.rows_vmem, f32[512,128]{1,0:T(8,128)S(1)} %add_add_fusion.refs_0_, f32[512,128]{1,0:T(8,128)S(1)} %collective-permute-done.10.refs_1_, f32[512,128]{1,0:T(8,128)S(1)} %collective-permute-done.11.refs_2_, ...), custom_call_target="tpu_custom_call" | custom-call | tf_op jit(solution)/shard_map/pallas_call | solution.py:181
  (5 shorter events, 0.1 us)
Async XLA Ops:
  0.1 41.6 %copy-start = (s32[16,128]{1,0:T(8,128)S(1)}, s32[16,128]{1,0:T(8,128)}, u32[]{:S(2)}) copy-start(s32[16,128]{1,0:T(8,128)} %ids_hbm.1) | copy-start | bytes 24580
  4.3 4.5 %collective-permute-start.1 = (f32[512,128]{1,0:T(8,128)S(1)}, f32[512,128]{1,0:T(8,128)S(1)}, u32[]{:S(2)}, u32[]{:S(2)}) collective-permute-start(f32[512,128]{1,0:T(8,128)S(1)} %get-tuple-element.16), channel_id=1, source_target_pairs={{0,8},{8,0},{16,24},{24,16},{32,40},{40,32},{48,56},{56,48},{64,72... | collective-permute-start | bytes 786440 | tf_op jit(solution)/shard_map/ppermute | solution.py:50
  7.7 2.5 %collective-permute-start.3 = (f32[512,128]{1,0:T(8,128)S(1)}, f32[512,128]{1,0:T(8,128)S(1)}, u32[]{:S(2)}, u32[]{:S(2)}) collective-permute-start(f32[512,128]{1,0:T(8,128)S(1)} %get-tuple-element.18), channel_id=1, source_target_pairs={{0,8},{8,0},{16,24},{24,16},{32,40},{40,32},{48,56},{56,48},{64,72... | collective-permute-start | bytes 786440 | tf_op jit(solution)/shard_map/ppermute | solution.py:50
  7.8 2.9 %collective-permute-start.5 = (f32[512,128]{1,0:T(8,128)S(1)}, f32[512,128]{1,0:T(8,128)S(1)}, u32[]{:S(2)}, u32[]{:S(2)}) collective-permute-start(f32[512,128]{1,0:T(8,128)S(1)} %get-tuple-element.20), channel_id=1, source_target_pairs={{0,8},{8,0},{16,24},{24,16},{32,40},{40,32},{48,56},{56,48},{64,72... | collective-permute-start | bytes 786440 | tf_op jit(solution)/shard_map/ppermute | solution.py:50
  8.2 4.3 %collective-permute-start = (f32[512,128]{1,0:T(8,128)S(1)}, f32[512,128]{1,0:T(8,128)S(1)}, u32[]{:S(2)}, u32[]{:S(2)}) collective-permute-start(f32[512,128]{1,0:T(8,128)S(1)} %get-tuple-element.14), channel_id=1, source_target_pairs={{0,8},{8,0},{16,24},{24,16},{32,40},{40,32},{48,56},{56,48},{64,72... | collective-permute-start | bytes 786440 | tf_op jit(solution)/shard_map/ppermute | solution.py:50
  8.9 7.1 %collective-permute-start.2 = (f32[512,128]{1,0:T(8,128)S(1)}, f32[512,128]{1,0:T(8,128)S(1)}, u32[]{:S(2)}, u32[]{:S(2)}) collective-permute-start(f32[512,128]{1,0:T(8,128)S(1)} %add.31), channel_id=1, source_target_pairs={{0,128},{8,40},{16,144},{24,56},{32,160},{40,8},{48,176},{56,24},{... | collective-permute-start | bytes 786440 | tf_op jit(solution)/shard_map/ppermute | solution.py:50
  10.2 7.2 %collective-permute-start.4 = (f32[512,128]{1,0:T(8,128)S(1)}, f32[512,128]{1,0:T(8,128)S(1)}, u32[]{:S(2)}, u32[]{:S(2)}) collective-permute-start(f32[512,128]{1,0:T(8,128)S(1)} %add.33), channel_id=1, source_target_pairs={{0,64},{8,24},{16,80},{24,8},{32,96},{40,56},{48,112},{56,40},{64,... | collective-permute-start | bytes 786440 | tf_op jit(solution)/shard_map/ppermute | solution.py:50
  10.7 8.1 %collective-permute-start.6 = (f32[512,128]{1,0:T(8,128)S(1)}, f32[512,128]{1,0:T(8,128)S(1)}, u32[]{:S(2)}, u32[]{:S(2)}) collective-permute-start(f32[512,128]{1,0:T(8,128)S(1)} %add.35), channel_id=1, source_target_pairs={{0,192},{8,56},{16,208},{24,40},{32,224},{40,24},{48,240},{56,8},{... | collective-permute-start | bytes 786440 | tf_op jit(solution)/shard_map/ppermute | solution.py:50
  18.8 7.1 %collective-permute-start.9 = (f32[512,128]{1,0:T(8,128)S(1)}, f32[512,128]{1,0:T(8,128)S(1)}, u32[]{:S(2)}, u32[]{:S(2)}) collective-permute-start(f32[512,128]{1,0:T(8,128)S(1)} %add_add_fusion.1), channel_id=1, source_target_pairs={{0,32},{8,136},{16,48},{24,152},{32,0},{40,168},{48,16},{56,184},{... | collective-permute-start | bytes 786440 | tf_op jit(solution)/shard_map/ppermute | solution.py:50
  20.3 7.2 %collective-permute-start.8 = (f32[512,128]{1,0:T(8,128)S(1)}, f32[512,128]{1,0:T(8,128)S(1)}, u32[]{:S(2)}, u32[]{:S(2)}) collective-permute-start(f32[512,128]{1,0:T(8,128)S(1)} %add_add_fusion.1), channel_id=1, source_target_pairs={{0,16},{8,72},{16,0},{24,88},{32,48},{40,104},{48,32},{56,120},{64... | collective-permute-start | bytes 786440 | tf_op jit(solution)/shard_map/ppermute | solution.py:50
  20.7 8.1 %collective-permute-start.7 = (f32[512,128]{1,0:T(8,128)S(1)}, f32[512,128]{1,0:T(8,128)S(1)}, u32[]{:S(2)}, u32[]{:S(2)}) collective-permute-start(f32[512,128]{1,0:T(8,128)S(1)} %add_add_fusion.1), channel_id=1, source_target_pairs={{0,48},{8,200},{16,32},{24,216},{32,16},{40,232},{48,0},{56,248},{... | collective-permute-start | bytes 786440 | tf_op jit(solution)/shard_map/ppermute | solution.py:50
  28.8 7.1 %collective-permute-start.12 = (f32[512,128]{1,0:T(8,128)S(1)}, f32[512,128]{1,0:T(8,128)S(1)}, u32[]{:S(2)}, u32[]{:S(2)}) collective-permute-start(f32[512,128]{1,0:T(8,128)S(1)} %add_add_fusion.refs_0_), channel_id=1, source_target_pairs={{0,128},{8,40},{16,144},{24,56},{32,160},{40,8},{48,176},{56,24},{... | collective-permute-start | bytes 786440 | tf_op jit(solution)/shard_map/ppermute | solution.py:50
  30.2 8.7 %collective-permute-start.11 = (f32[512,128]{1,0:T(8,128)S(1)}, f32[512,128]{1,0:T(8,128)S(1)}, u32[]{:S(2)}, u32[]{:S(2)}) collective-permute-start(f32[512,128]{1,0:T(8,128)S(1)} %add_add_fusion.refs_0_), channel_id=1, source_target_pairs={{0,64},{8,24},{16,80},{24,8},{32,96},{40,56},{48,112},{56,40},{64,... | collective-permute-start | bytes 786440 | tf_op jit(solution)/shard_map/ppermute | solution.py:50
  30.6 10.2 %collective-permute-start.10 = (f32[512,128]{1,0:T(8,128)S(1)}, f32[512,128]{1,0:T(8,128)S(1)}, u32[]{:S(2)}, u32[]{:S(2)}) collective-permute-start(f32[512,128]{1,0:T(8,128)S(1)} %add_add_fusion.refs_0_), channel_id=1, source_target_pairs={{0,192},{8,56},{16,208},{24,40},{32,224},{40,24},{48,240},{56,8},{... | collective-permute-start | bytes 786440 | tf_op jit(solution)/shard_map/ppermute | solution.py:50
  32.2 9.5 %collective-permute-start.13 = (f32[512,128]{1,0:T(8,128)S(1)}, f32[512,128]{1,0:T(8,128)S(1)}, u32[]{:S(2)}, u32[]{:S(2)}) collective-permute-start(f32[512,128]{1,0:T(8,128)S(1)} %add_add_fusion.refs_0_), channel_id=1, source_target_pairs={{0,8},{8,0},{16,24},{24,16},{32,40},{40,32},{48,56},{56,48},{64,72... | collective-permute-start | bytes 786440 | tf_op jit(solution)/shard_map/ppermute | solution.py:50
  35.9 5.8 %collective-permute-start.16 = (f32[512,128]{1,0:T(8,128)S(1)}, f32[512,128]{1,0:T(8,128)S(1)}, u32[]{:S(2)}, u32[]{:S(2)}) collective-permute-start(f32[512,128]{1,0:T(8,128)S(1)} %collective-permute-done.12.refs_3_), channel_id=1, source_target_pairs={{0,8},{8,0},{16,24},{24,16},{32,40},{40,32},{48,56},{56,48},{64,72... | collective-permute-start | bytes 786440 | tf_op jit(solution)/shard_map/ppermute | solution.py:50
  38.9 3.0 %collective-permute-start.15 = (f32[512,128]{1,0:T(8,128)S(1)}, f32[512,128]{1,0:T(8,128)S(1)}, u32[]{:S(2)}, u32[]{:S(2)}) collective-permute-start(f32[512,128]{1,0:T(8,128)S(1)} %collective-permute-done.11.refs_2_), channel_id=1, source_target_pairs={{0,8},{8,0},{16,24},{24,16},{32,40},{40,32},{48,56},{56,48},{64,72... | collective-permute-start | bytes 786440 | tf_op jit(solution)/shard_map/ppermute | solution.py:50
  40.8 2.0 %collective-permute-start.14 = (f32[512,128]{1,0:T(8,128)S(1)}, f32[512,128]{1,0:T(8,128)S(1)}, u32[]{:S(2)}, u32[]{:S(2)}) collective-permute-start(f32[512,128]{1,0:T(8,128)S(1)} %collective-permute-done.10.refs_1_), channel_id=1, source_target_pairs={{0,8},{8,0},{16,24},{24,16},{32,40},{40,32},{48,56},{56,48},{64,72... | collective-permute-start | bytes 786440 | tf_op jit(solution)/shard_map/ppermute | solution.py:50

commit v7 on v6

--- a/solution.py
+++ b/solution.py
@@ -15,7 +15,8 @@
 HALF = NBD // 2 * SUB
 PIECE = HALF // 4
 ALL_BLOCKS = 8 * NBD
-BATCH = 16
+SCATTER_BATCH = 8
+GATHER_BATCH = 16
 PAD = 64
 ORDER = (0, 3, 1, 2)
 VMEM = pltpu.VMEM
@@ -97,9 +98,9 @@
         load(g).wait()
         factor = coef[g].astype(jnp.float32)
         start = pl.multiple_of(g * GRID_ROWS, GRID_ROWS)
-        for first in range(0, K, BATCH):
-            slots = range(first, first + BATCH)
-            table = odd if first // BATCH % 2 else even
+        for first in range(0, K, SCATTER_BATCH):
+            slots = range(first, first + SCATTER_BATCH)
+            table = odd if first // SCATTER_BATCH % 2 else even
             rows = [block_rows(ids[g, j] * SUB) for j in slots]
             sums = [table[r, :] + stage[slot_rows(start, j), :] * factor for r, j in zip(rows, slots)]
             for r, total in zip(rows, sums):
@@ -124,23 +125,20 @@
         table[piece_rows(where_ref, 1 - core, k), :] = pieces[4 + i][...]
     rows_copy.wait()
 
-    def store(g):
-        part = pl.ds(pl.multiple_of(g * GRID_ROWS, GRID_ROWS), GRID_ROWS)
-        return pltpu.make_async_copy(stage.at[part, :], out_hbm.at[part, :], sems.at[g])
-
-    def copy_grid(g, carry):
-        start = pl.multiple_of(g * GRID_ROWS, GRID_ROWS)
-        for first in range(0, K, BATCH):
-            slots = range(first, first + BATCH)
+    stores = []
+    for g in range(GRIDS):
+        start = g * GRID_ROWS
+        for first in range(0, K, GATHER_BATCH):
+            slots = range(first, first + GATHER_BATCH)
             values = [table[block_rows(rows_ref[g, j]), :] for j in slots]
             for j, value in zip(slots, values):
                 stage[slot_rows(start, j), :] = value
-        store(g).start()
-        return carry
-
-    lax.fori_loop(0, GRIDS, copy_grid, 0)
-    for g in range(GRIDS):
-        store(g).wait()
+        part = pl.ds(start, GRID_ROWS)
+        store = pltpu.make_async_copy(stage.at[part, :], out_hbm.at[part, :], sems.at[g])
+        store.start()
+        stores.append(store)
+    for store in stores:
+        store.wait()
 
 
 def local(surplus, block_ids, coef):

time: 47 us -> 46.5 us (0.989)
  Pallas kernels: 8.33 us -> 7.83 us
where the time goes in v7:
time: 46.5 us; the launch traced here: 46.4 us
  starting transfers between devices  22.8 us (49%)
  waiting for transfers between devices  15.5 us (33%)
  Pallas kernels  7.83 us (17%)
    ppermute x17, starting transfers between devices, send(): return lax.ppermute(value, 'grp', partner)  22.8 us
    ppermute x17, waiting for transfers between devices, send(): return lax.ppermute(value, 'grp', partner)  15.5 us
    pallas_call x1, Pallas kernels, local(): pl.pallas_call(scatter, out_shape=(piece,) * 8, in_specs=[smem, hbm, hbm,...  4.16 us
    pallas_call x1, Pallas kernels, local(): pl.pallas_call(gather, out_shape=jax.ShapeDtypeStruct((GRIDS * GRID_ROWS,...  3.67 us
  transfers between devices with their start and end apart: 17, of which 10 were waited for; matrix products, arithmetic and copies ran while one was open for 0% of the time, Pallas kernels for 0%

profile of v7, /device:TPU:1, one launch (start us, length us, event | category | flops | bytes accessed | tf_op | source)
XLA Modules:
  0.0 46.4 jit_solution(4135080918986895068)
XLA Ops:
  0.0 0.1 pad_add_fusion.where_ref
  0.1 0.0 copy-start
  0.1 4.2 %shard_map.37 = (f32[512,128]{1,0:T(8,128)S(1)}, f32[512,128]{1,0:T(8,128)S(1)}, f32[512,128]{1,0:T(8,128)S(1)}, f32[512,128]{1,0:T(8,128)S(1)}, f32[512,128]{1,...) custom-call(s32[4]{0:T(128)S(1)} %pad_add_fusion.where_ref, s32[16]{0:T(128)} %coef_hbm.1, ...), custom_call_target="tpu_custom_call" | custom-call | tf_op jit(solution)/shard_map/pallas_call | solution.py:155
  4.2 3.3 %collective-permute-start.1 = (f32[512,128]{1,0:T(8,128)S(1)}, f32[512,128]{1,0:T(8,128)S(1)}, u32[]{:S(2)}, u32[]{:S(2)}) collective-permute-start(f32[512,128]{1,0:T(8,128)S(1)} %get-tuple-element.16), channel_id=1, source_target_pairs={{0,8},{8,0},{16,24},{24,16},{32,40},{40,32},{48,56},{56,48},{64,72... | collective-permute-start | bytes 786440 | tf_op jit(solution)/shard_map/ppermute | solution.py:51
  7.6 0.1 collective-permute-start.3
  7.7 0.4 collective-permute-start.5
  8.1 0.1 collective-permute-start
  8.2 0.6 %collective-permute-done.1 = f32[512,128]{1,0:T(8,128)S(1)} collective-permute-done((f32[512,128]{1,0:T(8,128)S(1)}, f32[512,128]{1,0:T(8,128)S(1)}, u32[]{:S(2)}, u32[]{:S(2)}) %collective-permute-start.1) | collective-permute-done | bytes 262176 | tf_op jit(solution)/shard_map/ppermute | solution.py:51
  8.8 1.3 %collective-permute-start.2 = (f32[512,128]{1,0:T(8,128)S(1)}, f32[512,128]{1,0:T(8,128)S(1)}, u32[]{:S(2)}, u32[]{:S(2)}) collective-permute-start(f32[512,128]{1,0:T(8,128)S(1)} %add.31), channel_id=1, source_target_pairs={{0,128},{8,40},{16,144},{24,56},{32,160},{40,8},{48,176},{56,24},{... | collective-permute-start | bytes 786440 | tf_op jit(solution)/shard_map/ppermute | solution.py:51
  10.0 0.0 collective-permute-done.3
  10.1 0.5 %collective-permute-start.4 = (f32[512,128]{1,0:T(8,128)S(1)}, f32[512,128]{1,0:T(8,128)S(1)}, u32[]{:S(2)}, u32[]{:S(2)}) collective-permute-start(f32[512,128]{1,0:T(8,128)S(1)} %add.33), channel_id=1, source_target_pairs={{0,64},{8,24},{16,80},{24,8},{32,96},{40,56},{48,112},{56,40},{64,... | collective-permute-start | bytes 786440 | tf_op jit(solution)/shard_map/ppermute | solution.py:51
  10.6 0.0 collective-permute-done.5
  10.6 1.8 %collective-permute-start.6 = (f32[512,128]{1,0:T(8,128)S(1)}, f32[512,128]{1,0:T(8,128)S(1)}, u32[]{:S(2)}, u32[]{:S(2)}) collective-permute-start(f32[512,128]{1,0:T(8,128)S(1)} %add.35), channel_id=1, source_target_pairs={{0,192},{8,56},{16,208},{24,40},{32,224},{40,24},{48,240},{56,8},{... | collective-permute-start | bytes 786440 | tf_op jit(solution)/shard_map/ppermute | solution.py:51
  12.4 0.0 collective-permute-done
  12.4 3.5 %collective-permute-done.2 = f32[512,128]{1,0:T(8,128)S(1)} collective-permute-done((f32[512,128]{1,0:T(8,128)S(1)}, f32[512,128]{1,0:T(8,128)S(1)}, u32[]{:S(2)}, u32[]{:S(2)}) %collective-permute-start.2) | collective-permute-done | bytes 262176 | tf_op jit(solution)/shard_map/ppermute | solution.py:51
  15.9 1.4 %collective-permute-done.4 = f32[512,128]{1,0:T(8,128)S(1)} collective-permute-done((f32[512,128]{1,0:T(8,128)S(1)}, f32[512,128]{1,0:T(8,128)S(1)}, u32[]{:S(2)}, u32[]{:S(2)}) %collective-permute-start.4) | collective-permute-done | bytes 262176 | tf_op jit(solution)/shard_map/ppermute | solution.py:51
  17.3 1.4 %collective-permute-done.6 = f32[512,128]{1,0:T(8,128)S(1)} collective-permute-done((f32[512,128]{1,0:T(8,128)S(1)}, f32[512,128]{1,0:T(8,128)S(1)}, u32[]{:S(2)}, u32[]{:S(2)}) %collective-permute-start.6) | collective-permute-done | bytes 262176 | tf_op jit(solution)/shard_map/ppermute | solution.py:51
  18.7 0.1 add_add_fusion.1
  18.8 1.5 %collective-permute-start.9 = (f32[512,128]{1,0:T(8,128)S(1)}, f32[512,128]{1,0:T(8,128)S(1)}, u32[]{:S(2)}, u32[]{:S(2)}) collective-permute-start(f32[512,128]{1,0:T(8,128)S(1)} %add_add_fusion.1), channel_id=1, source_target_pairs={{0,32},{8,136},{16,48},{24,152},{32,0},{40,168},{48,16},{56,184},{... | collective-permute-start | bytes 786440 | tf_op jit(solution)/shard_map/ppermute | solution.py:51
  20.2 0.4 collective-permute-start.8
  20.6 1.5 %collective-permute-start.7 = (f32[512,128]{1,0:T(8,128)S(1)}, f32[512,128]{1,0:T(8,128)S(1)}, u32[]{:S(2)}, u32[]{:S(2)}) collective-permute-start(f32[512,128]{1,0:T(8,128)S(1)} %add_add_fusion.1), channel_id=1, source_target_pairs={{0,48},{8,200},{16,32},{24,216},{32,16},{40,232},{48,0},{56,248},{... | collective-permute-start | bytes 786440 | tf_op jit(solution)/shard_map/ppermute | solution.py:51
  22.1 3.8 %collective-permute-done.9 = f32[512,128]{1,0:T(8,128)S(1)} collective-permute-done((f32[512,128]{1,0:T(8,128)S(1)}, f32[512,128]{1,0:T(8,128)S(1)}, u32[]{:S(2)}, u32[]{:S(2)}) %collective-permute-start.9) | collective-permute-done | bytes 262176 | tf_op jit(solution)/shard_map/ppermute | solution.py:51
  25.9 1.6 %collective-permute-done.8 = f32[512,128]{1,0:T(8,128)S(1)} collective-permute-done((f32[512,128]{1,0:T(8,128)S(1)}, f32[512,128]{1,0:T(8,128)S(1)}, u32[]{:S(2)}, u32[]{:S(2)}) %collective-permute-start.8) | collective-permute-done | bytes 262176 | tf_op jit(solution)/shard_map/ppermute | solution.py:51
  27.5 1.2 %collective-permute-done.7 = f32[512,128]{1,0:T(8,128)S(1)} collective-permute-done((f32[512,128]{1,0:T(8,128)S(1)}, f32[512,128]{1,0:T(8,128)S(1)}, u32[]{:S(2)}, u32[]{:S(2)}) %collective-permute-start.7) | collective-permute-done | bytes 262176 | tf_op jit(solution)/shard_map/ppermute | solution.py:51
  28.7 1.4 %collective-permute-start.12 = (f32[512,128]{1,0:T(8,128)S(1)}, f32[512,128]{1,0:T(8,128)S(1)}, u32[]{:S(2)}, u32[]{:S(2)}) collective-permute-start(f32[512,128]{1,0:T(8,128)S(1)} %add_add_fusion.refs_0_), channel_id=1, source_target_pairs={{0,128},{8,40},{16,144},{24,56},{32,160},{40,8},{48,176},{56,24},{... | collective-permute-start | bytes 786440 | tf_op jit(solution)/shard_map/ppermute | solution.py:51
  30.1 0.4 collective-permute-start.11
  30.5 1.5 %collective-permute-start.10 = (f32[512,128]{1,0:T(8,128)S(1)}, f32[512,128]{1,0:T(8,128)S(1)}, u32[]{:S(2)}, u32[]{:S(2)}) collective-permute-start(f32[512,128]{1,0:T(8,128)S(1)} %add_add_fusion.refs_0_), channel_id=1, source_target_pairs={{0,192},{8,56},{16,208},{24,40},{32,224},{40,24},{48,240},{56,8},{... | collective-permute-start | bytes 786440 | tf_op jit(solution)/shard_map/ppermute | solution.py:51
  32.1 2.9 %collective-permute-start.13 = (f32[512,128]{1,0:T(8,128)S(1)}, f32[512,128]{1,0:T(8,128)S(1)}, u32[]{:S(2)}, u32[]{:S(2)}) collective-permute-start(f32[512,128]{1,0:T(8,128)S(1)} %add_add_fusion.refs_0_), channel_id=1, source_target_pairs={{0,8},{8,0},{16,24},{24,16},{32,40},{40,32},{48,56},{56,48},{64,72... | collective-permute-start | bytes 786440 | tf_op jit(solution)/shard_map/ppermute | solution.py:51
  35.0 0.8 %collective-permute-done.12.refs_3_ = f32[512,128]{1,0:T(8,128)S(1)} collective-permute-done((f32[512,128]{1,0:T(8,128)S(1)}, f32[512,128]{1,0:T(8,128)S(1)}, u32[]{:S(2)}, u32[]{:S(2)}) %collective-permute-start.12) | collective-permute-done | bytes 262176 | tf_op jit(solution)/shard_map/ppermute | solution.py:51
  35.8 3.0 %collective-permute-start.16 = (f32[512,128]{1,0:T(8,128)S(1)}, f32[512,128]{1,0:T(8,128)S(1)}, u32[]{:S(2)}, u32[]{:S(2)}) collective-permute-start(f32[512,128]{1,0:T(8,128)S(1)} %collective-permute-done.12.refs_3_), channel_id=1, source_target_pairs={{0,8},{8,0},{16,24},{24,16},{32,40},{40,32},{48,56},{56,48},{64,72... | collective-permute-start | bytes 786440 | tf_op jit(solution)/shard_map/ppermute | solution.py:51
  38.8 0.0 collective-permute-done.11.refs_2_
  38.8 1.9 %collective-permute-start.15 = (f32[512,128]{1,0:T(8,128)S(1)}, f32[512,128]{1,0:T(8,128)S(1)}, u32[]{:S(2)}, u32[]{:S(2)}) collective-permute-start(f32[512,128]{1,0:T(8,128)S(1)} %collective-permute-done.11.refs_2_), channel_id=1, source_target_pairs={{0,8},{8,0},{16,24},{24,16},{32,40},{40,32},{48,56},{56,48},{64,72... | collective-permute-start | bytes 786440 | tf_op jit(solution)/shard_map/ppermute | solution.py:51
  40.7 0.0 collective-permute-done.10.refs_1_
  40.7 0.9 %collective-permute-start.14 = (f32[512,128]{1,0:T(8,128)S(1)}, f32[512,128]{1,0:T(8,128)S(1)}, u32[]{:S(2)}, u32[]{:S(2)}) collective-permute-start(f32[512,128]{1,0:T(8,128)S(1)} %collective-permute-done.10.refs_1_), channel_id=1, source_target_pairs={{0,8},{8,0},{16,24},{24,16},{32,40},{40,32},{48,56},{56,48},{64,72... | collective-permute-start | bytes 786440 | tf_op jit(solution)/shard_map/ppermute | solution.py:51
  41.6 0.0 copy-done
  41.6 0.0 collective-permute-done.13.refs_4_
  41.6 0.0 collective-permute-done.16.refs_7_
  41.6 0.3 collective-permute-done.15.refs_6_
  41.9 0.9 %collective-permute-done.14.refs_5_ = f32[512,128]{1,0:T(8,128)S(1)} collective-permute-done((f32[512,128]{1,0:T(8,128)S(1)}, f32[512,128]{1,0:T(8,128)S(1)}, u32[]{:S(2)}, u32[]{:S(2)}) %collective-permute-start.14) | collective-permute-done | bytes 262176 | tf_op jit(solution)/shard_map/ppermute | solution.py:51
  42.7 3.7 %shard_map.38 = f32[8192,128]{1,0:T(8,128)} custom-call(s32[4]{0:T(128)S(1)} %pad_add_fusion.where_ref, s32[16,128]{1,0:T(8,128)S(1)} %subtract_multiply_fusion.rows_vmem, f32[512,128]{1,0:T(8,128)S(1)} %add_add_fusion.refs_0_, f32[512,128]{1,0:T(8,128)S(1)} %collective-permute-done.10.refs_1_, f32[512,128]{1,0:T(8,128)S(1)} %collective-permute-done.11.refs_2_, ...), custom_call_target="tpu_custom_call" | custom-call | tf_op jit(solution)/shard_map/pallas_call | solution.py:179
  (5 shorter events, 0.1 us)
Async XLA Ops:
  0.1 41.5 %copy-start = (s32[16,128]{1,0:T(8,128)S(1)}, s32[16,128]{1,0:T(8,128)}, u32[]{:S(2)}) copy-start(s32[16,128]{1,0:T(8,128)} %ids_hbm.1) | copy-start | bytes 24580
  4.2 4.5 %collective-permute-start.1 = (f32[512,128]{1,0:T(8,128)S(1)}, f32[512,128]{1,0:T(8,128)S(1)}, u32[]{:S(2)}, u32[]{:S(2)}) collective-permute-start(f32[512,128]{1,0:T(8,128)S(1)} %get-tuple-element.16), channel_id=1, source_target_pairs={{0,8},{8,0},{16,24},{24,16},{32,40},{40,32},{48,56},{56,48},{64,72... | collective-permute-start | bytes 786440 | tf_op jit(solution)/shard_map/ppermute | solution.py:51
  7.6 2.5 %collective-permute-start.3 = (f32[512,128]{1,0:T(8,128)S(1)}, f32[512,128]{1,0:T(8,128)S(1)}, u32[]{:S(2)}, u32[]{:S(2)}) collective-permute-start(f32[512,128]{1,0:T(8,128)S(1)} %get-tuple-element.18), channel_id=1, source_target_pairs={{0,8},{8,0},{16,24},{24,16},{32,40},{40,32},{48,56},{56,48},{64,72... | collective-permute-start | bytes 786440 | tf_op jit(solution)/shard_map/ppermute | solution.py:51
  7.7 2.9 %collective-permute-start.5 = (f32[512,128]{1,0:T(8,128)S(1)}, f32[512,128]{1,0:T(8,128)S(1)}, u32[]{:S(2)}, u32[]{:S(2)}) collective-permute-start(f32[512,128]{1,0:T(8,128)S(1)} %get-tuple-element.20), channel_id=1, source_target_pairs={{0,8},{8,0},{16,24},{24,16},{32,40},{40,32},{48,56},{56,48},{64,72... | collective-permute-start | bytes 786440 | tf_op jit(solution)/shard_map/ppermute | solution.py:51
  8.1 4.3 %collective-permute-start = (f32[512,128]{1,0:T(8,128)S(1)}, f32[512,128]{1,0:T(8,128)S(1)}, u32[]{:S(2)}, u32[]{:S(2)}) collective-permute-start(f32[512,128]{1,0:T(8,128)S(1)} %get-tuple-element.14), channel_id=1, source_target_pairs={{0,8},{8,0},{16,24},{24,16},{32,40},{40,32},{48,56},{56,48},{64,72... | collective-permute-start | bytes 786440 | tf_op jit(solution)/shard_map/ppermute | solution.py:51
  8.8 7.1 %collective-permute-start.2 = (f32[512,128]{1,0:T(8,128)S(1)}, f32[512,128]{1,0:T(8,128)S(1)}, u32[]{:S(2)}, u32[]{:S(2)}) collective-permute-start(f32[512,128]{1,0:T(8,128)S(1)} %add.31), channel_id=1, source_target_pairs={{0,128},{8,40},{16,144},{24,56},{32,160},{40,8},{48,176},{56,24},{... | collective-permute-start | bytes 786440 | tf_op jit(solution)/shard_map/ppermute | solution.py:51
  10.1 7.2 %collective-permute-start.4 = (f32[512,128]{1,0:T(8,128)S(1)}, f32[512,128]{1,0:T(8,128)S(1)}, u32[]{:S(2)}, u32[]{:S(2)}) collective-permute-start(f32[512,128]{1,0:T(8,128)S(1)} %add.33), channel_id=1, source_target_pairs={{0,64},{8,24},{16,80},{24,8},{32,96},{40,56},{48,112},{56,40},{64,... | collective-permute-start | bytes 786440 | tf_op jit(solution)/shard_map/ppermute | solution.py:51
  10.6 8.1 %collective-permute-start.6 = (f32[512,128]{1,0:T(8,128)S(1)}, f32[512,128]{1,0:T(8,128)S(1)}, u32[]{:S(2)}, u32[]{:S(2)}) collective-permute-start(f32[512,128]{1,0:T(8,128)S(1)} %add.35), channel_id=1, source_target_pairs={{0,192},{8,56},{16,208},{24,40},{32,224},{40,24},{48,240},{56,8},{... | collective-permute-start | bytes 786440 | tf_op jit(solution)/shard_map/ppermute | solution.py:51
  18.8 7.1 %collective-permute-start.9 = (f32[512,128]{1,0:T(8,128)S(1)}, f32[512,128]{1,0:T(8,128)S(1)}, u32[]{:S(2)}, u32[]{:S(2)}) collective-permute-start(f32[512,128]{1,0:T(8,128)S(1)} %add_add_fusion.1), channel_id=1, source_target_pairs={{0,32},{8,136},{16,48},{24,152},{32,0},{40,168},{48,16},{56,184},{... | collective-permute-start | bytes 786440 | tf_op jit(solution)/shard_map/ppermute | solution.py:51
  20.2 7.2 %collective-permute-start.8 = (f32[512,128]{1,0:T(8,128)S(1)}, f32[512,128]{1,0:T(8,128)S(1)}, u32[]{:S(2)}, u32[]{:S(2)}) collective-permute-start(f32[512,128]{1,0:T(8,128)S(1)} %add_add_fusion.1), channel_id=1, source_target_pairs={{0,16},{8,72},{16,0},{24,88},{32,48},{40,104},{48,32},{56,120},{64... | collective-permute-start | bytes 786440 | tf_op jit(solution)/shard_map/ppermute | solution.py:51
  20.6 8.1 %collective-permute-start.7 = (f32[512,128]{1,0:T(8,128)S(1)}, f32[512,128]{1,0:T(8,128)S(1)}, u32[]{:S(2)}, u32[]{:S(2)}) collective-permute-start(f32[512,128]{1,0:T(8,128)S(1)} %add_add_fusion.1), channel_id=1, source_target_pairs={{0,48},{8,200},{16,32},{24,216},{32,16},{40,232},{48,0},{56,248},{... | collective-permute-start | bytes 786440 | tf_op jit(solution)/shard_map/ppermute | solution.py:51
  28.7 7.1 %collective-permute-start.12 = (f32[512,128]{1,0:T(8,128)S(1)}, f32[512,128]{1,0:T(8,128)S(1)}, u32[]{:S(2)}, u32[]{:S(2)}) collective-permute-start(f32[512,128]{1,0:T(8,128)S(1)} %add_add_fusion.refs_0_), channel_id=1, source_target_pairs={{0,128},{8,40},{16,144},{24,56},{32,160},{40,8},{48,176},{56,24},{... | collective-permute-start | bytes 786440 | tf_op jit(solution)/shard_map/ppermute | solution.py:51
  30.1 8.7 %collective-permute-start.11 = (f32[512,128]{1,0:T(8,128)S(1)}, f32[512,128]{1,0:T(8,128)S(1)}, u32[]{:S(2)}, u32[]{:S(2)}) collective-permute-start(f32[512,128]{1,0:T(8,128)S(1)} %add_add_fusion.refs_0_), channel_id=1, source_target_pairs={{0,64},{8,24},{16,80},{24,8},{32,96},{40,56},{48,112},{56,40},{64,... | collective-permute-start | bytes 786440 | tf_op jit(solution)/shard_map/ppermute | solution.py:51
  30.5 10.2 %collective-permute-start.10 = (f32[512,128]{1,0:T(8,128)S(1)}, f32[512,128]{1,0:T(8,128)S(1)}, u32[]{:S(2)}, u32[]{:S(2)}) collective-permute-start(f32[512,128]{1,0:T(8,128)S(1)} %add_add_fusion.refs_0_), channel_id=1, source_target_pairs={{0,192},{8,56},{16,208},{24,40},{32,224},{40,24},{48,240},{56,8},{... | collective-permute-start | bytes 786440 | tf_op jit(solution)/shard_map/ppermute | solution.py:51
  32.1 9.5 %collective-permute-start.13 = (f32[512,128]{1,0:T(8,128)S(1)}, f32[512,128]{1,0:T(8,128)S(1)}, u32[]{:S(2)}, u32[]{:S(2)}) collective-permute-start(f32[512,128]{1,0:T(8,128)S(1)} %add_add_fusion.refs_0_), channel_id=1, source_target_pairs={{0,8},{8,0},{16,24},{24,16},{32,40},{40,32},{48,56},{56,48},{64,72... | collective-permute-start | bytes 786440 | tf_op jit(solution)/shard_map/ppermute | solution.py:51
  35.8 5.8 %collective-permute-start.16 = (f32[512,128]{1,0:T(8,128)S(1)}, f32[512,128]{1,0:T(8,128)S(1)}, u32[]{:S(2)}, u32[]{:S(2)}) collective-permute-start(f32[512,128]{1,0:T(8,128)S(1)} %collective-permute-done.12.refs_3_), channel_id=1, source_target_pairs={{0,8},{8,0},{16,24},{24,16},{32,40},{40,32},{48,56},{56,48},{64,72... | collective-permute-start | bytes 786440 | tf_op jit(solution)/shard_map/ppermute | solution.py:51
  38.8 3.0 %collective-permute-start.15 = (f32[512,128]{1,0:T(8,128)S(1)}, f32[512,128]{1,0:T(8,128)S(1)}, u32[]{:S(2)}, u32[]{:S(2)}) collective-permute-start(f32[512,128]{1,0:T(8,128)S(1)} %collective-permute-done.11.refs_2_), channel_id=1, source_target_pairs={{0,8},{8,0},{16,24},{24,16},{32,40},{40,32},{48,56},{56,48},{64,72... | collective-permute-start | bytes 786440 | tf_op jit(solution)/shard_map/ppermute | solution.py:51
  40.7 2.0 %collective-permute-start.14 = (f32[512,128]{1,0:T(8,128)S(1)}, f32[512,128]{1,0:T(8,128)S(1)}, u32[]{:S(2)}, u32[]{:S(2)}) collective-permute-start(f32[512,128]{1,0:T(8,128)S(1)} %collective-permute-done.10.refs_1_), channel_id=1, source_target_pairs={{0,8},{8,0},{16,24},{24,16},{32,40},{40,32},{48,56},{56,48},{64,72... | collective-permute-start | bytes 786440 | tf_op jit(solution)/shard_map/ppermute | solution.py:51

commit v8 on v7

--- a/solution.py
+++ b/solution.py
@@ -133,10 +133,13 @@
             values = [table[block_rows(rows_ref[g, j]), :] for j in slots]
             for j, value in zip(slots, values):
                 stage[slot_rows(start, j), :] = value
-        part = pl.ds(start, GRID_ROWS)
-        store = pltpu.make_async_copy(stage.at[part, :], out_hbm.at[part, :], sems.at[g])
-        store.start()
-        stores.append(store)
+            done = (first + GATHER_BATCH) * SUB
+            if done == GRID_ROWS or g == GRIDS - 1 and done == GRID_ROWS // 2:
+                size = GRID_ROWS // 2 if g == GRIDS - 1 else GRID_ROWS
+                part = pl.ds(start + done - size, size)
+                copy = pltpu.make_async_copy(stage.at[part, :], out_hbm.at[part, :], sems.at[len(stores)])
+                copy.start()
+                stores.append(copy)
     for store in stores:
         store.wait()
 
@@ -185,7 +188,7 @@
             table,
             stage,
             pltpu.SMEM((GRIDS, K), jnp.int32),
-            pltpu.SemaphoreType.DMA((GRIDS,)),
+            pltpu.SemaphoreType.DMA((GRIDS + 1,)),
             pltpu.SemaphoreType.DMA,
         ],
         compiler_params=params,

time: 46.5 us -> 46.5 us (level)
  no operation moved by 1% of the time
where the time goes in v8:
time: 46.5 us; the launch traced here: 46.4 us
  starting transfers between devices  22.8 us (49%)
  waiting for transfers between devices  15.5 us (33%)
  Pallas kernels  7.82 us (17%)
    ppermute x17, starting transfers between devices, send(): return lax.ppermute(value, 'grp', partner)  22.8 us
    ppermute x17, waiting for transfers between devices, send(): return lax.ppermute(value, 'grp', partner)  15.5 us
    pallas_call x1, Pallas kernels, local(): pl.pallas_call(scatter, out_shape=(piece,) * 8, in_specs=[smem, hbm, hbm,...  4.16 us
    pallas_call x1, Pallas kernels, local(): pl.pallas_call(gather, out_shape=jax.ShapeDtypeStruct((GRIDS * GRID_ROWS,...  3.66 us
  transfers between devices with their start and end apart: 17, of which 10 were waited for; matrix products, arithmetic and copies ran while one was open for 0% of the time, Pallas kernels for 0%

profile of v8, /device:TPU:1, one launch (start us, length us, event | category | flops | bytes accessed | tf_op | source)
XLA Modules:
  0.0 46.4 jit_solution(9688135008409530336)
XLA Ops:
  0.0 0.1 pad_add_fusion.where_ref
  0.1 0.0 copy-start
  0.1 4.2 %shard_map.37 = (f32[512,128]{1,0:T(8,128)S(1)}, f32[512,128]{1,0:T(8,128)S(1)}, f32[512,128]{1,0:T(8,128)S(1)}, f32[512,128]{1,0:T(8,128)S(1)}, f32[512,128]{1,...) custom-call(s32[4]{0:T(128)S(1)} %pad_add_fusion.where_ref, s32[16]{0:T(128)} %coef_hbm.1, ...), custom_call_target="tpu_custom_call" | custom-call | tf_op jit(solution)/shard_map/pallas_call | solution.py:158
  4.2 3.3 %collective-permute-start.1 = (f32[512,128]{1,0:T(8,128)S(1)}, f32[512,128]{1,0:T(8,128)S(1)}, u32[]{:S(2)}, u32[]{:S(2)}) collective-permute-start(f32[512,128]{1,0:T(8,128)S(1)} %get-tuple-element.16), channel_id=1, source_target_pairs={{0,8},{8,0},{16,24},{24,16},{32,40},{40,32},{48,56},{56,48},{64,72... | collective-permute-start | bytes 786440 | tf_op jit(solution)/shard_map/ppermute | solution.py:51
  7.6 0.1 collective-permute-start.3
  7.7 0.4 collective-permute-start.5
  8.1 0.1 collective-permute-start
  8.2 0.6 %collective-permute-done.1 = f32[512,128]{1,0:T(8,128)S(1)} collective-permute-done((f32[512,128]{1,0:T(8,128)S(1)}, f32[512,128]{1,0:T(8,128)S(1)}, u32[]{:S(2)}, u32[]{:S(2)}) %collective-permute-start.1) | collective-permute-done | bytes 262176 | tf_op jit(solution)/shard_map/ppermute | solution.py:51
  8.8 1.3 %collective-permute-start.2 = (f32[512,128]{1,0:T(8,128)S(1)}, f32[512,128]{1,0:T(8,128)S(1)}, u32[]{:S(2)}, u32[]{:S(2)}) collective-permute-start(f32[512,128]{1,0:T(8,128)S(1)} %add.31), channel_id=1, source_target_pairs={{0,128},{8,40},{16,144},{24,56},{32,160},{40,8},{48,176},{56,24},{... | collective-permute-start | bytes 786440 | tf_op jit(solution)/shard_map/ppermute | solution.py:51
  10.0 0.0 collective-permute-done.3
  10.1 0.5 %collective-permute-start.4 = (f32[512,128]{1,0:T(8,128)S(1)}, f32[512,128]{1,0:T(8,128)S(1)}, u32[]{:S(2)}, u32[]{:S(2)}) collective-permute-start(f32[512,128]{1,0:T(8,128)S(1)} %add.33), channel_id=1, source_target_pairs={{0,64},{8,24},{16,80},{24,8},{32,96},{40,56},{48,112},{56,40},{64,... | collective-permute-start | bytes 786440 | tf_op jit(solution)/shard_map/ppermute | solution.py:51
  10.6 0.0 collective-permute-done.5
  10.6 1.8 %collective-permute-start.6 = (f32[512,128]{1,0:T(8,128)S(1)}, f32[512,128]{1,0:T(8,128)S(1)}, u32[]{:S(2)}, u32[]{:S(2)}) collective-permute-start(f32[512,128]{1,0:T(8,128)S(1)} %add.35), channel_id=1, source_target_pairs={{0,192},{8,56},{16,208},{24,40},{32,224},{40,24},{48,240},{56,8},{... | collective-permute-start | bytes 786440 | tf_op jit(solution)/shard_map/ppermute | solution.py:51
  12.4 0.0 collective-permute-done
  12.4 3.5 %collective-permute-done.2 = f32[512,128]{1,0:T(8,128)S(1)} collective-permute-done((f32[512,128]{1,0:T(8,128)S(1)}, f32[512,128]{1,0:T(8,128)S(1)}, u32[]{:S(2)}, u32[]{:S(2)}) %collective-permute-start.2) | collective-permute-done | bytes 262176 | tf_op jit(solution)/shard_map/ppermute | solution.py:51
  15.9 1.4 %collective-permute-done.4 = f32[512,128]{1,0:T(8,128)S(1)} collective-permute-done((f32[512,128]{1,0:T(8,128)S(1)}, f32[512,128]{1,0:T(8,128)S(1)}, u32[]{:S(2)}, u32[]{:S(2)}) %collective-permute-start.4) | collective-permute-done | bytes 262176 | tf_op jit(solution)/shard_map/ppermute | solution.py:51
  17.3 1.4 %collective-permute-done.6 = f32[512,128]{1,0:T(8,128)S(1)} collective-permute-done((f32[512,128]{1,0:T(8,128)S(1)}, f32[512,128]{1,0:T(8,128)S(1)}, u32[]{:S(2)}, u32[]{:S(2)}) %collective-permute-start.6) | collective-permute-done | bytes 262176 | tf_op jit(solution)/shard_map/ppermute | solution.py:51
  18.7 0.1 add_add_fusion.1
  18.8 1.5 %collective-permute-start.9 = (f32[512,128]{1,0:T(8,128)S(1)}, f32[512,128]{1,0:T(8,128)S(1)}, u32[]{:S(2)}, u32[]{:S(2)}) collective-permute-start(f32[512,128]{1,0:T(8,128)S(1)} %add_add_fusion.1), channel_id=1, source_target_pairs={{0,32},{8,136},{16,48},{24,152},{32,0},{40,168},{48,16},{56,184},{... | collective-permute-start | bytes 786440 | tf_op jit(solution)/shard_map/ppermute | solution.py:51
  20.2 0.4 collective-permute-start.8
  20.6 1.5 %collective-permute-start.7 = (f32[512,128]{1,0:T(8,128)S(1)}, f32[512,128]{1,0:T(8,128)S(1)}, u32[]{:S(2)}, u32[]{:S(2)}) collective-permute-start(f32[512,128]{1,0:T(8,128)S(1)} %add_add_fusion.1), channel_id=1, source_target_pairs={{0,48},{8,200},{16,32},{24,216},{32,16},{40,232},{48,0},{56,248},{... | collective-permute-start | bytes 786440 | tf_op jit(solution)/shard_map/ppermute | solution.py:51
  22.1 3.8 %collective-permute-done.9 = f32[512,128]{1,0:T(8,128)S(1)} collective-permute-done((f32[512,128]{1,0:T(8,128)S(1)}, f32[512,128]{1,0:T(8,128)S(1)}, u32[]{:S(2)}, u32[]{:S(2)}) %collective-permute-start.9) | collective-permute-done | bytes 262176 | tf_op jit(solution)/shard_map/ppermute | solution.py:51
  25.9 1.6 %collective-permute-done.8 = f32[512,128]{1,0:T(8,128)S(1)} collective-permute-done((f32[512,128]{1,0:T(8,128)S(1)}, f32[512,128]{1,0:T(8,128)S(1)}, u32[]{:S(2)}, u32[]{:S(2)}) %collective-permute-start.8) | collective-permute-done | bytes 262176 | tf_op jit(solution)/shard_map/ppermute | solution.py:51
  27.5 1.2 %collective-permute-done.7 = f32[512,128]{1,0:T(8,128)S(1)} collective-permute-done((f32[512,128]{1,0:T(8,128)S(1)}, f32[512,128]{1,0:T(8,128)S(1)}, u32[]{:S(2)}, u32[]{:S(2)}) %collective-permute-start.7) | collective-permute-done | bytes 262176 | tf_op jit(solution)/shard_map/ppermute | solution.py:51
  28.7 1.4 %collective-permute-start.12 = (f32[512,128]{1,0:T(8,128)S(1)}, f32[512,128]{1,0:T(8,128)S(1)}, u32[]{:S(2)}, u32[]{:S(2)}) collective-permute-start(f32[512,128]{1,0:T(8,128)S(1)} %add_add_fusion.refs_0_), channel_id=1, source_target_pairs={{0,128},{8,40},{16,144},{24,56},{32,160},{40,8},{48,176},{56,24},{... | collective-permute-start | bytes 786440 | tf_op jit(solution)/shard_map/ppermute | solution.py:51
  30.1 0.4 collective-permute-start.11
  30.5 1.5 %collective-permute-start.10 = (f32[512,128]{1,0:T(8,128)S(1)}, f32[512,128]{1,0:T(8,128)S(1)}, u32[]{:S(2)}, u32[]{:S(2)}) collective-permute-start(f32[512,128]{1,0:T(8,128)S(1)} %add_add_fusion.refs_0_), channel_id=1, source_target_pairs={{0,192},{8,56},{16,208},{24,40},{32,224},{40,24},{48,240},{56,8},{... | collective-permute-start | bytes 786440 | tf_op jit(solution)/shard_map/ppermute | solution.py:51
  32.1 2.9 %collective-permute-start.13 = (f32[512,128]{1,0:T(8,128)S(1)}, f32[512,128]{1,0:T(8,128)S(1)}, u32[]{:S(2)}, u32[]{:S(2)}) collective-permute-start(f32[512,128]{1,0:T(8,128)S(1)} %add_add_fusion.refs_0_), channel_id=1, source_target_pairs={{0,8},{8,0},{16,24},{24,16},{32,40},{40,32},{48,56},{56,48},{64,72... | collective-permute-start | bytes 786440 | tf_op jit(solution)/shard_map/ppermute | solution.py:51
  35.0 0.8 %collective-permute-done.12.refs_3_ = f32[512,128]{1,0:T(8,128)S(1)} collective-permute-done((f32[512,128]{1,0:T(8,128)S(1)}, f32[512,128]{1,0:T(8,128)S(1)}, u32[]{:S(2)}, u32[]{:S(2)}) %collective-permute-start.12) | collective-permute-done | bytes 262176 | tf_op jit(solution)/shard_map/ppermute | solution.py:51
  35.8 3.0 %collective-permute-start.16 = (f32[512,128]{1,0:T(8,128)S(1)}, f32[512,128]{1,0:T(8,128)S(1)}, u32[]{:S(2)}, u32[]{:S(2)}) collective-permute-start(f32[512,128]{1,0:T(8,128)S(1)} %collective-permute-done.12.refs_3_), channel_id=1, source_target_pairs={{0,8},{8,0},{16,24},{24,16},{32,40},{40,32},{48,56},{56,48},{64,72... | collective-permute-start | bytes 786440 | tf_op jit(solution)/shard_map/ppermute | solution.py:51
  38.8 0.0 collective-permute-done.11.refs_2_
  38.8 1.9 %collective-permute-start.15 = (f32[512,128]{1,0:T(8,128)S(1)}, f32[512,128]{1,0:T(8,128)S(1)}, u32[]{:S(2)}, u32[]{:S(2)}) collective-permute-start(f32[512,128]{1,0:T(8,128)S(1)} %collective-permute-done.11.refs_2_), channel_id=1, source_target_pairs={{0,8},{8,0},{16,24},{24,16},{32,40},{40,32},{48,56},{56,48},{64,72... | collective-permute-start | bytes 786440 | tf_op jit(solution)/shard_map/ppermute | solution.py:51
  40.7 0.0 collective-permute-done.10.refs_1_
  40.7 0.9 %collective-permute-start.14 = (f32[512,128]{1,0:T(8,128)S(1)}, f32[512,128]{1,0:T(8,128)S(1)}, u32[]{:S(2)}, u32[]{:S(2)}) collective-permute-start(f32[512,128]{1,0:T(8,128)S(1)} %collective-permute-done.10.refs_1_), channel_id=1, source_target_pairs={{0,8},{8,0},{16,24},{24,16},{32,40},{40,32},{48,56},{56,48},{64,72... | collective-permute-start | bytes 786440 | tf_op jit(solution)/shard_map/ppermute | solution.py:51
  41.6 0.0 copy-done
  41.6 0.0 collective-permute-done.13.refs_4_
  41.6 0.0 collective-permute-done.16.refs_7_
  41.6 0.3 collective-permute-done.15.refs_6_
  41.9 0.9 %collective-permute-done.14.refs_5_ = f32[512,128]{1,0:T(8,128)S(1)} collective-permute-done((f32[512,128]{1,0:T(8,128)S(1)}, f32[512,128]{1,0:T(8,128)S(1)}, u32[]{:S(2)}, u32[]{:S(2)}) %collective-permute-start.14) | collective-permute-done | bytes 262176 | tf_op jit(solution)/shard_map/ppermute | solution.py:51
  42.7 3.7 %shard_map.38 = f32[8192,128]{1,0:T(8,128)} custom-call(s32[4]{0:T(128)S(1)} %pad_add_fusion.where_ref, s32[16,128]{1,0:T(8,128)S(1)} %subtract_multiply_fusion.rows_vmem, f32[512,128]{1,0:T(8,128)S(1)} %add_add_fusion.refs_0_, f32[512,128]{1,0:T(8,128)S(1)} %collective-permute-done.10.refs_1_, f32[512,128]{1,0:T(8,128)S(1)} %collective-permute-done.11.refs_2_, ...), custom_call_target="tpu_custom_call" | custom-call | tf_op jit(solution)/shard_map/pallas_call | solution.py:182
  (5 shorter events, 0.1 us)
Async XLA Ops:
  0.1 41.5 %copy-start = (s32[16,128]{1,0:T(8,128)S(1)}, s32[16,128]{1,0:T(8,128)}, u32[]{:S(2)}) copy-start(s32[16,128]{1,0:T(8,128)} %ids_hbm.1) | copy-start | bytes 24580
  4.2 4.5 %collective-permute-start.1 = (f32[512,128]{1,0:T(8,128)S(1)}, f32[512,128]{1,0:T(8,128)S(1)}, u32[]{:S(2)}, u32[]{:S(2)}) collective-permute-start(f32[512,128]{1,0:T(8,128)S(1)} %get-tuple-element.16), channel_id=1, source_target_pairs={{0,8},{8,0},{16,24},{24,16},{32,40},{40,32},{48,56},{56,48},{64,72... | collective-permute-start | bytes 786440 | tf_op jit(solution)/shard_map/ppermute | solution.py:51
  7.6 2.5 %collective-permute-start.3 = (f32[512,128]{1,0:T(8,128)S(1)}, f32[512,128]{1,0:T(8,128)S(1)}, u32[]{:S(2)}, u32[]{:S(2)}) collective-permute-start(f32[512,128]{1,0:T(8,128)S(1)} %get-tuple-element.18), channel_id=1, source_target_pairs={{0,8},{8,0},{16,24},{24,16},{32,40},{40,32},{48,56},{56,48},{64,72... | collective-permute-start | bytes 786440 | tf_op jit(solution)/shard_map/ppermute | solution.py:51
  7.7 2.9 %collective-permute-start.5 = (f32[512,128]{1,0:T(8,128)S(1)}, f32[512,128]{1,0:T(8,128)S(1)}, u32[]{:S(2)}, u32[]{:S(2)}) collective-permute-start(f32[512,128]{1,0:T(8,128)S(1)} %get-tuple-element.20), channel_id=1, source_target_pairs={{0,8},{8,0},{16,24},{24,16},{32,40},{40,32},{48,56},{56,48},{64,72... | collective-permute-start | bytes 786440 | tf_op jit(solution)/shard_map/ppermute | solution.py:51
  8.1 4.3 %collective-permute-start = (f32[512,128]{1,0:T(8,128)S(1)}, f32[512,128]{1,0:T(8,128)S(1)}, u32[]{:S(2)}, u32[]{:S(2)}) collective-permute-start(f32[512,128]{1,0:T(8,128)S(1)} %get-tuple-element.14), channel_id=1, source_target_pairs={{0,8},{8,0},{16,24},{24,16},{32,40},{40,32},{48,56},{56,48},{64,72... | collective-permute-start | bytes 786440 | tf_op jit(solution)/shard_map/ppermute | solution.py:51
  8.8 7.1 %collective-permute-start.2 = (f32[512,128]{1,0:T(8,128)S(1)}, f32[512,128]{1,0:T(8,128)S(1)}, u32[]{:S(2)}, u32[]{:S(2)}) collective-permute-start(f32[512,128]{1,0:T(8,128)S(1)} %add.31), channel_id=1, source_target_pairs={{0,128},{8,40},{16,144},{24,56},{32,160},{40,8},{48,176},{56,24},{... | collective-permute-start | bytes 786440 | tf_op jit(solution)/shard_map/ppermute | solution.py:51
  10.1 7.2 %collective-permute-start.4 = (f32[512,128]{1,0:T(8,128)S(1)}, f32[512,128]{1,0:T(8,128)S(1)}, u32[]{:S(2)}, u32[]{:S(2)}) collective-permute-start(f32[512,128]{1,0:T(8,128)S(1)} %add.33), channel_id=1, source_target_pairs={{0,64},{8,24},{16,80},{24,8},{32,96},{40,56},{48,112},{56,40},{64,... | collective-permute-start | bytes 786440 | tf_op jit(solution)/shard_map/ppermute | solution.py:51
  10.6 8.1 %collective-permute-start.6 = (f32[512,128]{1,0:T(8,128)S(1)}, f32[512,128]{1,0:T(8,128)S(1)}, u32[]{:S(2)}, u32[]{:S(2)}) collective-permute-start(f32[512,128]{1,0:T(8,128)S(1)} %add.35), channel_id=1, source_target_pairs={{0,192},{8,56},{16,208},{24,40},{32,224},{40,24},{48,240},{56,8},{... | collective-permute-start | bytes 786440 | tf_op jit(solution)/shard_map/ppermute | solution.py:51
  18.8 7.1 %collective-permute-start.9 = (f32[512,128]{1,0:T(8,128)S(1)}, f32[512,128]{1,0:T(8,128)S(1)}, u32[]{:S(2)}, u32[]{:S(2)}) collective-permute-start(f32[512,128]{1,0:T(8,128)S(1)} %add_add_fusion.1), channel_id=1, source_target_pairs={{0,32},{8,136},{16,48},{24,152},{32,0},{40,168},{48,16},{56,184},{... | collective-permute-start | bytes 786440 | tf_op jit(solution)/shard_map/ppermute | solution.py:51
  20.2 7.2 %collective-permute-start.8 = (f32[512,128]{1,0:T(8,128)S(1)}, f32[512,128]{1,0:T(8,128)S(1)}, u32[]{:S(2)}, u32[]{:S(2)}) collective-permute-start(f32[512,128]{1,0:T(8,128)S(1)} %add_add_fusion.1), channel_id=1, source_target_pairs={{0,16},{8,72},{16,0},{24,88},{32,48},{40,104},{48,32},{56,120},{64... | collective-permute-start | bytes 786440 | tf_op jit(solution)/shard_map/ppermute | solution.py:51
  20.6 8.1 %collective-permute-start.7 = (f32[512,128]{1,0:T(8,128)S(1)}, f32[512,128]{1,0:T(8,128)S(1)}, u32[]{:S(2)}, u32[]{:S(2)}) collective-permute-start(f32[512,128]{1,0:T(8,128)S(1)} %add_add_fusion.1), channel_id=1, source_target_pairs={{0,48},{8,200},{16,32},{24,216},{32,16},{40,232},{48,0},{56,248},{... | collective-permute-start | bytes 786440 | tf_op jit(solution)/shard_map/ppermute | solution.py:51
  28.7 7.1 %collective-permute-start.12 = (f32[512,128]{1,0:T(8,128)S(1)}, f32[512,128]{1,0:T(8,128)S(1)}, u32[]{:S(2)}, u32[]{:S(2)}) collective-permute-start(f32[512,128]{1,0:T(8,128)S(1)} %add_add_fusion.refs_0_), channel_id=1, source_target_pairs={{0,128},{8,40},{16,144},{24,56},{32,160},{40,8},{48,176},{56,24},{... | collective-permute-start | bytes 786440 | tf_op jit(solution)/shard_map/ppermute | solution.py:51
  30.1 8.7 %collective-permute-start.11 = (f32[512,128]{1,0:T(8,128)S(1)}, f32[512,128]{1,0:T(8,128)S(1)}, u32[]{:S(2)}, u32[]{:S(2)}) collective-permute-start(f32[512,128]{1,0:T(8,128)S(1)} %add_add_fusion.refs_0_), channel_id=1, source_target_pairs={{0,64},{8,24},{16,80},{24,8},{32,96},{40,56},{48,112},{56,40},{64,... | collective-permute-start | bytes 786440 | tf_op jit(solution)/shard_map/ppermute | solution.py:51
  30.5 10.2 %collective-permute-start.10 = (f32[512,128]{1,0:T(8,128)S(1)}, f32[512,128]{1,0:T(8,128)S(1)}, u32[]{:S(2)}, u32[]{:S(2)}) collective-permute-start(f32[512,128]{1,0:T(8,128)S(1)} %add_add_fusion.refs_0_), channel_id=1, source_target_pairs={{0,192},{8,56},{16,208},{24,40},{32,224},{40,24},{48,240},{56,8},{... | collective-permute-start | bytes 786440 | tf_op jit(solution)/shard_map/ppermute | solution.py:51
  32.1 9.5 %collective-permute-start.13 = (f32[512,128]{1,0:T(8,128)S(1)}, f32[512,128]{1,0:T(8,128)S(1)}, u32[]{:S(2)}, u32[]{:S(2)}) collective-permute-start(f32[512,128]{1,0:T(8,128)S(1)} %add_add_fusion.refs_0_), channel_id=1, source_target_pairs={{0,8},{8,0},{16,24},{24,16},{32,40},{40,32},{48,56},{56,48},{64,72... | collective-permute-start | bytes 786440 | tf_op jit(solution)/shard_map/ppermute | solution.py:51
  35.8 5.8 %collective-permute-start.16 = (f32[512,128]{1,0:T(8,128)S(1)}, f32[512,128]{1,0:T(8,128)S(1)}, u32[]{:S(2)}, u32[]{:S(2)}) collective-permute-start(f32[512,128]{1,0:T(8,128)S(1)} %collective-permute-done.12.refs_3_), channel_id=1, source_target_pairs={{0,8},{8,0},{16,24},{24,16},{32,40},{40,32},{48,56},{56,48},{64,72... | collective-permute-start | bytes 786440 | tf_op jit(solution)/shard_map/ppermute | solution.py:51
  38.8 3.0 %collective-permute-start.15 = (f32[512,128]{1,0:T(8,128)S(1)}, f32[512,128]{1,0:T(8,128)S(1)}, u32[]{:S(2)}, u32[]{:S(2)}) collective-permute-start(f32[512,128]{1,0:T(8,128)S(1)} %collective-permute-done.11.refs_2_), channel_id=1, source_target_pairs={{0,8},{8,0},{16,24},{24,16},{32,40},{40,32},{48,56},{56,48},{64,72... | collective-permute-start | bytes 786440 | tf_op jit(solution)/shard_map/ppermute | solution.py:51
  40.7 2.0 %collective-permute-start.14 = (f32[512,128]{1,0:T(8,128)S(1)}, f32[512,128]{1,0:T(8,128)S(1)}, u32[]{:S(2)}, u32[]{:S(2)}) collective-permute-start(f32[512,128]{1,0:T(8,128)S(1)} %collective-permute-done.10.refs_1_), channel_id=1, source_target_pairs={{0,8},{8,0},{16,24},{24,16},{32,40},{40,32},{48,56},{56,48},{64,72... | collective-permute-start | bytes 786440 | tf_op jit(solution)/shard_map/ppermute | solution.py:51
